TPU v7x, 256 devices: a whole 4x4x8 slice. The times are simulated.
256 devices in a mesh: ctx: 64 (over x_hi, z, y), head: 4 (over x_lo, core).
Axes of the slice: x: 4 (x_hi: 2, x_lo: 2; x = x_hi * 2 + x_lo), y: 4, z: 8, core: 2. Of those that a mesh axis runs over, the one named last changes fastest.
Arguments:
- tokens: bfloat16 [16384, 1024], P('ctx', 'head')
- gain: float32 [1024], replicated, may hold values from 0.25 to 1.75
- w_query: bfloat16 [1024, 1024], P(None, 'head'), may hold values from -0.1875 to 0.1875
- w_key: bfloat16 [1024, 1024], P(None, 'head'), may hold values from -0.1875 to 0.1875
- w_value: bfloat16 [1024, 1024], P(None, 'head'), may hold values from -0.1875 to 0.1875
- w_out: bfloat16 [1024, 1024], P('head'), may hold values from -0.1875 to 0.1875
- temper: float32 [16], P('head'), may hold values from 4 to 12
- adjacency: int32 [128, 128], replicated, may hold values from 0 to 1, as said below
- order: int32 [128], replicated, may hold values from 0 to 127, each once
Outputs:
- update: bfloat16 [16384, 1024], P('ctx', 'head')
Inputs may be any that keep to these rules, and one draw needn't show every extreme that they name: Entries are 0 or 1; adjacency[a][a] is 1 for every compartment block a. `order`: each compartment block appears once.
All inputs are finite; a program needn't handle non-finite values.
Results may differ from a plain program's by a relative error of at most 0.015.
Values may be sent and summed in bfloat16 or wider, within the bound.
No kernel may reach another device: no remote copies, remote signals or barrier semaphores. Data moves between devices by JAX's collectives and lax.ppermute only.
A program may use at most 64 MiB of HBM per device.

v0:
```python
import jax
import jax.numpy as jnp
from jax import lax
from jax.sharding import PartitionSpec as P

BLOCK = 128


def shifted(shard, axis, by):
    length = lax.axis_size(axis)
    return lax.ppermute(shard, axis, [(i, (i + by) % length) for i in range(length)])


def normalize(values):
    return values * lax.rsqrt(jnp.mean(values * values, axis=-1, keepdims=True) + 1e-06)


def shards(tokens, gain, w_query, w_key, w_value, w_out, temper, adjacency, order):
    whole = lax.all_gather(tokens, "head", axis=1, tiled=True)
    normed = (normalize(whole.astype(jnp.float32)) * gain).astype(jnp.bfloat16)
    rows = whole.shape[0]
    heads = temper.shape[0]
    width = w_query.shape[1]
    size = width // heads
    query = normalize(
        jnp.dot(normed, w_query, preferred_element_type=jnp.float32).reshape(rows, heads, size)
    )
    query = (query * (temper[None, :, None] / size)).astype(jnp.bfloat16)
    keys = normalize(
        jnp.dot(normed, w_key, preferred_element_type=jnp.float32).reshape(rows, heads, size)
    )
    keys = keys.astype(jnp.bfloat16).reshape(rows, width)
    values = jnp.dot(normed, w_value, preferred_element_type=jnp.float32).astype(jnp.bfloat16)
    stacked = jnp.stack([keys, values])
    cycle = lax.axis_size("ctx")
    place = lax.axis_index("ctx")
    local_blocks = rows // BLOCK
    linked = adjacency[order][:, order]
    mine = lax.dynamic_slice_in_dim(linked, place * local_blocks, local_blocks, 0)
    query_live = jnp.repeat(mine, BLOCK, axis=0)

    def attend(carry, piece, start):
        count = piece.shape[1]
        key_block = (start + jnp.arange(count, dtype=jnp.int32)) // BLOCK
        allowed = (jnp.take(query_live, key_block, axis=1) > 0) & True

        def compute(state):
            summed, weight = state
            keys_piece = piece[0].reshape(count, heads, size)
            values_piece = piece[1].reshape(count, heads, size)
            scores = jnp.einsum(
                "qhd,khd->hqk", query, keys_piece, preferred_element_type=jnp.float32
            )
            probs = jnp.where(allowed[None], jnp.exp(scores), 0.0)
            weight = weight + jnp.sum(probs, axis=-1)
            summed = summed + jnp.einsum(
                "hqk,khd->qhd",
                probs.astype(jnp.bfloat16),
                values_piece,
                preferred_element_type=jnp.float32,
            )
            return (summed, weight)

        def keep(state):
            return state

        return lax.cond(jnp.any(allowed), compute, keep, carry)

    initial = (jnp.zeros((rows, heads, size), jnp.float32), jnp.zeros((heads, rows), jnp.float32))
    state = attend(initial, stacked, place * rows)

    def turn(step, pack):
        moving, state = pack
        moving = shifted(moving, "ctx", 1)
        source = (place - step - 1) % cycle
        return (moving, attend(state, moving, source * rows))

    moved, state = lax.fori_loop(0, cycle - 1, turn, (stacked, state))
    summed, weight = state
    attended = (summed / weight.T[:, :, None]).astype(jnp.bfloat16).reshape(rows, width)
    partial_value = jnp.dot(attended, w_out, preferred_element_type=jnp.float32)
    return lax.psum_scatter(
        partial_value.astype(jnp.bfloat16), "head", scatter_dimension=1, tiled=True
    )


def solution(mesh):
    in_specs = (
        P("ctx", "head"),
        P(),
        P(None, "head"),
        P(None, "head"),
        P(None, "head"),
        P("head", None),
        P("head"),
        P(),
        P(),
    )
    out_specs = P("ctx", "head")
    return jax.shard_map(shards, mesh=mesh, in_specs=in_specs, out_specs=out_specs, check_vma=False)
```

profile of v0, /device:TPU:1, one launch (start us, length us, event | category | flops | bytes accessed | tf_op | source)
XLA Modules:
  0.0 901.2 jit_solution(10523663099705868472)
XLA Ops:
  12.9 9.7 %all_gather.3 = bf16[256,1024]{1,0:T(8,128)(2,1)S(1)} all-gather(bf16[256,256]{1,0:T(8,128)(2,1)S(1)} %copy-done.1), channel_id=1, replica_groups=mesh['ctx'=64,'head'=4] {'head'}, dimensions={1}, use_global_device_ids=true | all-gather | bytes 655360 | tf_op jit(solution)/shard_map/all_gather | solution.py:19
  26.7 787.0 %while.21 = (s32[]{:T(128)}, bf16[2,256,256]{1,2,0:T(8,128)(2,1)S(1)}, f32[256,4,64]{0,2,1:T(8,128)S(1)}, f32[4,256]{1,0:T(4,128)S(1)}, s32[]{:T(128)}, /*index=...) while((s32[]{:T(128)}, ...), condition=%wide.region_12.14_spmd.clone, body=%wide.region_7.13_spmd.clone.sunk | while | flops 68168976 | bytes 5399444 | solution.py:78
  29.7 12.8 %collective-permute-done = bf16[2,256,256]{1,2,0:T(8,128)(2,1)S(1)} collective-permute-done((bf16[2,256,256]{1,2,0:T(8,128)(2,1)S(1)}, bf16[2,256,256]{1,2,0:T(8,128)(2,1)S(1)}, u32[]{:S(2)}, u32[]{:S(2)}) %collective-permute-start) | collective-permute-done | bytes 262176 | tf_op jit(solution)/shard_map/while/body/eval_jaxpr/ppermute | solution.py:11
  45.9 10.1 %collective-permute-done = bf16[2,256,256]{1,2,0:T(8,128)(2,1)S(1)} collective-permute-done((bf16[2,256,256]{1,2,0:T(8,128)(2,1)S(1)}, bf16[2,256,256]{1,2,0:T(8,128)(2,1)S(1)}, u32[]{:S(2)}, u32[]{:S(2)}) %collective-permute-start) | collective-permute-done | bytes 262176 | tf_op jit(solution)/shard_map/while/body/eval_jaxpr/ppermute | solution.py:11
  59.6 9.2 %collective-permute-done = bf16[2,256,256]{1,2,0:T(8,128)(2,1)S(1)} collective-permute-done((bf16[2,256,256]{1,2,0:T(8,128)(2,1)S(1)}, bf16[2,256,256]{1,2,0:T(8,128)(2,1)S(1)}, u32[]{:S(2)}, u32[]{:S(2)}) %collective-permute-start) | collective-permute-done | bytes 262176 | tf_op jit(solution)/shard_map/while/body/eval_jaxpr/ppermute | solution.py:11
  154.6 9.2 %collective-permute-done = bf16[2,256,256]{1,2,0:T(8,128)(2,1)S(1)} collective-permute-done((bf16[2,256,256]{1,2,0:T(8,128)(2,1)S(1)}, bf16[2,256,256]{1,2,0:T(8,128)(2,1)S(1)}, u32[]{:S(2)}, u32[]{:S(2)}) %collective-permute-start) | collective-permute-done | bytes 262176 | tf_op jit(solution)/shard_map/while/body/eval_jaxpr/ppermute | solution.py:11
  167.3 10.3 %collective-permute-done = bf16[2,256,256]{1,2,0:T(8,128)(2,1)S(1)} collective-permute-done((bf16[2,256,256]{1,2,0:T(8,128)(2,1)S(1)}, bf16[2,256,256]{1,2,0:T(8,128)(2,1)S(1)}, u32[]{:S(2)}, u32[]{:S(2)}) %collective-permute-start) | collective-permute-done | bytes 262176 | tf_op jit(solution)/shard_map/while/body/eval_jaxpr/ppermute | solution.py:11
  181.1 11.1 %collective-permute-done = bf16[2,256,256]{1,2,0:T(8,128)(2,1)S(1)} collective-permute-done((bf16[2,256,256]{1,2,0:T(8,128)(2,1)S(1)}, bf16[2,256,256]{1,2,0:T(8,128)(2,1)S(1)}, u32[]{:S(2)}, u32[]{:S(2)}) %collective-permute-start) | collective-permute-done | bytes 262176 | tf_op jit(solution)/shard_map/while/body/eval_jaxpr/ppermute | solution.py:11
  195.6 10.2 %collective-permute-done = bf16[2,256,256]{1,2,0:T(8,128)(2,1)S(1)} collective-permute-done((bf16[2,256,256]{1,2,0:T(8,128)(2,1)S(1)}, bf16[2,256,256]{1,2,0:T(8,128)(2,1)S(1)}, u32[]{:S(2)}, u32[]{:S(2)}) %collective-permute-start) | collective-permute-done | bytes 262176 | tf_op jit(solution)/shard_map/while/body/eval_jaxpr/ppermute | solution.py:11
  302.0 9.4 %collective-permute-done = bf16[2,256,256]{1,2,0:T(8,128)(2,1)S(1)} collective-permute-done((bf16[2,256,256]{1,2,0:T(8,128)(2,1)S(1)}, bf16[2,256,256]{1,2,0:T(8,128)(2,1)S(1)}, u32[]{:S(2)}, u32[]{:S(2)}) %collective-permute-start) | collective-permute-done | bytes 262176 | tf_op jit(solution)/shard_map/while/body/eval_jaxpr/ppermute | solution.py:11
  314.9 10.5 %collective-permute-done = bf16[2,256,256]{1,2,0:T(8,128)(2,1)S(1)} collective-permute-done((bf16[2,256,256]{1,2,0:T(8,128)(2,1)S(1)}, bf16[2,256,256]{1,2,0:T(8,128)(2,1)S(1)}, u32[]{:S(2)}, u32[]{:S(2)}) %collective-permute-start) | collective-permute-done | bytes 262176 | tf_op jit(solution)/shard_map/while/body/eval_jaxpr/ppermute | solution.py:11
  328.9 10.8 %collective-permute-done = bf16[2,256,256]{1,2,0:T(8,128)(2,1)S(1)} collective-permute-done((bf16[2,256,256]{1,2,0:T(8,128)(2,1)S(1)}, bf16[2,256,256]{1,2,0:T(8,128)(2,1)S(1)}, u32[]{:S(2)}, u32[]{:S(2)}) %collective-permute-start) | collective-permute-done | bytes 262176 | tf_op jit(solution)/shard_map/while/body/eval_jaxpr/ppermute | solution.py:11
  343.2 9.9 %collective-permute-done = bf16[2,256,256]{1,2,0:T(8,128)(2,1)S(1)} collective-permute-done((bf16[2,256,256]{1,2,0:T(8,128)(2,1)S(1)}, bf16[2,256,256]{1,2,0:T(8,128)(2,1)S(1)}, u32[]{:S(2)}, u32[]{:S(2)}) %collective-permute-start) | collective-permute-done | bytes 262176 | tf_op jit(solution)/shard_map/while/body/eval_jaxpr/ppermute | solution.py:11
  356.6 9.0 collective-permute-done
  438.8 9.0 %collective-permute-done = bf16[2,256,256]{1,2,0:T(8,128)(2,1)S(1)} collective-permute-done((bf16[2,256,256]{1,2,0:T(8,128)(2,1)S(1)}, bf16[2,256,256]{1,2,0:T(8,128)(2,1)S(1)}, u32[]{:S(2)}, u32[]{:S(2)}) %collective-permute-start) | collective-permute-done | bytes 262176 | tf_op jit(solution)/shard_map/while/body/eval_jaxpr/ppermute | solution.py:11
  451.4 10.1 %collective-permute-done = bf16[2,256,256]{1,2,0:T(8,128)(2,1)S(1)} collective-permute-done((bf16[2,256,256]{1,2,0:T(8,128)(2,1)S(1)}, bf16[2,256,256]{1,2,0:T(8,128)(2,1)S(1)}, u32[]{:S(2)}, u32[]{:S(2)}) %collective-permute-start) | collective-permute-done | bytes 262176 | tf_op jit(solution)/shard_map/while/body/eval_jaxpr/ppermute | solution.py:11
  465.0 10.6 %collective-permute-done = bf16[2,256,256]{1,2,0:T(8,128)(2,1)S(1)} collective-permute-done((bf16[2,256,256]{1,2,0:T(8,128)(2,1)S(1)}, bf16[2,256,256]{1,2,0:T(8,128)(2,1)S(1)}, u32[]{:S(2)}, u32[]{:S(2)}) %collective-permute-start) | collective-permute-done | bytes 262176 | tf_op jit(solution)/shard_map/while/body/eval_jaxpr/ppermute | solution.py:11
  479.1 10.7 %collective-permute-done = bf16[2,256,256]{1,2,0:T(8,128)(2,1)S(1)} collective-permute-done((bf16[2,256,256]{1,2,0:T(8,128)(2,1)S(1)}, bf16[2,256,256]{1,2,0:T(8,128)(2,1)S(1)}, u32[]{:S(2)}, u32[]{:S(2)}) %collective-permute-start) | collective-permute-done | bytes 262176 | tf_op jit(solution)/shard_map/while/body/eval_jaxpr/ppermute | solution.py:11
  493.2 9.8 %collective-permute-done = bf16[2,256,256]{1,2,0:T(8,128)(2,1)S(1)} collective-permute-done((bf16[2,256,256]{1,2,0:T(8,128)(2,1)S(1)}, bf16[2,256,256]{1,2,0:T(8,128)(2,1)S(1)}, u32[]{:S(2)}, u32[]{:S(2)}) %collective-permute-start) | collective-permute-done | bytes 262176 | tf_op jit(solution)/shard_map/while/body/eval_jaxpr/ppermute | solution.py:11
  506.5 8.8 collective-permute-done
  600.6 9.5 %collective-permute-done = bf16[2,256,256]{1,2,0:T(8,128)(2,1)S(1)} collective-permute-done((bf16[2,256,256]{1,2,0:T(8,128)(2,1)S(1)}, bf16[2,256,256]{1,2,0:T(8,128)(2,1)S(1)}, u32[]{:S(2)}, u32[]{:S(2)}) %collective-permute-start) | collective-permute-done | bytes 262176 | tf_op jit(solution)/shard_map/while/body/eval_jaxpr/ppermute | solution.py:11
  613.6 10.6 %collective-permute-done = bf16[2,256,256]{1,2,0:T(8,128)(2,1)S(1)} collective-permute-done((bf16[2,256,256]{1,2,0:T(8,128)(2,1)S(1)}, bf16[2,256,256]{1,2,0:T(8,128)(2,1)S(1)}, u32[]{:S(2)}, u32[]{:S(2)}) %collective-permute-start) | collective-permute-done | bytes 262176 | tf_op jit(solution)/shard_map/while/body/eval_jaxpr/ppermute | solution.py:11
  627.7 10.6 %collective-permute-done = bf16[2,256,256]{1,2,0:T(8,128)(2,1)S(1)} collective-permute-done((bf16[2,256,256]{1,2,0:T(8,128)(2,1)S(1)}, bf16[2,256,256]{1,2,0:T(8,128)(2,1)S(1)}, u32[]{:S(2)}, u32[]{:S(2)}) %collective-permute-start) | collective-permute-done | bytes 262176 | tf_op jit(solution)/shard_map/while/body/eval_jaxpr/ppermute | solution.py:11
  641.9 9.7 %collective-permute-done = bf16[2,256,256]{1,2,0:T(8,128)(2,1)S(1)} collective-permute-done((bf16[2,256,256]{1,2,0:T(8,128)(2,1)S(1)}, bf16[2,256,256]{1,2,0:T(8,128)(2,1)S(1)}, u32[]{:S(2)}, u32[]{:S(2)}) %collective-permute-start) | collective-permute-done | bytes 262176 | tf_op jit(solution)/shard_map/while/body/eval_jaxpr/ppermute | solution.py:11
  655.1 8.8 collective-permute-done
  737.9 8.5 collective-permute-done
  749.9 9.6 %collective-permute-done = bf16[2,256,256]{1,2,0:T(8,128)(2,1)S(1)} collective-permute-done((bf16[2,256,256]{1,2,0:T(8,128)(2,1)S(1)}, bf16[2,256,256]{1,2,0:T(8,128)(2,1)S(1)}, u32[]{:S(2)}, u32[]{:S(2)}) %collective-permute-start) | collective-permute-done | bytes 262176 | tf_op jit(solution)/shard_map/while/body/eval_jaxpr/ppermute | solution.py:11
  763.0 10.7 %collective-permute-done = bf16[2,256,256]{1,2,0:T(8,128)(2,1)S(1)} collective-permute-done((bf16[2,256,256]{1,2,0:T(8,128)(2,1)S(1)}, bf16[2,256,256]{1,2,0:T(8,128)(2,1)S(1)}, u32[]{:S(2)}, u32[]{:S(2)}) %collective-permute-start) | collective-permute-done | bytes 262176 | tf_op jit(solution)/shard_map/while/body/eval_jaxpr/ppermute | solution.py:11
  777.1 10.6 %collective-permute-done = bf16[2,256,256]{1,2,0:T(8,128)(2,1)S(1)} collective-permute-done((bf16[2,256,256]{1,2,0:T(8,128)(2,1)S(1)}, bf16[2,256,256]{1,2,0:T(8,128)(2,1)S(1)}, u32[]{:S(2)}, u32[]{:S(2)}) %collective-permute-start) | collective-permute-done | bytes 262176 | tf_op jit(solution)/shard_map/while/body/eval_jaxpr/ppermute | solution.py:11
  791.2 9.6 %collective-permute-done = bf16[2,256,256]{1,2,0:T(8,128)(2,1)S(1)} collective-permute-done((bf16[2,256,256]{1,2,0:T(8,128)(2,1)S(1)}, bf16[2,256,256]{1,2,0:T(8,128)(2,1)S(1)}, u32[]{:S(2)}, u32[]{:S(2)}) %collective-permute-start) | collective-permute-done | bytes 262176 | tf_op jit(solution)/shard_map/while/body/eval_jaxpr/ppermute | solution.py:11
  804.3 8.7 collective-permute-done
  814.9 79.4 %reduce-scatter.2.cloned.1.call-done = bf16[256,256]{1,0:T(8,128)(2,1)} async-done(((bf16[256,1024]{1,0:T(8,128)(2,1)}), bf16[256,256]{1,0:T(8,128)(2,1)}) %reduce-scatter.2.cloned.1.call-update) | async-done | bytes 131088 | tf_op jit(solution)/shard_map/reduce_scatter | solution.py:82
  (947 shorter events, 505.0 us)
Async XLA Ops:
  6.5 887.8 %reduce-scatter.2.cloned.1.call-start = ((), (), s32[]{:S(2)}) async-start(), calls=%async_computation.1 | async-start | bytes 655360 | tf_op jit(solution)/shard_map/reduce_scatter | solution.py:82
  26.7 15.7 %collective-permute-start = (bf16[2,256,256]{1,2,0:T(8,128)(2,1)S(1)}, bf16[2,256,256]{1,2,0:T(8,128)(2,1)S(1)}, u32[]{:S(2)}, u32[]{:S(2)}) collective-permute-start(bf16[2,256,256]{1,2,0:T(8,128)(2,1)S(1)} %get-tuple-element.389), channel_id=1, source_target_pairs={{0,4},{4,8},{8,12},{12,16},{16,20},{20,24},{24,28},{28,32},{32,36}... | collective-permute-start | bytes 786440 | tf_op jit(solution)/shard_map/while/body/eval_jaxpr/ppermute | solution.py:11
  43.2 12.9 %collective-permute-start = (bf16[2,256,256]{1,2,0:T(8,128)(2,1)S(1)}, bf16[2,256,256]{1,2,0:T(8,128)(2,1)S(1)}, u32[]{:S(2)}, u32[]{:S(2)}) collective-permute-start(bf16[2,256,256]{1,2,0:T(8,128)(2,1)S(1)} %get-tuple-element.389), channel_id=1, source_target_pairs={{0,4},{4,8},{8,12},{12,16},{16,20},{20,24},{24,28},{28,32},{32,36}... | collective-permute-start | bytes 786440 | tf_op jit(solution)/shard_map/while/body/eval_jaxpr/ppermute | solution.py:11
  56.8 12.0 %collective-permute-start = (bf16[2,256,256]{1,2,0:T(8,128)(2,1)S(1)}, bf16[2,256,256]{1,2,0:T(8,128)(2,1)S(1)}, u32[]{:S(2)}, u32[]{:S(2)}) collective-permute-start(bf16[2,256,256]{1,2,0:T(8,128)(2,1)S(1)} %get-tuple-element.389), channel_id=1, source_target_pairs={{0,4},{4,8},{8,12},{12,16},{16,20},{20,24},{24,28},{28,32},{32,36}... | collective-permute-start | bytes 786440 | tf_op jit(solution)/shard_map/while/body/eval_jaxpr/ppermute | solution.py:11
  151.8 12.0 %collective-permute-start = (bf16[2,256,256]{1,2,0:T(8,128)(2,1)S(1)}, bf16[2,256,256]{1,2,0:T(8,128)(2,1)S(1)}, u32[]{:S(2)}, u32[]{:S(2)}) collective-permute-start(bf16[2,256,256]{1,2,0:T(8,128)(2,1)S(1)} %get-tuple-element.389), channel_id=1, source_target_pairs={{0,4},{4,8},{8,12},{12,16},{16,20},{20,24},{24,28},{28,32},{32,36}... | collective-permute-start | bytes 786440 | tf_op jit(solution)/shard_map/while/body/eval_jaxpr/ppermute | solution.py:11
  164.5 13.1 %collective-permute-start = (bf16[2,256,256]{1,2,0:T(8,128)(2,1)S(1)}, bf16[2,256,256]{1,2,0:T(8,128)(2,1)S(1)}, u32[]{:S(2)}, u32[]{:S(2)}) collective-permute-start(bf16[2,256,256]{1,2,0:T(8,128)(2,1)S(1)} %get-tuple-element.389), channel_id=1, source_target_pairs={{0,4},{4,8},{8,12},{12,16},{16,20},{20,24},{24,28},{28,32},{32,36}... | collective-permute-start | bytes 786440 | tf_op jit(solution)/shard_map/while/body/eval_jaxpr/ppermute | solution.py:11
  178.3 13.8 %collective-permute-start = (bf16[2,256,256]{1,2,0:T(8,128)(2,1)S(1)}, bf16[2,256,256]{1,2,0:T(8,128)(2,1)S(1)}, u32[]{:S(2)}, u32[]{:S(2)}) collective-permute-start(bf16[2,256,256]{1,2,0:T(8,128)(2,1)S(1)} %get-tuple-element.389), channel_id=1, source_target_pairs={{0,4},{4,8},{8,12},{12,16},{16,20},{20,24},{24,28},{28,32},{32,36}... | collective-permute-start | bytes 786440 | tf_op jit(solution)/shard_map/while/body/eval_jaxpr/ppermute | solution.py:11
  192.9 12.9 %collective-permute-start = (bf16[2,256,256]{1,2,0:T(8,128)(2,1)S(1)}, bf16[2,256,256]{1,2,0:T(8,128)(2,1)S(1)}, u32[]{:S(2)}, u32[]{:S(2)}) collective-permute-start(bf16[2,256,256]{1,2,0:T(8,128)(2,1)S(1)} %get-tuple-element.389), channel_id=1, source_target_pairs={{0,4},{4,8},{8,12},{12,16},{16,20},{20,24},{24,28},{28,32},{32,36}... | collective-permute-start | bytes 786440 | tf_op jit(solution)/shard_map/while/body/eval_jaxpr/ppermute | solution.py:11
  287.4 11.1 %collective-permute-start = (bf16[2,256,256]{1,2,0:T(8,128)(2,1)S(1)}, bf16[2,256,256]{1,2,0:T(8,128)(2,1)S(1)}, u32[]{:S(2)}, u32[]{:S(2)}) collective-permute-start(bf16[2,256,256]{1,2,0:T(8,128)(2,1)S(1)} %get-tuple-element.389), channel_id=1, source_target_pairs={{0,4},{4,8},{8,12},{12,16},{16,20},{20,24},{24,28},{28,32},{32,36}... | collective-permute-start | bytes 786440 | tf_op jit(solution)/shard_map/while/body/eval_jaxpr/ppermute | solution.py:11
  299.3 12.2 %collective-permute-start = (bf16[2,256,256]{1,2,0:T(8,128)(2,1)S(1)}, bf16[2,256,256]{1,2,0:T(8,128)(2,1)S(1)}, u32[]{:S(2)}, u32[]{:S(2)}) collective-permute-start(bf16[2,256,256]{1,2,0:T(8,128)(2,1)S(1)} %get-tuple-element.389), channel_id=1, source_target_pairs={{0,4},{4,8},{8,12},{12,16},{16,20},{20,24},{24,28},{28,32},{32,36}... | collective-permute-start | bytes 786440 | tf_op jit(solution)/shard_map/while/body/eval_jaxpr/ppermute | solution.py:11
  312.2 13.3 %collective-permute-start = (bf16[2,256,256]{1,2,0:T(8,128)(2,1)S(1)}, bf16[2,256,256]{1,2,0:T(8,128)(2,1)S(1)}, u32[]{:S(2)}, u32[]{:S(2)}) collective-permute-start(bf16[2,256,256]{1,2,0:T(8,128)(2,1)S(1)} %get-tuple-element.389), channel_id=1, source_target_pairs={{0,4},{4,8},{8,12},{12,16},{16,20},{20,24},{24,28},{28,32},{32,36}... | collective-permute-start | bytes 786440 | tf_op jit(solution)/shard_map/while/body/eval_jaxpr/ppermute | solution.py:11
  326.2 13.6 %collective-permute-start = (bf16[2,256,256]{1,2,0:T(8,128)(2,1)S(1)}, bf16[2,256,256]{1,2,0:T(8,128)(2,1)S(1)}, u32[]{:S(2)}, u32[]{:S(2)}) collective-permute-start(bf16[2,256,256]{1,2,0:T(8,128)(2,1)S(1)} %get-tuple-element.389), channel_id=1, source_target_pairs={{0,4},{4,8},{8,12},{12,16},{16,20},{20,24},{24,28},{28,32},{32,36}... | collective-permute-start | bytes 786440 | tf_op jit(solution)/shard_map/while/body/eval_jaxpr/ppermute | solution.py:11
  340.4 12.6 %collective-permute-start = (bf16[2,256,256]{1,2,0:T(8,128)(2,1)S(1)}, bf16[2,256,256]{1,2,0:T(8,128)(2,1)S(1)}, u32[]{:S(2)}, u32[]{:S(2)}) collective-permute-start(bf16[2,256,256]{1,2,0:T(8,128)(2,1)S(1)} %get-tuple-element.389), channel_id=1, source_target_pairs={{0,4},{4,8},{8,12},{12,16},{16,20},{20,24},{24,28},{28,32},{32,36}... | collective-permute-start | bytes 786440 | tf_op jit(solution)/shard_map/while/body/eval_jaxpr/ppermute | solution.py:11
  353.8 11.7 %collective-permute-start = (bf16[2,256,256]{1,2,0:T(8,128)(2,1)S(1)}, bf16[2,256,256]{1,2,0:T(8,128)(2,1)S(1)}, u32[]{:S(2)}, u32[]{:S(2)}) collective-permute-start(bf16[2,256,256]{1,2,0:T(8,128)(2,1)S(1)} %get-tuple-element.389), channel_id=1, source_target_pairs={{0,4},{4,8},{8,12},{12,16},{16,20},{20,24},{24,28},{28,32},{32,36}... | collective-permute-start | bytes 786440 | tf_op jit(solution)/shard_map/while/body/eval_jaxpr/ppermute | solution.py:11
  436.1 11.8 %collective-permute-start = (bf16[2,256,256]{1,2,0:T(8,128)(2,1)S(1)}, bf16[2,256,256]{1,2,0:T(8,128)(2,1)S(1)}, u32[]{:S(2)}, u32[]{:S(2)}) collective-permute-start(bf16[2,256,256]{1,2,0:T(8,128)(2,1)S(1)} %get-tuple-element.389), channel_id=1, source_target_pairs={{0,4},{4,8},{8,12},{12,16},{16,20},{20,24},{24,28},{28,32},{32,36}... | collective-permute-start | bytes 786440 | tf_op jit(solution)/shard_map/while/body/eval_jaxpr/ppermute | solution.py:11
  448.6 12.9 %collective-permute-start = (bf16[2,256,256]{1,2,0:T(8,128)(2,1)S(1)}, bf16[2,256,256]{1,2,0:T(8,128)(2,1)S(1)}, u32[]{:S(2)}, u32[]{:S(2)}) collective-permute-start(bf16[2,256,256]{1,2,0:T(8,128)(2,1)S(1)} %get-tuple-element.389), channel_id=1, source_target_pairs={{0,4},{4,8},{8,12},{12,16},{16,20},{20,24},{24,28},{28,32},{32,36}... | collective-permute-start | bytes 786440 | tf_op jit(solution)/shard_map/while/body/eval_jaxpr/ppermute | solution.py:11
  462.2 13.3 %collective-permute-start = (bf16[2,256,256]{1,2,0:T(8,128)(2,1)S(1)}, bf16[2,256,256]{1,2,0:T(8,128)(2,1)S(1)}, u32[]{:S(2)}, u32[]{:S(2)}) collective-permute-start(bf16[2,256,256]{1,2,0:T(8,128)(2,1)S(1)} %get-tuple-element.389), channel_id=1, source_target_pairs={{0,4},{4,8},{8,12},{12,16},{16,20},{20,24},{24,28},{28,32},{32,36}... | collective-permute-start | bytes 786440 | tf_op jit(solution)/shard_map/while/body/eval_jaxpr/ppermute | solution.py:11
  476.3 13.4 %collective-permute-start = (bf16[2,256,256]{1,2,0:T(8,128)(2,1)S(1)}, bf16[2,256,256]{1,2,0:T(8,128)(2,1)S(1)}, u32[]{:S(2)}, u32[]{:S(2)}) collective-permute-start(bf16[2,256,256]{1,2,0:T(8,128)(2,1)S(1)} %get-tuple-element.389), channel_id=1, source_target_pairs={{0,4},{4,8},{8,12},{12,16},{16,20},{20,24},{24,28},{28,32},{32,36}... | collective-permute-start | bytes 786440 | tf_op jit(solution)/shard_map/while/body/eval_jaxpr/ppermute | solution.py:11
  490.5 12.5 %collective-permute-start = (bf16[2,256,256]{1,2,0:T(8,128)(2,1)S(1)}, bf16[2,256,256]{1,2,0:T(8,128)(2,1)S(1)}, u32[]{:S(2)}, u32[]{:S(2)}) collective-permute-start(bf16[2,256,256]{1,2,0:T(8,128)(2,1)S(1)} %get-tuple-element.389), channel_id=1, source_target_pairs={{0,4},{4,8},{8,12},{12,16},{16,20},{20,24},{24,28},{28,32},{32,36}... | collective-permute-start | bytes 786440 | tf_op jit(solution)/shard_map/while/body/eval_jaxpr/ppermute | solution.py:11
  503.7 11.6 %collective-permute-start = (bf16[2,256,256]{1,2,0:T(8,128)(2,1)S(1)}, bf16[2,256,256]{1,2,0:T(8,128)(2,1)S(1)}, u32[]{:S(2)}, u32[]{:S(2)}) collective-permute-start(bf16[2,256,256]{1,2,0:T(8,128)(2,1)S(1)} %get-tuple-element.389), channel_id=1, source_target_pairs={{0,4},{4,8},{8,12},{12,16},{16,20},{20,24},{24,28},{28,32},{32,36}... | collective-permute-start | bytes 786440 | tf_op jit(solution)/shard_map/while/body/eval_jaxpr/ppermute | solution.py:11
  585.9 11.2 %collective-permute-start = (bf16[2,256,256]{1,2,0:T(8,128)(2,1)S(1)}, bf16[2,256,256]{1,2,0:T(8,128)(2,1)S(1)}, u32[]{:S(2)}, u32[]{:S(2)}) collective-permute-start(bf16[2,256,256]{1,2,0:T(8,128)(2,1)S(1)} %get-tuple-element.389), channel_id=1, source_target_pairs={{0,4},{4,8},{8,12},{12,16},{16,20},{20,24},{24,28},{28,32},{32,36}... | collective-permute-start | bytes 786440 | tf_op jit(solution)/shard_map/while/body/eval_jaxpr/ppermute | solution.py:11
  597.8 12.3 %collective-permute-start = (bf16[2,256,256]{1,2,0:T(8,128)(2,1)S(1)}, bf16[2,256,256]{1,2,0:T(8,128)(2,1)S(1)}, u32[]{:S(2)}, u32[]{:S(2)}) collective-permute-start(bf16[2,256,256]{1,2,0:T(8,128)(2,1)S(1)} %get-tuple-element.389), channel_id=1, source_target_pairs={{0,4},{4,8},{8,12},{12,16},{16,20},{20,24},{24,28},{28,32},{32,36}... | collective-permute-start | bytes 786440 | tf_op jit(solution)/shard_map/while/body/eval_jaxpr/ppermute | solution.py:11
  610.9 13.4 %collective-permute-start = (bf16[2,256,256]{1,2,0:T(8,128)(2,1)S(1)}, bf16[2,256,256]{1,2,0:T(8,128)(2,1)S(1)}, u32[]{:S(2)}, u32[]{:S(2)}) collective-permute-start(bf16[2,256,256]{1,2,0:T(8,128)(2,1)S(1)} %get-tuple-element.389), channel_id=1, source_target_pairs={{0,4},{4,8},{8,12},{12,16},{16,20},{20,24},{24,28},{28,32},{32,36}... | collective-permute-start | bytes 786440 | tf_op jit(solution)/shard_map/while/body/eval_jaxpr/ppermute | solution.py:11
  625.0 13.4 %collective-permute-start = (bf16[2,256,256]{1,2,0:T(8,128)(2,1)S(1)}, bf16[2,256,256]{1,2,0:T(8,128)(2,1)S(1)}, u32[]{:S(2)}, u32[]{:S(2)}) collective-permute-start(bf16[2,256,256]{1,2,0:T(8,128)(2,1)S(1)} %get-tuple-element.389), channel_id=1, source_target_pairs={{0,4},{4,8},{8,12},{12,16},{16,20},{20,24},{24,28},{28,32},{32,36}... | collective-permute-start | bytes 786440 | tf_op jit(solution)/shard_map/while/body/eval_jaxpr/ppermute | solution.py:11
  639.1 12.5 %collective-permute-start = (bf16[2,256,256]{1,2,0:T(8,128)(2,1)S(1)}, bf16[2,256,256]{1,2,0:T(8,128)(2,1)S(1)}, u32[]{:S(2)}, u32[]{:S(2)}) collective-permute-start(bf16[2,256,256]{1,2,0:T(8,128)(2,1)S(1)} %get-tuple-element.389), channel_id=1, source_target_pairs={{0,4},{4,8},{8,12},{12,16},{16,20},{20,24},{24,28},{28,32},{32,36}... | collective-permute-start | bytes 786440 | tf_op jit(solution)/shard_map/while/body/eval_jaxpr/ppermute | solution.py:11
  652.3 11.5 %collective-permute-start = (bf16[2,256,256]{1,2,0:T(8,128)(2,1)S(1)}, bf16[2,256,256]{1,2,0:T(8,128)(2,1)S(1)}, u32[]{:S(2)}, u32[]{:S(2)}) collective-permute-start(bf16[2,256,256]{1,2,0:T(8,128)(2,1)S(1)} %get-tuple-element.389), channel_id=1, source_target_pairs={{0,4},{4,8},{8,12},{12,16},{16,20},{20,24},{24,28},{28,32},{32,36}... | collective-permute-start | bytes 786440 | tf_op jit(solution)/shard_map/while/body/eval_jaxpr/ppermute | solution.py:11
  735.1 11.3 %collective-permute-start = (bf16[2,256,256]{1,2,0:T(8,128)(2,1)S(1)}, bf16[2,256,256]{1,2,0:T(8,128)(2,1)S(1)}, u32[]{:S(2)}, u32[]{:S(2)}) collective-permute-start(bf16[2,256,256]{1,2,0:T(8,128)(2,1)S(1)} %get-tuple-element.389), channel_id=1, source_target_pairs={{0,4},{4,8},{8,12},{12,16},{16,20},{20,24},{24,28},{28,32},{32,36}... | collective-permute-start | bytes 786440 | tf_op jit(solution)/shard_map/while/body/eval_jaxpr/ppermute | solution.py:11
  747.1 12.3 %collective-permute-start = (bf16[2,256,256]{1,2,0:T(8,128)(2,1)S(1)}, bf16[2,256,256]{1,2,0:T(8,128)(2,1)S(1)}, u32[]{:S(2)}, u32[]{:S(2)}) collective-permute-start(bf16[2,256,256]{1,2,0:T(8,128)(2,1)S(1)} %get-tuple-element.389), channel_id=1, source_target_pairs={{0,4},{4,8},{8,12},{12,16},{16,20},{20,24},{24,28},{28,32},{32,36}... | collective-permute-start | bytes 786440 | tf_op jit(solution)/shard_map/while/body/eval_jaxpr/ppermute | solution.py:11
  760.2 13.4 %collective-permute-start = (bf16[2,256,256]{1,2,0:T(8,128)(2,1)S(1)}, bf16[2,256,256]{1,2,0:T(8,128)(2,1)S(1)}, u32[]{:S(2)}, u32[]{:S(2)}) collective-permute-start(bf16[2,256,256]{1,2,0:T(8,128)(2,1)S(1)} %get-tuple-element.389), channel_id=1, source_target_pairs={{0,4},{4,8},{8,12},{12,16},{16,20},{20,24},{24,28},{28,32},{32,36}... | collective-permute-start | bytes 786440 | tf_op jit(solution)/shard_map/while/body/eval_jaxpr/ppermute | solution.py:11
  774.4 13.3 %collective-permute-start = (bf16[2,256,256]{1,2,0:T(8,128)(2,1)S(1)}, bf16[2,256,256]{1,2,0:T(8,128)(2,1)S(1)}, u32[]{:S(2)}, u32[]{:S(2)}) collective-permute-start(bf16[2,256,256]{1,2,0:T(8,128)(2,1)S(1)} %get-tuple-element.389), channel_id=1, source_target_pairs={{0,4},{4,8},{8,12},{12,16},{16,20},{20,24},{24,28},{28,32},{32,36}... | collective-permute-start | bytes 786440 | tf_op jit(solution)/shard_map/while/body/eval_jaxpr/ppermute | solution.py:11
  788.4 12.4 %collective-permute-start = (bf16[2,256,256]{1,2,0:T(8,128)(2,1)S(1)}, bf16[2,256,256]{1,2,0:T(8,128)(2,1)S(1)}, u32[]{:S(2)}, u32[]{:S(2)}) collective-permute-start(bf16[2,256,256]{1,2,0:T(8,128)(2,1)S(1)} %get-tuple-element.389), channel_id=1, source_target_pairs={{0,4},{4,8},{8,12},{12,16},{16,20},{20,24},{24,28},{28,32},{32,36}... | collective-permute-start | bytes 786440 | tf_op jit(solution)/shard_map/while/body/eval_jaxpr/ppermute | solution.py:11
  801.5 11.5 %collective-permute-start = (bf16[2,256,256]{1,2,0:T(8,128)(2,1)S(1)}, bf16[2,256,256]{1,2,0:T(8,128)(2,1)S(1)}, u32[]{:S(2)}, u32[]{:S(2)}) collective-permute-start(bf16[2,256,256]{1,2,0:T(8,128)(2,1)S(1)} %get-tuple-element.389), channel_id=1, source_target_pairs={{0,4},{4,8},{8,12},{12,16},{16,20},{20,24},{24,28},{28,32},{32,36}... | collective-permute-start | bytes 786440 | tf_op jit(solution)/shard_map/while/body/eval_jaxpr/ppermute | solution.py:11
  (40 other events, 1175.5 us)
Sparse Core Ops, SparseCore 0:
  815.1 79.2 reduce-scatter.1
where the time goes:
time: 904 us; the launch traced here: 901 us
  waiting for transfers between devices  649 us (72%)
  local copies, waits for them, and re-layouts  82.8 us (9%)
  other arithmetic  53.9 us (6%)
  loops' own time  45.3 us (5%)
  matrix products  40.7 us (5%)
  between operations  14.2 us (2%)
  blocking collectives  9.72 us (1%)
    ppermute x63, waiting for transfers between devices, shifted(): lax.ppermute(shard, axis, [(i, (i + by) % length) for i in range(length)])  570 us
    reduce_scatter x1, waiting for transfers between devices, shards(): lax.psum_scatter(partial_value.astype(jnp.bfloat16), 'head', scatter_dime...  79.4 us
    gather x64, local copies, waits for them, and re-layouts, attend(): allowed = (jnp.take(query_live, key_block, axis=1) > 0) & True  62 us
    reduce_or x64, other arithmetic, attend(): return lax.cond(jnp.any(allowed), compute, keep, carry)  50.5 us
    another operation x1, loops' own time, shards(): moved, state = lax.fori_loop(0, cycle - 1, turn, (stacked, state))  44.3 us
    dot_general x60, matrix products, compute(): jnp.einsum('qhd,khd->hqk', query, keys_piece, preferred_element_type=jnp....  25.2 us
  transfers between devices with their start and end apart: 64, of which 64 were waited for; matrix products, arithmetic and copies ran while one was open for 14% of the time, Pallas kernels for 0%

commit v1 on v0

v1 whole, which is shorter than its diff:
```python
import jax
import jax.numpy as jnp
from jax import lax
from jax.experimental import pallas as pl
from jax.experimental.pallas import tpu as pltpu
from jax.sharding import Mesh, PartitionSpec as P

CTX = ("xh", "z", "y")
HEAD = ("xl", "core")
NXH, NZ, NY, NXL, NCORE = 2, 8, 4, 2, 2
SWAP = ("xh", "y", "core")
BLOCK = 128
HD = 64
ROWS = 256
EPS = 1e-06
LOG2E = 1.4426950408889634
DEAD = -30000.0
F32 = jnp.float32
BF16 = jnp.bfloat16
VMEM = pl.BlockSpec(memory_space=pltpu.VMEM)
SMEM = pl.BlockSpec(memory_space=pltpu.SMEM)


def swap_index(xh, y, core):
    return (xh * NY + y) * NCORE + core


def forward_pairs(s):
    return [
        (swap_index(xh, y, k), swap_index(k, (y + s) % NY, xh))
        for xh in range(NXH)
        for y in range(NY)
        for k in range(NCORE)
    ]


def backward_pairs(s):
    return [(b, a) for a, b in forward_pairs(s)]


def project_kernel(y_ref, x_ref, gain_ref, wq_ref, wk_ref, wv_ref, temper_ref, out_ref):
    y = y_ref[0]
    x = x_ref[...].astype(F32)
    scale = lax.rsqrt(jnp.mean(x * x, axis=-1, keepdims=True) + EPS)
    normed = (x * scale * gain_ref[...]).astype(BF16)
    query = jnp.dot(normed, wq_ref[...], preferred_element_type=F32)
    keys = jnp.dot(normed, wk_ref[...], preferred_element_type=F32)
    values = jnp.dot(normed, wv_ref[...], preferred_element_type=F32)

    def unit(part):
        return part * lax.rsqrt(jnp.mean(part * part, axis=-1, keepdims=True) + EPS)

    for j in range(4):
        cols = slice(HD * j, HD * (j + 1))
        q = unit(query[:, cols]) * (temper_ref[0, j] * (LOG2E / HD))
        k = unit(keys[:, cols])
        v = values[:, cols]
        slot = lax.rem(j - y + NY, NY)
        out_ref[slot, :ROWS, :] = jnp.concatenate([k, v], axis=1).astype(BF16)
        out_ref[slot, ROWS:, :] = jnp.concatenate([q[:BLOCK], q[BLOCK:]], axis=1).astype(BF16)


def project(y, whole, gain, w_query, w_key, w_value, temper):
    return pl.pallas_call(
        project_kernel,
        out_shape=jax.ShapeDtypeStruct((4, ROWS + BLOCK, 128), BF16),
        in_specs=[SMEM, VMEM, VMEM, VMEM, VMEM, VMEM, SMEM],
        out_specs=VMEM,
        compiler_params=pltpu.CompilerParams(vmem_limit_bytes=32 << 20),
        name="project",
    )(y, whole, gain, w_query, w_key, w_value, temper)


QT = 256
KT = 512
NQ = 2048
NK = 1024


def widen_kernel(mine_ref, other_ref, out_ref):
    lane = lax.broadcasted_iota(jnp.int32, (BLOCK, 128), 1)
    for m in range(8):
        pair = (mine_ref if m < 4 else other_ref)[m % 4].astype(F32)
        for b in range(2):
            part = pair if b == 0 else pltpu.roll(pair, 64, 1)
            flag = jnp.where(lane == HD + 2 * m + b, 1.0, 0.0)
            at = (2 * m + b) * BLOCK
            out_ref[at : at + BLOCK, :] = jnp.where(lane < HD, part, flag).astype(BF16)


def widen(mine, other):
    return pl.pallas_call(
        widen_kernel,
        out_shape=jax.ShapeDtypeStruct((NQ, 128), BF16),
        in_specs=[VMEM, VMEM],
        out_specs=VMEM,
        name="widen",
    )(mine, other)


def attend_kernel(first, pieces, where_ref, q_ref, bias_ref, *refs):
    kv_refs, acc_ref = refs[: len(pieces)], refs[-1]
    lane = lax.broadcasted_iota(jnp.int32, (KT, 128), 1)
    if first:
        acc_ref[...] = jnp.zeros_like(acc_ref)

    for n, (slot, offset) in enumerate(pieces):

        def tile(c, carry):
            kv = kv_refs[n][pl.ds(pl.multiple_of(c * KT, KT), KT), :].astype(F32)
            at = offset // BLOCK + c * (KT // BLOCK)
            chunk = where_ref[slot]
            bias = jnp.concatenate(
                [
                    jnp.broadcast_to(bias_ref[chunk, pl.ds(at + b, 1), :], (BLOCK, 128))
                    for b in range(KT // BLOCK)
                ],
                axis=0,
            )
            kx = jnp.where(lane < HD, kv, bias).astype(BF16)
            vx = jnp.where(lane < HD, 1.0, kv).astype(BF16)
            for t in range(NQ // QT):
                rows = slice(t * QT, (t + 1) * QT)
                scores = lax.dot_general(
                    q_ref[rows, :], kx, (((1,), (1,)), ((), ())), preferred_element_type=F32
                )
                probs = jnp.exp2(scores).astype(BF16)
                acc_ref[rows, :] += jnp.dot(probs, vx, preferred_element_type=F32)
            return carry

        lax.fori_loop(0, kv_refs[n].shape[0] // KT, tile, 0)


def attend(where, q, bias, kvs, acc):
    first = acc is None
    pieces = tuple((slot, offset) for _, slot, offset in kvs)
    operands = [where, q, bias] + [kv for kv, _, _ in kvs] + ([] if first else [acc])
    body = lambda *refs: attend_kernel(first, pieces, *refs)
    return pl.pallas_call(
        body,
        out_shape=jax.ShapeDtypeStruct((NQ, 128), F32),
        in_specs=[SMEM] + [VMEM] * (len(operands) - 1),
        out_specs=VMEM,
        input_output_aliases={} if first else {len(operands) - 1: 0},
        compiler_params=pltpu.CompilerParams(vmem_limit_bytes=32 << 20),
        cost_estimate=pl.CostEstimate(
            flops=512 * NQ * sum(kv.shape[0] for kv, _, _ in kvs),
            transcendentals=NQ * sum(kv.shape[0] for kv, _, _ in kvs),
            bytes_accessed=4 << 20,
        ),
        name="attend",
    )(*operands)


def finish_kernel(mine_ref, other_ref, out_ref):
    total = mine_ref[...] + other_ref[...]
    ratio = total / pltpu.roll(total, 64, 1)
    lane = lax.broadcasted_iota(jnp.int32, (BLOCK, 128), 1)
    for m in range(4):
        first = pltpu.roll(ratio[2 * m * BLOCK : (2 * m + 1) * BLOCK], 64, 1)
        second = ratio[(2 * m + 1) * BLOCK : (2 * m + 2) * BLOCK]
        out_ref[m] = jnp.where(lane < HD, first, second).astype(BF16)


def finish(mine, other):
    return pl.pallas_call(
        finish_kernel,
        out_shape=jax.ShapeDtypeStruct((4, BLOCK, 128), BF16),
        in_specs=[VMEM, VMEM],
        out_specs=VMEM,
        name="finish",
    )(mine, other)


def output_kernel(y_ref, a_ref, w_ref, out_ref):
    y = y_ref[0]
    lane = lax.broadcasted_iota(jnp.int32, (BLOCK, 128), 1)
    lefts, rights, weights = [], [], []
    for source in range(4):
        for s in range(4):
            pair = a_ref[4 * source + s].astype(F32)
            lefts.append(jnp.where(lane < HD, pair, 0.0).astype(BF16))
            rights.append(jnp.where(lane < HD, 0.0, pair).astype(BF16))
            j = lax.rem(y + s, NY)
            row = pl.multiple_of(source * 256 + j * HD, HD)
            w = w_ref[pl.ds(row, HD), :]
            weights += [w, w]
    w = jnp.concatenate(weights, axis=0)
    out_ref[:BLOCK, :] = jnp.dot(jnp.concatenate(lefts, axis=1), w, preferred_element_type=F32).astype(BF16)
    out_ref[BLOCK:, :] = jnp.dot(jnp.concatenate(rights, axis=1), w, preferred_element_type=F32).astype(BF16)


def output(y, attended, w):
    return pl.pallas_call(
        output_kernel,
        out_shape=jax.ShapeDtypeStruct((ROWS, 256), BF16),
        in_specs=[SMEM, VMEM, VMEM],
        out_specs=VMEM,
        compiler_params=pltpu.CompilerParams(vmem_limit_bytes=32 << 20),
        name="output",
    )(y, attended, w)


def columns(w_out):
    me = lax.axis_index(HEAD)
    pieces = [lax.dynamic_slice_in_dim(w_out, me * 256, 256, 1)]
    for d in (1, 2, 3):
        block = lax.dynamic_slice_in_dim(w_out, ((me + d) % 4) * 256, 256, 1)
        pieces.append(lax.ppermute(block, HEAD, [(i, (i + d) % 4) for i in range(4)]))
    whole = jnp.zeros((1024, 256), w_out.dtype)
    for d in range(4):
        whole = lax.dynamic_update_slice_in_dim(whole, pieces[d], ((me - d) % 4) * 256, 0)
    return whole


def bias_table(adjacency, order):
    core, y, z = lax.axis_index("core"), lax.axis_index("y"), lax.axis_index("z")
    spin = (y - jnp.arange(NY, dtype=jnp.int32)) % NY
    two = jnp.arange(2, dtype=jnp.int32)
    block = lambda xh, zs: 2 * ((xh * NZ + zs[:, None, None]) * NY + spin[None, :, None]) + two[None, None, :]
    keys = block(core, jnp.arange(NZ, dtype=jnp.int32)).reshape(-1)
    queries = jnp.concatenate([block(core, z[None]).reshape(-1), block(1 - core, z[None]).reshape(-1)])
    ids = jnp.arange(128, dtype=jnp.int32)
    pick = lambda at: (order[at][:, None] == ids[None, :]).astype(BF16)
    picked = jnp.dot(pick(queries), adjacency.astype(BF16), preferred_element_type=F32).astype(BF16)
    live = jnp.dot(pick(keys), picked.T, preferred_element_type=F32)
    bias = jnp.where(live > 0.5, 0.0, DEAD)
    return jnp.pad(bias, ((0, 0), (64, 48))).reshape(NZ, NK // BLOCK, 128)


def shards(tokens, gain, w_query, w_key, w_value, w_out, temper, adjacency, order):
    y = lax.axis_index("y").astype(jnp.int32)[None]
    whole = lax.all_gather(tokens, HEAD, axis=1, tiled=True)
    messages = project(y, whole, gain[None, :], w_query, w_key, w_value, temper[None, :])
    got = [lax.ppermute(messages[s], SWAP, forward_pairs(s)) for s in range(NY)]
    got = jnp.stack(got)
    kv = got[:, :ROWS, :].reshape(4 * ROWS, 128)
    query = got[:, ROWS:, :]
    up = [(i, (i + 1) % NZ) for i in range(NZ)]
    down = [(i, (i - 1) % NZ) for i in range(NZ)]
    z = lax.axis_index("z").astype(jnp.int32)
    where = (z + jnp.array([0, -1, 1, -2, 2, -3, 3, 4], jnp.int32)) % NZ
    lower, upper = [kv], [kv]
    query_other = lax.ppermute(query, "core", [(0, 1), (1, 0)])
    lower.append(lax.ppermute(kv, "z", up))
    upper.append(lax.ppermute(kv, "z", down))
    w_columns = columns(w_out)
    bias = bias_table(adjacency, order)
    q = widen(query, query_other)
    acc = attend(where, q, bias, [(kv, 0, 0)], None)
    for d in (1, 2, 3):
        low, high, acc = lax.optimization_barrier((lower[d], upper[d], acc))
        if d < 3:
            lower.append(lax.ppermute(low, "z", up))
            upper.append(lax.ppermute(high, "z", down))
        else:
            far_low = lax.ppermute(low[: NK // 2], "z", up)
            far_high = lax.ppermute(high[NK // 2 :], "z", down)
        acc = attend(where, q, bias, [(low, 2 * d - 1, 0), (high, 2 * d, 0)], acc)
        if d == 2:
            acc, w_columns = lax.optimization_barrier((acc, w_columns))
    acc = attend(where, q, bias, [(far_low, 7, 0), (far_high, 7, NK // 2)], acc)
    other = lax.ppermute(acc[NQ // 2 :], "core", [(0, 1), (1, 0)])
    attended = finish(acc[: NQ // 2], other)
    back = jnp.stack([lax.ppermute(attended[s], SWAP, backward_pairs(s)) for s in range(NY)])
    gathered = lax.all_gather(back, HEAD, axis=0, tiled=True)
    return output(y, gathered, w_columns)


def solution(mesh):
    fine = Mesh(mesh.devices.reshape(NXH, NZ, NY, NXL, NCORE), CTX + HEAD)
    in_specs = (
        P(CTX, HEAD),
        P(),
        P(None, HEAD),
        P(None, HEAD),
        P(None, HEAD),
        P(HEAD, None),
        P(HEAD),
        P(),
        P(),
    )
    return jax.shard_map(shards, mesh=fine, in_specs=in_specs, out_specs=P(CTX, HEAD), check_vma=False)
```

time: 904 us -> 115 us (0.13)
  waiting for transfers between devices: 649 us -> 7.31 us
  local copies, waits for them, and re-layouts: 82.8 us -> 9.71 us
  other arithmetic: 53.9 us -> 0.34 us
  loops' own time: 45.3 us -> 0 us
  Pallas kernels: 0 us -> 41.4 us
  matrix products: 40.7 us -> 0.29 us
  starting transfers between devices: 5.45 us -> 39.5 us
  between operations: 14.2 us -> 0.37 us
    ppermute x63 -> x21, waiting for transfers between devices: 570 us -> 7.31 us  [the longest x4 3.46 us: shards(): lax.ppermute(attended[s], SWAP, backward_pairs(s))]
    reduce_scatter x1 -> x0, waiting for transfers between devices: 79.4 us -> none  [shards(): lax.psum_scatter(partial_value.astype(jnp.bfloat16), 'head', scatter_dime...]
    gather x67 -> x2, local copies, waits for them, and re-layouts: 64.2 us -> 1.43 us  [bias_table(): pick = lambda at: (order[at][:, None] == ids[None, :]).astype(BF16)]
    reduce_or x64 -> x0, other arithmetic: 50.5 us -> none  [attend(): return lax.cond(jnp.any(allowed), compute, keep, carry)]
    another operation x65 -> x0, loops' own time: 45.3 us -> none  [the longest x1 44.3 us: shards(): moved, state = lax.fori_loop(0, cycle - 1, turn, (stacked, state))]
    pallas_call x0 -> x9, Pallas kernels: none -> 41.4 us  [the longest x5 33.1 us: attend(): pl.pallas_call(body, out_shape=jax.ShapeDtypeStruct((NQ, 128), F32), in_s...]
    dot_general x124 -> x1, matrix products: 40.7 us -> 0.29 us  [bias_table(): live = jnp.dot(pick(keys), picked.T, preferred_element_type=F32)]
    ppermute x63 -> x21, starting transfers between devices: 5.45 us -> 39.5 us  [the longest x4 11.1 us: shards(): lax.ppermute(attended[s], SWAP, backward_pairs(s))]
  transfers between devices with their start and end apart: 64 -> 21, of which waited for: 64 -> 5; matrix products, arithmetic and copies ran while one was open for 14% -> 3% of each run, Pallas kernels for 0% -> 27%
where the time goes in v1:
time: 115 us
  Pallas kernels  41.4 us (36%)
  starting transfers between devices  39.5 us (34%)
  blocking collectives  15.9 us (14%)
  local copies, waits for them, and re-layouts  9.71 us (8%)
  waiting for transfers between devices  7.31 us (6%)
    pallas_call x5, Pallas kernels, attend(): pl.pallas_call(body, out_shape=jax.ShapeDtypeStruct((NQ, 128), F32), in_s...  33.1 us
    ppermute x4, starting transfers between devices, shards(): lax.ppermute(attended[s], SWAP, backward_pairs(s))  11.1 us
    ppermute x4, starting transfers between devices, shards(): got = [lax.ppermute(messages[s], SWAP, forward_pairs(s)) for s in range(NY)]  10.5 us
    all_gather x1, blocking collectives, shards(): whole = lax.all_gather(tokens, HEAD, axis=1, tiled=True)  9.92 us
    all_gather x1, blocking collectives, shards(): gathered = lax.all_gather(back, HEAD, axis=0, tiled=True)  6 us
    unnamed x27, local copies, waits for them, and re-layouts  5.8 us
    ppermute x1, starting transfers between devices, shards(): upper.append(lax.ppermute(kv, 'z', down))  5.64 us
    ppermute x2, starting transfers between devices, shards(): upper.append(lax.ppermute(high, 'z', down))  5.59 us
  transfers between devices with their start and end apart: 21, of which 5 were waited for; matrix products, arithmetic and copies ran while one was open for 3% of the time, Pallas kernels for 27%

profile of v1, /device:TPU:1, one launch (start us, length us, event | category | flops | bytes accessed | tf_op | source)
XLA Modules:
  0.0 114.8 jit_solution(18207704201188996571)
XLA Ops:
  0.0 9.9 %all_gather.6.x_ref = bf16[256,1024]{1,0:T(8,128)(2,1)S(1)} all-gather(bf16[256,256]{1,0:T(8,128)(2,1)} %param.10), channel_id=1, replica_groups=mesh['xh'=2,'z'=8,'y'=4,'xl'=2,'core'=2] {'xl','core'}, dimensions={1}, use_global_device_ids=true | all-gather | bytes 655360 | tf_op jit(solution)/shard_map/all_gather | solution.py:233
  10.6 1.0 copy-done.3
  11.7 1.0 copy-done.4
  12.7 3.1 %project.1 = bf16[4,384,128]{2,1,0:T(8,128)(2,1)S(1)} custom-call(s32[1]{0:T(128)} %bitcast.y_ref, bf16[256,1024]{1,0:T(8,128)(2,1)S(1)} %all_gather.6.x_ref, f32[1,1024]{1,0:T(1,128)S(1)} %bitcast.45, bf16[1024,256]{1,0:T(8,128)(2,1)S(1)} %copy-done.2, bf16[1024,256]{1,0:T(8,128)(2,1)S(1)} %copy-done.3, bf16[1024,256]{1,0:T(8,128)(2,1)S(1)} %copy-done.4, ...), custom_call_target="tpu_custom_call" | custom-call | tf_op jit(solution)/shard_map/project/pallas_call | solution.py:64
  15.8 3.5 %collective-permute-start = (bf16[384,128]{1,0:T(8,128)(2,1)S(1)}, bf16[384,128]{1,0:T(8,128)(2,1)S(1)}, u32[]{:S(2)}, u32[]{:S(2)}) collective-permute-start(bf16[384,128]{1,0:T(8,128)(2,1)S(1)} %get-tuple-element.33), channel_id=1, source_target_pairs={{0,0},{1,128},{4,4},{5,132},{8,8},{9,136},{12,12},{13,140},{128,1}... | collective-permute-start | bytes 294920 | tf_op jit(solution)/shard_map/ppermute | solution.py:235
  19.3 3.3 %collective-permute-start.3 = (bf16[384,128]{1,0:T(8,128)(2,1)S(1)}, bf16[384,128]{1,0:T(8,128)(2,1)S(1)}, u32[]{:S(2)}, u32[]{:S(2)}) collective-permute-start(bf16[384,128]{1,0:T(8,128)(2,1)S(1)} %get-tuple-element.34), channel_id=1, source_target_pairs={{0,12},{1,140},{4,0},{5,128},{8,4},{9,132},{12,8},{13,136},{128,13... | collective-permute-start | bytes 294920 | tf_op jit(solution)/shard_map/ppermute | solution.py:235
  22.6 2.6 %collective-permute-start.2 = (bf16[384,128]{1,0:T(8,128)(2,1)S(1)}, bf16[384,128]{1,0:T(8,128)(2,1)S(1)}, u32[]{:S(2)}, u32[]{:S(2)}) collective-permute-start(bf16[384,128]{1,0:T(8,128)(2,1)S(1)} %get-tuple-element.35), channel_id=1, source_target_pairs={{0,8},{1,136},{4,12},{5,140},{8,0},{9,128},{12,4},{13,132},{128,9}... | collective-permute-start | bytes 294920 | tf_op jit(solution)/shard_map/ppermute | solution.py:235
  25.2 1.2 %collective-permute-start.1 = (bf16[384,128]{1,0:T(8,128)(2,1)S(1)}, bf16[384,128]{1,0:T(8,128)(2,1)S(1)}, u32[]{:S(2)}, u32[]{:S(2)}) collective-permute-start(bf16[384,128]{1,0:T(8,128)(2,1)S(1)} %get-tuple-element.36), channel_id=1, source_target_pairs={{0,4},{1,132},{4,8},{5,136},{8,12},{9,140},{12,0},{13,128},{128,5}... | collective-permute-start | bytes 294920 | tf_op jit(solution)/shard_map/ppermute | solution.py:235
  29.7 1.8 %collective-permute-start.11 = (bf16[256,256]{1,0:T(8,128)(2,1)S(1)}, bf16[256,256]{1,0:T(8,128)(2,1)S(1)}, u32[]{:S(2)}, u32[]{:S(2)}) collective-permute-start(bf16[256,256]{1,0:T(8,128)(2,1)S(1)} %get-tuple-element.30), channel_id=1, source_target_pairs={{0,1},{1,2},{2,3},{3,0},{4,5},{5,6},{6,7},{7,4},{8,9},{9,10},{10,1... | collective-permute-start | bytes 393224 | tf_op jit(solution)/shard_map/ppermute | solution.py:209
  31.5 1.4 %collective-permute-done.1 = bf16[384,128]{1,0:T(8,128)(2,1)S(1)} collective-permute-done((bf16[384,128]{1,0:T(8,128)(2,1)S(1)}, bf16[384,128]{1,0:T(8,128)(2,1)S(1)}, u32[]{:S(2)}, u32[]{:S(2)}) %collective-permute-start.1) | collective-permute-done | bytes 98336 | tf_op jit(solution)/shard_map/ppermute | solution.py:235
  32.9 5.6 %collective-permute-start.6 = (bf16[1024,128]{1,0:T(8,128)(2,1)S(1)}, bf16[1024,128]{1,0:T(8,128)(2,1)S(1)}, u32[]{:S(2)}, u32[]{:S(2)}) collective-permute-start(bf16[1024,128]{1,0:T(8,128)(2,1)S(1)} %bitcast.42), channel_id=1, source_target_pairs={{0,112},{16,0},{32,16},{48,32},{64,48},{80,64},{96,80},{112,96},{1... | collective-permute-start | bytes 786440 | tf_op jit(solution)/shard_map/ppermute | solution.py:246
  40.5 1.9 %widen.1.refs_1_ = bf16[2048,128]{1,0:T(8,128)(2,1)} custom-call(bf16[4,128,128]{2,1,0:T(8,128)(2,1)} %copy-done.9, bf16[4,128,128]{2,1,0:T(8,128)(2,1)} %copy-done.10), custom_call_target="tpu_custom_call" | custom-call | tf_op jit(solution)/shard_map/widen/pallas_call | solution.py:92
  42.4 1.0 copy-done.1
  43.5 4.4 %attend.5.refs_5_ = f32[2048,128]{1,0:T(8,128)S(1)} custom-call(s32[8]{0:T(128)S(1)} %and_select_fusion.1.refs_0_, bf16[2048,128]{1,0:T(8,128)(2,1)S(1)} %copy-done.1, f32[8,8,128]{2,1,0:T(8,128)S(1)} %pad_bitcast_fusion.refs_2_, bf16[1024,128]{1,0:T(8,128)(2,1)S(1)} %bitcast.44), custom_call_target="tpu_custom_call" | custom-call | flops 1073741824 | bytes 4194304 | tf_op jit(solution)/shard_map/attend/pallas_call | solution.py:139
  48.0 2.9 %collective-permute-start.8 = (bf16[1024,128]{1,0:T(8,128)(2,1)S(1)}, bf16[1024,128]{1,0:T(8,128)(2,1)S(1)}, u32[]{:S(2)}, u32[]{:S(2)}) collective-permute-start(bf16[1024,128]{1,0:T(8,128)(2,1)S(1)} %collective-permute-done.6.refs_4_), channel_id=1, source_target_pairs={{0,112},{16,0},{32,16},{48,32},{64,48},{80,64},{96,80},{112,96},{1... | collective-permute-start | bytes 786440 | tf_op jit(solution)/shard_map/ppermute | solution.py:255
  51.0 8.2 %attend.6.refs_5_ = f32[2048,128]{1,0:T(8,128)S(1)} custom-call(s32[8]{0:T(128)S(1)} %and_select_fusion.1.refs_0_, bf16[2048,128]{1,0:T(8,128)(2,1)S(1)} %copy-done.1, f32[8,8,128]{2,1,0:T(8,128)S(1)} %pad_bitcast_fusion.refs_2_, bf16[1024,128]{1,0:T(8,128)(2,1)S(1)} %collective-permute-done.5.refs_3_, ...), custom_call_target="tpu_custom_call", output_to_operand_aliasing={{}: (5, {})} | custom-call | flops 2147483648 | bytes 4194304 | tf_op jit(solution)/shard_map/attend/pallas_call | solution.py:139
  59.3 2.7 %collective-permute-start.10 = (bf16[1024,128]{1,0:T(8,128)(2,1)S(1)}, bf16[1024,128]{1,0:T(8,128)(2,1)S(1)}, u32[]{:S(2)}, u32[]{:S(2)}) collective-permute-start(bf16[1024,128]{1,0:T(8,128)(2,1)S(1)} %collective-permute-done.8.refs_4_), channel_id=1, source_target_pairs={{0,112},{16,0},{32,16},{48,32},{64,48},{80,64},{96,80},{112,96},{1... | collective-permute-start | bytes 786440 | tf_op jit(solution)/shard_map/ppermute | solution.py:255
  61.9 8.2 %attend.7.refs_5_ = f32[2048,128]{1,0:T(8,128)S(1)} custom-call(s32[8]{0:T(128)S(1)} %and_select_fusion.1.refs_0_, bf16[2048,128]{1,0:T(8,128)(2,1)S(1)} %copy-done.1, f32[8,8,128]{2,1,0:T(8,128)S(1)} %pad_bitcast_fusion.refs_2_, bf16[1024,128]{1,0:T(8,128)(2,1)S(1)} %collective-permute-done.7.refs_3_, ...), custom_call_target="tpu_custom_call", output_to_operand_aliasing={{}: (5, {})} | custom-call | flops 2147483648 | bytes 4194304 | tf_op jit(solution)/shard_map/attend/pallas_call | solution.py:139
  70.3 2.7 %collective-permute-start.15 = (bf16[512,128]{1,0:T(8,128)(2,1)S(1)}, bf16[512,128]{1,0:T(8,128)(2,1)S(1)}, u32[]{:S(2)}, u32[]{:S(2)}) collective-permute-start(bf16[512,128]{1,0:T(8,128)(2,1)S(1)} %slice.49), channel_id=1, source_target_pairs={{0,112},{16,0},{32,16},{48,32},{64,48},{80,64},{96,80},{112,96},{1... | collective-permute-start | bytes 393224 | tf_op jit(solution)/shard_map/ppermute | solution.py:258
  72.9 8.2 %attend.8.refs_5_ = f32[2048,128]{1,0:T(8,128)S(1)} custom-call(s32[8]{0:T(128)S(1)} %and_select_fusion.1.refs_0_, bf16[2048,128]{1,0:T(8,128)(2,1)S(1)} %copy-done.1, f32[8,8,128]{2,1,0:T(8,128)S(1)} %pad_bitcast_fusion.refs_2_, bf16[1024,128]{1,0:T(8,128)(2,1)S(1)} %collective-permute-done.9.refs_3_, ...), custom_call_target="tpu_custom_call", output_to_operand_aliasing={{}: (5, {})} | custom-call | flops 2147483648 | bytes 4194304 | tf_op jit(solution)/shard_map/attend/pallas_call | solution.py:139
  81.1 4.2 %attend.9 = f32[2048,128]{1,0:T(8,128)S(1)} custom-call(s32[8]{0:T(128)S(1)} %and_select_fusion.1.refs_0_, bf16[2048,128]{1,0:T(8,128)(2,1)S(1)} %copy-done.1, f32[8,8,128]{2,1,0:T(8,128)S(1)} %pad_bitcast_fusion.refs_2_, bf16[512,128]{1,0:T(8,128)(2,1)S(1)} %collective-permute-done.14.refs_3_, ...), custom_call_target="tpu_custom_call", output_to_operand_aliasing={{}: (5, {})} | custom-call | flops 1073741824 | bytes 4194304 | tf_op jit(solution)/shard_map/attend/pallas_call | solution.py:139
  86.2 1.6 %collective-permute-start.16 = (f32[1024,128]{1,0:T(8,128)S(1)}, f32[1024,128]{1,0:T(8,128)S(1)}, u32[]{:S(2)}, u32[]{:S(2)}) collective-permute-start(f32[1024,128]{1,0:T(8,128)S(1)} %get-tuple-element.27), channel_id=1, source_target_pairs={{0,1},{1,0},{2,3},{3,2},{4,5},{5,4},{6,7},{7,6},{8,9},{9,8},{10,11... | collective-permute-start | bytes 1572872 | tf_op jit(solution)/shard_map/ppermute | solution.py:263
  87.8 1.5 %collective-permute-done.16.other_ref = f32[1024,128]{1,0:T(8,128)S(1)} collective-permute-done((f32[1024,128]{1,0:T(8,128)S(1)}, f32[1024,128]{1,0:T(8,128)S(1)}, u32[]{:S(2)}, u32[]{:S(2)}) %collective-permute-start.16) | collective-permute-done | bytes 524320 | tf_op jit(solution)/shard_map/ppermute | solution.py:263
  90.1 2.1 %finish.1 = bf16[4,128,128]{2,1,0:T(8,128)(2,1)} custom-call(f32[1024,128]{1,0:T(8,128)} %get-tuple-element.28.mine_ref, f32[1024,128]{1,0:T(8,128)} %copy-done.7), custom_call_target="tpu_custom_call" | custom-call | tf_op jit(solution)/shard_map/finish/pallas_call | solution.py:166
  93.1 4.0 %collective-permute-start.17 = (bf16[128,128]{1,0:T(8,128)(2,1)S(1)}, bf16[128,128]{1,0:T(8,128)(2,1)S(1)}, u32[]{:S(2)}, u32[]{:S(2)}) collective-permute-start(bf16[128,128]{1,0:T(8,128)(2,1)S(1)} %get-tuple-element.37), channel_id=1, source_target_pairs={{0,0},{128,1},{4,4},{132,5},{8,8},{136,9},{12,12},{140,13},{1,128}... | collective-permute-start | bytes 98312 | tf_op jit(solution)/shard_map/ppermute | solution.py:265
  97.0 1.7 %collective-permute-start.20 = (bf16[128,128]{1,0:T(8,128)(2,1)S(1)}, bf16[128,128]{1,0:T(8,128)(2,1)S(1)}, u32[]{:S(2)}, u32[]{:S(2)}) collective-permute-start(bf16[128,128]{1,0:T(8,128)(2,1)S(1)} %get-tuple-element.38), channel_id=1, source_target_pairs={{12,0},{140,1},{0,4},{128,5},{4,8},{132,9},{8,12},{136,13},{13,128... | collective-permute-start | bytes 98312 | tf_op jit(solution)/shard_map/ppermute | solution.py:265
  98.7 3.2 %collective-permute-start.19 = (bf16[128,128]{1,0:T(8,128)(2,1)S(1)}, bf16[128,128]{1,0:T(8,128)(2,1)S(1)}, u32[]{:S(2)}, u32[]{:S(2)}) collective-permute-start(bf16[128,128]{1,0:T(8,128)(2,1)S(1)} %get-tuple-element.39), channel_id=1, source_target_pairs={{8,0},{136,1},{12,4},{140,5},{0,8},{128,9},{4,12},{132,13},{9,128}... | collective-permute-start | bytes 98312 | tf_op jit(solution)/shard_map/ppermute | solution.py:265
  101.9 2.3 %collective-permute-start.18 = (bf16[128,128]{1,0:T(8,128)(2,1)S(1)}, bf16[128,128]{1,0:T(8,128)(2,1)S(1)}, u32[]{:S(2)}, u32[]{:S(2)}) collective-permute-start(bf16[128,128]{1,0:T(8,128)(2,1)S(1)} %get-tuple-element.40), channel_id=1, source_target_pairs={{4,0},{132,1},{8,4},{136,5},{12,8},{140,9},{0,12},{128,13},{5,128}... | collective-permute-start | bytes 98312 | tf_op jit(solution)/shard_map/ppermute | solution.py:265
  104.2 1.8 %collective-permute-done.19 = bf16[128,128]{1,0:T(8,128)(2,1)S(1)} collective-permute-done((bf16[128,128]{1,0:T(8,128)(2,1)S(1)}, bf16[128,128]{1,0:T(8,128)(2,1)S(1)}, u32[]{:S(2)}, u32[]{:S(2)}) %collective-permute-start.19) | collective-permute-done | bytes 32800 | tf_op jit(solution)/shard_map/ppermute | solution.py:265
  106.0 1.7 %collective-permute-done.18 = bf16[128,128]{1,0:T(8,128)(2,1)S(1)} collective-permute-done((bf16[128,128]{1,0:T(8,128)(2,1)S(1)}, bf16[128,128]{1,0:T(8,128)(2,1)S(1)}, u32[]{:S(2)}, u32[]{:S(2)}) %collective-permute-start.18) | collective-permute-done | bytes 32800 | tf_op jit(solution)/shard_map/ppermute | solution.py:265
  107.7 6.0 %all_gather.7.a_ref = bf16[16,128,128]{2,1,0:T(8,128)(2,1)S(1)} all-gather(bf16[4,128,128]{2,1,0:T(8,128)(2,1)S(1)} %pad_maximum_fusion.4), channel_id=1, replica_groups=mesh['xh'=2,'z'=8,'y'=4,'xl'=2,'core'=2] {'xl','core'}, dimensions={0}, use_global_device_ids=true | all-gather | bytes 655360 | tf_op jit(solution)/shard_map/all_gather | solution.py:266
  113.7 1.1 output.1
  (83 shorter events, 8.8 us)
Async XLA Ops:
  0.0 27.4 %copy-start = (s32[128]{0:T(128)S(1)}, s32[128]{0:T(128)}, u32[]{:S(2)}) copy-start(s32[128]{0:T(128)} %param.18) | copy-start | bytes 1540
  0.0 9.9 %copy-start.2 = (bf16[1024,256]{1,0:T(8,128)(2,1)S(1)}, bf16[1024,256]{1,0:T(8,128)(2,1)}, u32[]{:S(2)}) copy-start(bf16[1024,256]{1,0:T(8,128)(2,1)} %wq_ref.1) | copy-start | bytes 1572868
  9.9 0.7 copy-start.5
  9.9 0.7 copy-start.6
  10.6 1.0 copy-start.3
  11.7 1.0 copy-start.4
  15.8 10.5 %copy-start.8 = (bf16[256,1024]{1,0:T(8,128)(2,1)S(1)}, bf16[256,1024]{1,0:T(8,128)(2,1)}, u32[]{:S(2)}) copy-start(bf16[256,1024]{1,0:T(8,128)(2,1)} %param.15) | copy-start | bytes 1572868
  15.8 13.8 %collective-permute-start = (bf16[384,128]{1,0:T(8,128)(2,1)S(1)}, bf16[384,128]{1,0:T(8,128)(2,1)S(1)}, u32[]{:S(2)}, u32[]{:S(2)}) collective-permute-start(bf16[384,128]{1,0:T(8,128)(2,1)S(1)} %get-tuple-element.33), channel_id=1, source_target_pairs={{0,0},{1,128},{4,4},{5,132},{8,8},{9,136},{12,12},{13,140},{128,1}... | collective-permute-start | bytes 294920 | tf_op jit(solution)/shard_map/ppermute | solution.py:235
  19.3 12.1 %collective-permute-start.3 = (bf16[384,128]{1,0:T(8,128)(2,1)S(1)}, bf16[384,128]{1,0:T(8,128)(2,1)S(1)}, u32[]{:S(2)}, u32[]{:S(2)}) collective-permute-start(bf16[384,128]{1,0:T(8,128)(2,1)S(1)} %get-tuple-element.34), channel_id=1, source_target_pairs={{0,12},{1,140},{4,0},{5,128},{8,4},{9,132},{12,8},{13,136},{128,13... | collective-permute-start | bytes 294920 | tf_op jit(solution)/shard_map/ppermute | solution.py:235
  22.6 8.9 %collective-permute-start.2 = (bf16[384,128]{1,0:T(8,128)(2,1)S(1)}, bf16[384,128]{1,0:T(8,128)(2,1)S(1)}, u32[]{:S(2)}, u32[]{:S(2)}) collective-permute-start(bf16[384,128]{1,0:T(8,128)(2,1)S(1)} %get-tuple-element.35), channel_id=1, source_target_pairs={{0,8},{1,136},{4,12},{5,140},{8,0},{9,128},{12,4},{13,132},{128,9}... | collective-permute-start | bytes 294920 | tf_op jit(solution)/shard_map/ppermute | solution.py:235
  25.2 7.7 %collective-permute-start.1 = (bf16[384,128]{1,0:T(8,128)(2,1)S(1)}, bf16[384,128]{1,0:T(8,128)(2,1)S(1)}, u32[]{:S(2)}, u32[]{:S(2)}) collective-permute-start(bf16[384,128]{1,0:T(8,128)(2,1)S(1)} %get-tuple-element.36), channel_id=1, source_target_pairs={{0,4},{1,132},{4,8},{5,136},{8,12},{9,140},{12,0},{13,128},{128,5}... | collective-permute-start | bytes 294920 | tf_op jit(solution)/shard_map/ppermute | solution.py:235
  26.5 35.4 %collective-permute-start.13 = (bf16[256,256]{1,0:T(8,128)(2,1)S(1)}, bf16[256,256]{1,0:T(8,128)(2,1)S(1)}, u32[]{:S(2)}, u32[]{:S(2)}) collective-permute-start(bf16[256,256]{1,0:T(8,128)(2,1)S(1)} %get-tuple-element.29), channel_id=1, source_target_pairs={{0,3},{1,0},{2,1},{3,2},{4,7},{5,4},{6,5},{7,6},{8,11},{9,8},{10,9... | collective-permute-start | bytes 393224 | tf_op jit(solution)/shard_map/ppermute | solution.py:209
  28.1 0.8 copy-start.11
  29.7 8.9 %collective-permute-start.11 = (bf16[256,256]{1,0:T(8,128)(2,1)S(1)}, bf16[256,256]{1,0:T(8,128)(2,1)S(1)}, u32[]{:S(2)}, u32[]{:S(2)}) collective-permute-start(bf16[256,256]{1,0:T(8,128)(2,1)S(1)} %get-tuple-element.30), channel_id=1, source_target_pairs={{0,1},{1,2},{2,3},{3,0},{4,5},{5,6},{6,7},{7,4},{8,9},{9,10},{10,1... | collective-permute-start | bytes 393224 | tf_op jit(solution)/shard_map/ppermute | solution.py:209
  32.9 6.1 %copy-start.9 = (bf16[4,128,128]{2,1,0:T(8,128)(2,1)}, bf16[4,128,128]{2,1,0:T(8,128)(2,1)S(1)}, u32[]{:S(2)}) copy-start(bf16[4,128,128]{2,1,0:T(8,128)(2,1)S(1)} %pad_maximum_fusion.3.mine_ref) | copy-start | bytes 393220
  32.9 15.0 %collective-permute-start.6 = (bf16[1024,128]{1,0:T(8,128)(2,1)S(1)}, bf16[1024,128]{1,0:T(8,128)(2,1)S(1)}, u32[]{:S(2)}, u32[]{:S(2)}) collective-permute-start(bf16[1024,128]{1,0:T(8,128)(2,1)S(1)} %bitcast.42), channel_id=1, source_target_pairs={{0,112},{16,0},{32,16},{48,32},{64,48},{80,64},{96,80},{112,96},{1... | collective-permute-start | bytes 786440 | tf_op jit(solution)/shard_map/ppermute | solution.py:246
  38.5 9.4 %collective-permute-start.5 = (bf16[1024,128]{1,0:T(8,128)(2,1)S(1)}, bf16[1024,128]{1,0:T(8,128)(2,1)S(1)}, u32[]{:S(2)}, u32[]{:S(2)}) collective-permute-start(bf16[1024,128]{1,0:T(8,128)(2,1)S(1)} %bitcast.43), channel_id=1, source_target_pairs={{0,16},{16,32},{32,48},{48,64},{64,80},{80,96},{96,112},{112,0},{1... | collective-permute-start | bytes 786440 | tf_op jit(solution)/shard_map/ppermute | solution.py:245
  38.5 1.3 %collective-permute-start.4 = (bf16[4,128,128]{2,1,0:T(8,128)(2,1)S(1)}, bf16[4,128,128]{2,1,0:T(8,128)(2,1)S(1)}, u32[]{:S(2)}, u32[]{:S(2)}) collective-permute-start(bf16[4,128,128]{2,1,0:T(8,128)(2,1)S(1)} %pad_maximum_fusion.3.mine_ref), channel_id=1, source_target_pairs={{0,1},{1,0},{2,3},{3,2},{4,5},{5,4},{6,7},{7,6},{8,9},{9,8},{10,11... | collective-permute-start | bytes 393224 | tf_op jit(solution)/shard_map/ppermute | solution.py:244
  38.6 12.3 %collective-permute-start.12 = (bf16[256,256]{1,0:T(8,128)(2,1)S(1)}, bf16[256,256]{1,0:T(8,128)(2,1)S(1)}, u32[]{:S(2)}, u32[]{:S(2)}) collective-permute-start(bf16[256,256]{1,0:T(8,128)(2,1)S(1)} %get-tuple-element.32), channel_id=1, source_target_pairs={{0,2},{1,3},{2,0},{3,1},{4,6},{5,7},{6,4},{7,5},{8,10},{9,11},{10,... | collective-permute-start | bytes 393224 | tf_op jit(solution)/shard_map/ppermute | solution.py:209
  42.4 1.0 copy-start.1
  47.9 11.2 %collective-permute-start.7 = (bf16[1024,128]{1,0:T(8,128)(2,1)S(1)}, bf16[1024,128]{1,0:T(8,128)(2,1)S(1)}, u32[]{:S(2)}, u32[]{:S(2)}) collective-permute-start(bf16[1024,128]{1,0:T(8,128)(2,1)S(1)} %collective-permute-done.5.refs_3_), channel_id=1, source_target_pairs={{0,16},{16,32},{32,48},{48,64},{64,80},{80,96},{96,112},{112,0},{1... | collective-permute-start | bytes 786440 | tf_op jit(solution)/shard_map/ppermute | solution.py:254
  48.0 11.1 %collective-permute-start.8 = (bf16[1024,128]{1,0:T(8,128)(2,1)S(1)}, bf16[1024,128]{1,0:T(8,128)(2,1)S(1)}, u32[]{:S(2)}, u32[]{:S(2)}) collective-permute-start(bf16[1024,128]{1,0:T(8,128)(2,1)S(1)} %collective-permute-done.6.refs_4_), channel_id=1, source_target_pairs={{0,112},{16,0},{32,16},{48,32},{64,48},{80,64},{96,80},{112,96},{1... | collective-permute-start | bytes 786440 | tf_op jit(solution)/shard_map/ppermute | solution.py:255
  59.2 11.0 %collective-permute-start.9 = (bf16[1024,128]{1,0:T(8,128)(2,1)S(1)}, bf16[1024,128]{1,0:T(8,128)(2,1)S(1)}, u32[]{:S(2)}, u32[]{:S(2)}) collective-permute-start(bf16[1024,128]{1,0:T(8,128)(2,1)S(1)} %collective-permute-done.7.refs_3_), channel_id=1, source_target_pairs={{0,16},{16,32},{32,48},{48,64},{64,80},{80,96},{96,112},{112,0},{1... | collective-permute-start | bytes 786440 | tf_op jit(solution)/shard_map/ppermute | solution.py:254
  59.3 10.9 %collective-permute-start.10 = (bf16[1024,128]{1,0:T(8,128)(2,1)S(1)}, bf16[1024,128]{1,0:T(8,128)(2,1)S(1)}, u32[]{:S(2)}, u32[]{:S(2)}) collective-permute-start(bf16[1024,128]{1,0:T(8,128)(2,1)S(1)} %collective-permute-done.8.refs_4_), channel_id=1, source_target_pairs={{0,112},{16,0},{32,16},{48,32},{64,48},{80,64},{96,80},{112,96},{1... | collective-permute-start | bytes 786440 | tf_op jit(solution)/shard_map/ppermute | solution.py:255
  70.2 10.9 %collective-permute-start.14 = (bf16[512,128]{1,0:T(8,128)(2,1)S(1)}, bf16[512,128]{1,0:T(8,128)(2,1)S(1)}, u32[]{:S(2)}, u32[]{:S(2)}) collective-permute-start(bf16[512,128]{1,0:T(8,128)(2,1)S(1)} %slice.48), channel_id=1, source_target_pairs={{0,16},{16,32},{32,48},{48,64},{64,80},{80,96},{96,112},{112,0},{1... | collective-permute-start | bytes 393224 | tf_op jit(solution)/shard_map/ppermute | solution.py:257
  70.3 10.9 %collective-permute-start.15 = (bf16[512,128]{1,0:T(8,128)(2,1)S(1)}, bf16[512,128]{1,0:T(8,128)(2,1)S(1)}, u32[]{:S(2)}, u32[]{:S(2)}) collective-permute-start(bf16[512,128]{1,0:T(8,128)(2,1)S(1)} %slice.49), channel_id=1, source_target_pairs={{0,112},{16,0},{32,16},{48,32},{64,48},{80,64},{96,80},{112,96},{1... | collective-permute-start | bytes 393224 | tf_op jit(solution)/shard_map/ppermute | solution.py:258
  86.2 3.1 %collective-permute-start.16 = (f32[1024,128]{1,0:T(8,128)S(1)}, f32[1024,128]{1,0:T(8,128)S(1)}, u32[]{:S(2)}, u32[]{:S(2)}) collective-permute-start(f32[1024,128]{1,0:T(8,128)S(1)} %get-tuple-element.27), channel_id=1, source_target_pairs={{0,1},{1,0},{2,3},{3,2},{4,5},{5,4},{6,7},{7,6},{8,9},{9,8},{10,11... | collective-permute-start | bytes 1572872 | tf_op jit(solution)/shard_map/ppermute | solution.py:263
  89.3 0.8 copy-start.7
  93.1 11.1 %collective-permute-start.17 = (bf16[128,128]{1,0:T(8,128)(2,1)S(1)}, bf16[128,128]{1,0:T(8,128)(2,1)S(1)}, u32[]{:S(2)}, u32[]{:S(2)}) collective-permute-start(bf16[128,128]{1,0:T(8,128)(2,1)S(1)} %get-tuple-element.37), channel_id=1, source_target_pairs={{0,0},{128,1},{4,4},{132,5},{8,8},{136,9},{12,12},{140,13},{1,128}... | collective-permute-start | bytes 98312 | tf_op jit(solution)/shard_map/ppermute | solution.py:265
  97.0 7.1 %collective-permute-start.20 = (bf16[128,128]{1,0:T(8,128)(2,1)S(1)}, bf16[128,128]{1,0:T(8,128)(2,1)S(1)}, u32[]{:S(2)}, u32[]{:S(2)}) collective-permute-start(bf16[128,128]{1,0:T(8,128)(2,1)S(1)} %get-tuple-element.38), channel_id=1, source_target_pairs={{12,0},{140,1},{0,4},{128,5},{4,8},{132,9},{8,12},{136,13},{13,128... | collective-permute-start | bytes 98312 | tf_op jit(solution)/shard_map/ppermute | solution.py:265
  98.7 7.2 %collective-permute-start.19 = (bf16[128,128]{1,0:T(8,128)(2,1)S(1)}, bf16[128,128]{1,0:T(8,128)(2,1)S(1)}, u32[]{:S(2)}, u32[]{:S(2)}) collective-permute-start(bf16[128,128]{1,0:T(8,128)(2,1)S(1)} %get-tuple-element.39), channel_id=1, source_target_pairs={{8,0},{136,1},{12,4},{140,5},{0,8},{128,9},{4,12},{132,13},{9,128}... | collective-permute-start | bytes 98312 | tf_op jit(solution)/shard_map/ppermute | solution.py:265
  101.9 5.7 %collective-permute-start.18 = (bf16[128,128]{1,0:T(8,128)(2,1)S(1)}, bf16[128,128]{1,0:T(8,128)(2,1)S(1)}, u32[]{:S(2)}, u32[]{:S(2)}) collective-permute-start(bf16[128,128]{1,0:T(8,128)(2,1)S(1)} %get-tuple-element.40), channel_id=1, source_target_pairs={{4,0},{132,1},{8,4},{136,5},{12,8},{140,9},{0,12},{128,13},{5,128}... | collective-permute-start | bytes 98312 | tf_op jit(solution)/shard_map/ppermute | solution.py:265
  (2 other events, 1.3 us)

commit v2 on v0

v2 whole, which is shorter than its diff:
```python
import jax
import jax.numpy as jnp
from jax import lax
from jax.experimental import pallas as pl
from jax.experimental.pallas import tpu as pltpu
from jax.sharding import Mesh, PartitionSpec as P

CTX = ("xh", "z", "y")
HEAD = ("xl", "core")
NXH, NZ, NY, NXL, NCORE = 2, 8, 4, 2, 2
BLOCK = 128
HD = 64
ROWS = 256
EPS = 1e-06
LOG2E = 1.4426950408889634
DEAD = -30000.0
F32 = jnp.float32
BF16 = jnp.bfloat16
VMEM = pl.BlockSpec(memory_space=pltpu.VMEM)
SMEM = pl.BlockSpec(memory_space=pltpu.SMEM)
HBM = pl.BlockSpec(memory_space=pltpu.HBM)
PARAMS = pltpu.CompilerParams(vmem_limit_bytes=32 << 20)


def ring(length, by):
    return [(i, (i + by) % length) for i in range(length)]


def project_kernel(
    temper_ref, x_ref, gain_hbm, wq_hbm, wk_hbm, wv_hbm, *refs
):
    out_refs, (stage_ref, gain_ref, wq_ref, wk_ref, wv_ref, sems) = refs[:NY], refs[NY:]
    pairs = ((gain_hbm, gain_ref), (wq_hbm, wq_ref), (wk_hbm, wk_ref), (wv_hbm, wv_ref))
    copies = [pltpu.make_async_copy(source, target, sems.at[n]) for n, (source, target) in enumerate(pairs)]
    for copy in copies:
        copy.start()
    x = x_ref[...].astype(F32)
    scaled = x * lax.rsqrt(jnp.mean(x * x, axis=-1, keepdims=True) + EPS)
    copies[0].wait()
    normed = (scaled * gain_ref[...]).astype(BF16)
    copies[1].wait()
    query = jnp.dot(normed, wq_ref[...], preferred_element_type=F32)
    copies[2].wait()
    keys = jnp.dot(normed, wk_ref[...], preferred_element_type=F32)
    copies[3].wait()
    values = jnp.dot(normed, wv_ref[...], preferred_element_type=F32)

    def unit(part):
        return part * lax.rsqrt(jnp.mean(part * part, axis=-1, keepdims=True) + EPS)

    for j in range(4):
        cols = slice(HD * j, HD * (j + 1))
        q = unit(query[:, cols]) * (temper_ref[j] * (LOG2E / HD))
        k = unit(keys[:, cols])
        v = values[:, cols]
        stage_ref[j, :ROWS, :] = jnp.concatenate([k, v], axis=1).astype(BF16)
        stage_ref[j, ROWS:, :] = jnp.concatenate([q[:BLOCK], q[BLOCK:]], axis=1).astype(BF16)
    y = lax.axis_index("y").astype(jnp.int32)
    for s in range(NY):
        out_refs[s][...] = stage_ref[lax.rem(y + s, NY)]


def project(whole, gain, w_query, w_key, w_value, temper):
    hold = lambda x: pltpu.with_memory_space_constraint(x, pltpu.HBM)
    return pl.pallas_call(
        project_kernel,
        out_shape=[jax.ShapeDtypeStruct((ROWS + BLOCK, 128), BF16)] * NY,
        in_specs=[SMEM, VMEM, HBM, HBM, HBM, HBM],
        out_specs=[VMEM] * NY,
        scratch_shapes=[
            pltpu.VMEM((NY, ROWS + BLOCK, 128), BF16),
            pltpu.VMEM((1, 1024), F32),
            pltpu.VMEM((1024, 256), BF16),
            pltpu.VMEM((1024, 256), BF16),
            pltpu.VMEM((1024, 256), BF16),
            pltpu.SemaphoreType.DMA((4,)),
        ],
        compiler_params=PARAMS,
        name="project",
    )(temper, whole, hold(gain), hold(w_query), hold(w_key), hold(w_value))


QT = 256
NQ = 1024
NK = 1024


def widen(packed_ref, first, out_ref):
    lane = lax.broadcasted_iota(jnp.int32, (BLOCK, 128), 1)
    for m in range(NY):
        pair = packed_ref[m].astype(F32)
        for b in range(2):
            part = pair if b == 0 else pltpu.roll(pair, 64, 1)
            flag = jnp.where(lane == HD + first + 2 * m + b, 1.0, 0.0)
            at = (2 * m + b) * BLOCK
            out_ref[at : at + BLOCK, :] = jnp.where(lane < HD, part, flag).astype(BF16)


def bias_rows(order_ref, adjacency_ref, keys_ref, queries_ref, bias_ref):
    z, y, xh = (lax.axis_index(a).astype(jnp.int32) for a in ("z", "y", "xh"))
    lane = lax.broadcasted_iota(jnp.int32, (1, 128), 1)

    def pick(side, zs, s, b):
        block = 2 * ((side * NZ + zs) * NY + lax.rem(y - s + NY, NY)) + b
        return jnp.where(lane == order_ref[block], 1.0, 0.0)

    queries_ref[...] = jnp.zeros_like(queries_ref)
    for s in range(NY):
        for b in range(2):
            n = 2 * s + b
            queries_ref[HD + n : HD + n + 1, :] = pick(xh, z, s, b)
            queries_ref[HD + 8 + n : HD + 9 + n, :] = pick(1 - xh, z, s, b)
            for zs in range(NZ):
                keys_ref[8 * zs + n : 8 * zs + n + 1, :] = pick(xh, zs, s, b)
    turned = (((1,), (1,)), ((), ()))
    adjacency = adjacency_ref[...].astype(F32).astype(BF16)
    keys, queries = keys_ref[...].astype(BF16), queries_ref[...].astype(BF16)
    picked = lax.dot_general(keys, adjacency, turned, preferred_element_type=F32).astype(BF16)
    live = lax.dot_general(picked, queries, turned, preferred_element_type=F32)
    bias_ref[...] = jnp.where(live > 0.5, 0.0, DEAD).reshape(NZ, NK // BLOCK, 128)


def chunk_at(distance):
    return lax.rem(lax.axis_index("z").astype(jnp.int32) + (distance + NZ), NZ)


def split_kv(kv, distance, bias_ref):
    lane = lax.broadcasted_iota(jnp.int32, (NK, 128), 1)
    kv = kv.astype(F32)
    table = bias_ref[chunk_at(distance)]
    bias = jnp.concatenate(
        [jnp.broadcast_to(table[b : b + 1, :], (BLOCK, 128)) for b in range(NK // BLOCK)], axis=0
    )
    return jnp.where(lane < HD, kv, bias).astype(BF16), jnp.where(lane < HD, 1.0, kv).astype(BF16)


def tile(q_ref, kx, vx, store):
    for t in range(NQ // QT):
        rows = slice(t * QT, (t + 1) * QT)
        scores = lax.dot_general(q_ref[rows, :], kx, (((1,), (1,)), ((), ())), preferred_element_type=F32)
        probs = jnp.exp2(scores).astype(BF16)
        store(rows, jnp.dot(probs, vx, preferred_element_type=F32))


def put(ref):
    def store(rows, part):
        ref[rows, :] = part

    return store


def add(ref):
    def store(rows, part):
        ref[rows, :] += part

    return store


def cost(keys):
    return pl.CostEstimate(flops=512 * NQ * keys, transcendentals=NQ * keys, bytes_accessed=4 << 20)


ACC = jax.ShapeDtypeStruct((NQ, 128), F32)
WIDE = jax.ShapeDtypeStruct((NQ, 128), BF16)


def first_kernel(order_ref, adjacency_ref, mine_ref, kv_ref, q_ref, bias_ref, acc_ref, keys_ref, queries_ref):
    bias_rows(order_ref, adjacency_ref, keys_ref, queries_ref, bias_ref)
    widen(mine_ref, 0, q_ref)
    kx, vx = split_kv(kv_ref[...], 0, bias_ref)
    tile(q_ref, kx, vx, put(acc_ref))


def attend_first(order, adjacency, mine, kv):
    return pl.pallas_call(
        first_kernel,
        out_shape=(WIDE, jax.ShapeDtypeStruct((NZ, NK // BLOCK, 128), F32), ACC),
        in_specs=[SMEM, VMEM, VMEM, VMEM],
        out_specs=(VMEM, VMEM, VMEM),
        scratch_shapes=[pltpu.VMEM((64, 128), F32), pltpu.VMEM((128, 128), F32)],
        compiler_params=PARAMS,
        cost_estimate=cost(NK),
        name="attend_first",
    )(order, adjacency, mine, kv)


def both_tiles(step, bias_ref, low_ref, high_ref, kx_ref, vx_ref, pairs):
    kx_ref[0], vx_ref[0] = split_kv(low_ref[...], -step, bias_ref)
    kx_ref[1], vx_ref[1] = split_kv(high_ref[...], step, bias_ref)

    def body(n, carry):
        kx, vx = kx_ref[n], vx_ref[n]
        for q_ref, acc_ref in pairs:
            tile(q_ref, kx, vx, add(acc_ref))
        return carry

    lax.fori_loop(0, 2, body, 0)


SPLIT = [pltpu.VMEM((2, NK, 128), BF16), pltpu.VMEM((2, NK, 128), BF16)]


def second_kernel(
    q_ref, other_ref, bias_ref, kv_ref, low_ref, high_ref, acc_in, q2_ref, acc_ref, acc2_ref, kx_ref, vx_ref
):
    widen(other_ref, 8, q2_ref)
    kx, vx = split_kv(kv_ref[...], 0, bias_ref)
    tile(q2_ref, kx, vx, put(acc2_ref))
    both_tiles(1, bias_ref, low_ref, high_ref, kx_ref, vx_ref, ((q_ref, acc_ref), (q2_ref, acc2_ref)))


def attend_second(q, other, bias, kv, low, high, acc):
    return pl.pallas_call(
        second_kernel,
        out_shape=(WIDE, ACC, ACC),
        in_specs=[VMEM] * 7,
        out_specs=(VMEM, VMEM, VMEM),
        scratch_shapes=SPLIT,
        input_output_aliases={6: 1},
        compiler_params=PARAMS,
        cost_estimate=cost(5 * NK),
        name="attend_second",
    )(q, other, bias, kv, low, high, acc)


def middle_kernel(step, q_ref, q2_ref, bias_ref, low_ref, high_ref, in1, in2, acc_ref, acc2_ref, kx_ref, vx_ref):
    both_tiles(step, bias_ref, low_ref, high_ref, kx_ref, vx_ref, ((q_ref, acc_ref), (q2_ref, acc2_ref)))


def attend_middle(step, q, q2, bias, low, high, acc, acc2):
    return pl.pallas_call(
        lambda *refs: middle_kernel(step, *refs),
        out_shape=(ACC, ACC),
        in_specs=[VMEM] * 7,
        out_specs=(VMEM, VMEM),
        scratch_shapes=SPLIT,
        input_output_aliases={5: 0, 6: 1},
        compiler_params=PARAMS,
        cost_estimate=cost(4 * NK),
        name="attend_middle",
    )(q, q2, bias, low, high, acc, acc2)


HALF = NQ // 2
SUMS = 16


def split_last(low_ref, high_ref, bias_ref):
    return split_kv(jnp.concatenate([low_ref[...], high_ref[...]], axis=0), NZ // 2, bias_ref)


def last_other_kernel(q_ref, bias_ref, low_ref, high_ref, in_ref, message_ref, acc_ref):
    def store(rows, part):
        acc_ref[rows, :] = in_ref[rows, :] + part

    tile(q_ref, *split_last(low_ref, high_ref, bias_ref), store)
    lane = lax.broadcasted_iota(jnp.int32, (BLOCK, 128), 1)
    row = lax.broadcasted_iota(jnp.int32, (SUMS, 128), 0)
    column = lax.broadcasted_iota(jnp.int32, (SUMS, 128), 1)
    sums = jnp.zeros((SUMS, BLOCK), F32)
    blocks = [acc_ref[n * BLOCK : (n + 1) * BLOCK, :] for n in range(8)]
    for m in range(NY):
        pair = jnp.where(lane < HD, pltpu.roll(blocks[2 * m], 64, 1), blocks[2 * m + 1])
        message_ref[m * BLOCK : (m + 1) * BLOCK, :] = pair.astype(BF16)
    for n in range(8):
        coarse = blocks[n].astype(BF16).astype(F32)
        spread = jnp.where(lane == 0, coarse, jnp.where(lane == 1, blocks[n] - coarse, 0.0)).astype(BF16)
        at = jnp.where((row // 2 == n) & (row % 2 == column), 1.0, 0.0).astype(BF16)
        sums += lax.dot_general(at, spread, (((1,), (1,)), ((), ())), preferred_element_type=F32)
    message_ref[HALF:, :] = sums.astype(BF16)


def attend_last_other(q2, bias, low, high, acc2):
    return pl.pallas_call(
        last_other_kernel,
        out_shape=jax.ShapeDtypeStruct((HALF + SUMS, 128), BF16),
        in_specs=[VMEM] * 5,
        out_specs=VMEM,
        scratch_shapes=[pltpu.VMEM((NQ, 128), F32)],
        compiler_params=PARAMS,
        cost_estimate=cost(NK),
        name="attend_last_other",
    )(q2, bias, low, high, acc2)


def last_mine_kernel(q_ref, bias_ref, low_ref, high_ref, in_ref, acc_ref):
    tile(q_ref, *split_last(low_ref, high_ref, bias_ref), add(acc_ref))


def attend_last_mine(q, bias, low, high, acc):
    return pl.pallas_call(
        last_mine_kernel,
        out_shape=ACC,
        in_specs=[VMEM] * 5,
        out_specs=VMEM,
        input_output_aliases={4: 0},
        compiler_params=PARAMS,
        cost_estimate=cost(NK),
        name="attend_last_mine",
    )(q, bias, low, high, acc)


def finish_kernel(mine_ref, message_ref, *out_refs):
    lane = lax.broadcasted_iota(jnp.int32, (BLOCK, 128), 1)
    row = lax.broadcasted_iota(jnp.int32, (SUMS, 128), 0)
    sums = message_ref[HALF:, :]
    blocks = [mine_ref[n * BLOCK : (n + 1) * BLOCK, :] for n in range(8)]
    spread = []
    for n in range(8):
        at = jnp.where(row // 2 == n, 1.0, 0.0).astype(BF16)
        spread.append(lax.dot_general(sums, at, (((0,), (0,)), ((), ())), preferred_element_type=F32))
    for m in range(NY):
        one, two = blocks[2 * m], blocks[2 * m + 1]
        total = jnp.where(lane < HD, pltpu.roll(one, 64, 1), two)
        total += message_ref[m * BLOCK : (m + 1) * BLOCK, :].astype(F32)
        weight = jnp.where(lane < HD, one + spread[2 * m], pltpu.roll(two, 64, 1) + spread[2 * m + 1])
        out_refs[m][...] = (total / weight).astype(BF16)


def finish(mine, message):
    return pl.pallas_call(
        finish_kernel,
        out_shape=[jax.ShapeDtypeStruct((BLOCK, 128), BF16)] * NY,
        in_specs=[VMEM, VMEM],
        out_specs=[VMEM] * NY,
        compiler_params=PARAMS,
        name="finish",
    )(mine, message)


def output_kernel(a_ref, w_ref, out_ref):
    y = lax.axis_index("y").astype(jnp.int32)
    lane = lax.broadcasted_iota(jnp.int32, (BLOCK, 128), 1)
    lefts, rights, weights = [], [], []
    for source in range(4):
        for s in range(4):
            pair = a_ref[4 * source + s].astype(F32)
            lefts.append(jnp.where(lane < HD, pair, 0.0).astype(BF16))
            rights.append(jnp.where(lane < HD, 0.0, pair).astype(BF16))
            j = lax.rem(y + s, NY)
            row = pl.multiple_of(source * 256 + j * HD, HD)
            w = w_ref[pl.ds(row, HD), :]
            weights += [w, w]
    w = jnp.concatenate(weights, axis=0)
    out_ref[:BLOCK, :] = jnp.dot(jnp.concatenate(lefts, axis=1), w, preferred_element_type=F32).astype(BF16)
    out_ref[BLOCK:, :] = jnp.dot(jnp.concatenate(rights, axis=1), w, preferred_element_type=F32).astype(BF16)


def output(attended, w):
    return pl.pallas_call(
        output_kernel,
        out_shape=jax.ShapeDtypeStruct((ROWS, 256), BF16),
        in_specs=[VMEM, VMEM],
        out_specs=VMEM,
        compiler_params=PARAMS,
        name="output",
    )(attended, w)


def shards(tokens, gain, w_query, w_key, w_value, w_out, temper, adjacency, order):
    whole = lax.all_gather(tokens, HEAD, axis=1, tiled=True)
    messages = project(whole, gain[None, :], w_query, w_key, w_value, temper)
    got = jnp.stack([messages[0]] + [lax.ppermute(messages[s], "y", ring(NY, s)) for s in range(1, NY)])
    kv = got[:, :ROWS, :].reshape(NK, 128)
    query = got[:, ROWS:, :]
    query, kv = lax.optimization_barrier((query, kv))
    low, high = lax.ppermute(kv, "z", ring(NZ, 1)), lax.ppermute(kv, "z", ring(NZ, -1))
    other = lax.ppermute(query, "xh", [(0, 1), (1, 0)])
    q, bias, acc = attend_first(order, adjacency, query, kv)
    w_late, _ = lax.optimization_barrier((w_out, kv))
    w_whole = lax.all_gather(w_late, HEAD, axis=0, tiled=True)
    for step in (1, 2, 3):
        low, high, acc = lax.optimization_barrier((low, high, acc))
        if step < 3:
            next_low, next_high = lax.ppermute(low, "z", ring(NZ, 1)), lax.ppermute(high, "z", ring(NZ, -1))
        else:
            next_low = lax.ppermute(low[: NK // 2], "z", ring(NZ, 1))
            next_high = lax.ppermute(high[NK // 2 :], "z", ring(NZ, -1))
        if step == 1:
            q2, acc, acc2 = attend_second(q, other, bias, kv, low, high, acc)
        else:
            acc, acc2 = attend_middle(step, q, q2, bias, low, high, acc, acc2)
        low, high = next_low, next_high
    low, high, acc, w_whole = lax.optimization_barrier((low, high, acc, w_whole))
    w_columns = lax.dynamic_slice_in_dim(w_whole, lax.axis_index(HEAD) * 256, 256, 1)
    message = attend_last_other(q2, bias, low, high, acc2)
    message, acc = lax.optimization_barrier((message, acc))
    message = lax.ppermute(message, "xh", [(0, 1), (1, 0)])
    attended = finish(attend_last_mine(q, bias, low, high, acc), message)
    back = jnp.stack([attended[0]] + [lax.ppermute(attended[s], "y", ring(NY, -s)) for s in range(1, NY)])
    gathered = lax.all_gather(back, HEAD, axis=0, tiled=True)
    return output(gathered, w_columns)


def solution(mesh):
    fine = Mesh(mesh.devices.reshape(NXH, NZ, NY, NXL, NCORE), CTX + HEAD)
    in_specs = (
        P(CTX, HEAD),
        P(),
        P(None, HEAD),
        P(None, HEAD),
        P(None, HEAD),
        P(HEAD, None),
        P(HEAD),
        P(),
        P(),
    )
    return jax.shard_map(shards, mesh=fine, in_specs=in_specs, out_specs=P(CTX, HEAD), check_vma=False)
```

time: 904 us -> 98.9 us (0.11)
  waiting for transfers between devices: 649 us -> 8.94 us
  local copies, waits for them, and re-layouts: 82.8 us -> 1.76 us
  other arithmetic: 53.9 us -> 0.05 us
  loops' own time: 45.3 us -> 0 us
  matrix products: 40.7 us -> 0 us
  Pallas kernels: 0 us -> 25.8 us
  starting transfers between devices: 5.45 us -> 25.6 us
  blocking collectives: 9.72 us -> 23 us
    ppermute x63 -> x16, waiting for transfers between devices: 570 us -> 8.9 us  [the longest x3 3.91 us: shards(): lax.ppermute(messages[s], 'y', ring(NY, s))]
    reduce_scatter x1 -> x0, waiting for transfers between devices: 79.4 us -> none  [shards(): lax.psum_scatter(partial_value.astype(jnp.bfloat16), 'head', scatter_dime...]
    gather x67 -> x0, local copies, waits for them, and re-layouts: 64.2 us -> none  [the longest x64 62 us: attend(): allowed = (jnp.take(query_live, key_block, axis=1) > 0) & True]
    reduce_or x64 -> x0, other arithmetic: 50.5 us -> none  [attend(): return lax.cond(jnp.any(allowed), compute, keep, carry)]
    another operation x65 -> x0, loops' own time: 45.3 us -> none  [the longest x1 44.3 us: shards(): moved, state = lax.fori_loop(0, cycle - 1, turn, (stacked, state))]
    dot_general x124 -> x0, matrix products: 40.7 us -> none  [the longest x60 25.2 us: compute(): jnp.einsum('qhd,khd->hqk', query, keys_piece, preferred_element_type=jnp....]
    pallas_call x0 -> x9, Pallas kernels: none -> 25.8 us  [the longest x2 9.75 us: attend_middle(): pl.pallas_call(lambda *refs: middle_kernel(step, *refs), out_shape=(ACC,...]
    ppermute x63 -> x16, starting transfers between devices: 5.45 us -> 25.6 us  [the longest x2 5.34 us: shards(): lax.ppermute(high, 'z', ring(NZ, -1))]
  transfers between devices with their start and end apart: 64 -> 17, of which waited for: 64 -> 7; matrix products, arithmetic and copies ran while one was open for 14% -> 1% of each run, Pallas kernels for 0% -> 20%
where the time goes in v2:
time: 98.9 us; the launch traced here: 98.7 us
  Pallas kernels  25.8 us (26%)
  starting transfers between devices  25.6 us (26%)
  blocking collectives  23 us (23%)
  between operations  13.6 us (14%)
  waiting for transfers between devices  8.94 us (9%)
  local copies, waits for them, and re-layouts  1.76 us (2%)
    all_gather x1, blocking collectives, shards(): gathered = lax.all_gather(back, HEAD, axis=0, tiled=True)  13.1 us
    all_gather x1, blocking collectives, shards(): whole = lax.all_gather(tokens, HEAD, axis=1, tiled=True)  9.92 us
    pallas_call x2, Pallas kernels, attend_middle(): pl.pallas_call(lambda *refs: middle_kernel(step, *refs), out_shape=(ACC,...  9.75 us
    pallas_call x1, Pallas kernels, attend_second(): pl.pallas_call(second_kernel, out_shape=(WIDE, ACC, ACC), in_specs=[VMEM]...  6.24 us
    ppermute x2, starting transfers between devices, shards(): lax.ppermute(high, 'z', ring(NZ, -1))  5.34 us
    ppermute x1, starting transfers between devices, shards(): lax.ppermute(kv, 'z', ring(NZ, -1))  4.03 us
    ppermute x3, starting transfers between devices, shards(): lax.ppermute(messages[s], 'y', ring(NY, s))  3.99 us
    ppermute x3, waiting for transfers between devices, shards(): lax.ppermute(messages[s], 'y', ring(NY, s))  3.91 us
  transfers between devices with their start and end apart: 17, of which 7 were waited for; matrix products, arithmetic and copies ran while one was open for 1% of the time, Pallas kernels for 20%

profile of v2, /device:TPU:1, one launch (start us, length us, event | category | flops | bytes accessed | tf_op | source)
XLA Modules:
  0.0 98.7 jit_solution(13977537042073071448)
XLA Ops:
  6.5 9.9 %all_gather.9.x_ref = bf16[256,1024]{1,0:T(8,128)(2,1)S(1)} all-gather(bf16[256,256]{1,0:T(8,128)(2,1)} %param.9), channel_id=1, replica_groups=mesh['xh'=2,'z'=8,'y'=4,'xl'=2,'core'=2] {'xl','core'}, dimensions={1}, use_global_device_ids=true | all-gather | bytes 655360 | tf_op jit(solution)/shard_map/all_gather | solution.py:361
  16.5 0.7 copy-done
  17.1 3.5 %project.1 = (bf16[384,128]{1,0:T(8,128)(2,1)S(1)}, bf16[384,128]{1,0:T(8,128)(2,1)S(1)}, bf16[384,128]{1,0:T(8,128)(2,1)S(1)}, bf16[384,128]{1,0:T(8,128)(2,1)S(1)}) custom-call(f32[4]{0:T(128)S(1)} %copy-done, bf16[256,1024]{1,0:T(8,128)(2,1)S(1)} %all_gather.9.x_ref, f32[1,1024]{1,0:T(1,128)} %bitcast.26, bf16[1024,256]{1,0:T(8,128)(2,1)} %wq_hbm.1, ...), custom_call_target="tpu_custom_call" | custom-call | tf_op jit(solution)/shard_map/project/pallas_call | solution.py:65
  20.7 0.3 collective-permute-start
  21.0 2.6 %collective-permute-start.1 = (bf16[384,128]{1,0:T(8,128)(2,1)S(1)}, bf16[384,128]{1,0:T(8,128)(2,1)S(1)}, u32[]{:S(2)}, u32[]{:S(2)}) collective-permute-start(bf16[384,128]{1,0:T(8,128)(2,1)S(1)} %get-tuple-element.43), channel_id=1, source_target_pairs={{0,8},{4,12},{8,0},{12,4},{1,9},{5,13},{9,1},{13,5},{2,10},{6,14},... | collective-permute-start | bytes 294920 | tf_op jit(solution)/shard_map/ppermute | solution.py:363
  23.6 1.1 %collective-permute-start.2 = (bf16[384,128]{1,0:T(8,128)(2,1)S(1)}, bf16[384,128]{1,0:T(8,128)(2,1)S(1)}, u32[]{:S(2)}, u32[]{:S(2)}) collective-permute-start(bf16[384,128]{1,0:T(8,128)(2,1)S(1)} %get-tuple-element.44), channel_id=1, source_target_pairs={{0,12},{4,0},{8,4},{12,8},{1,13},{5,1},{9,5},{13,9},{2,14},{6,2},{... | collective-permute-start | bytes 294920 | tf_op jit(solution)/shard_map/ppermute | solution.py:363
  24.6 1.5 %collective-permute-done = bf16[384,128]{1,0:T(8,128)(2,1)S(1)} collective-permute-done((bf16[384,128]{1,0:T(8,128)(2,1)S(1)}, bf16[384,128]{1,0:T(8,128)(2,1)S(1)}, u32[]{:S(2)}, u32[]{:S(2)}) %collective-permute-start) | collective-permute-done | bytes 98336 | tf_op jit(solution)/shard_map/ppermute | solution.py:363
  26.2 2.3 %collective-permute-done.1 = bf16[384,128]{1,0:T(8,128)(2,1)S(1)} collective-permute-done((bf16[384,128]{1,0:T(8,128)(2,1)S(1)}, bf16[384,128]{1,0:T(8,128)(2,1)S(1)}, u32[]{:S(2)}, u32[]{:S(2)}) %collective-permute-start.1) | collective-permute-done | bytes 98336 | tf_op jit(solution)/shard_map/ppermute | solution.py:363
  28.6 1.6 %collective-permute-start.3 = (bf16[1024,128]{1,0:T(8,128)(2,1)S(1)}, bf16[1024,128]{1,0:T(8,128)(2,1)S(1)}, u32[]{:S(2)}, u32[]{:S(2)}) collective-permute-start(bf16[1024,128]{1,0:T(8,128)(2,1)S(1)} %bitcast.12), channel_id=1, source_target_pairs={{0,16},{16,32},{32,48},{48,64},{64,80},{80,96},{96,112},{112,0},{1... | collective-permute-start | bytes 786440 | tf_op jit(solution)/shard_map/ppermute | solution.py:367
  30.2 4.0 %collective-permute-start.4 = (bf16[1024,128]{1,0:T(8,128)(2,1)S(1)}, bf16[1024,128]{1,0:T(8,128)(2,1)S(1)}, u32[]{:S(2)}, u32[]{:S(2)}) collective-permute-start(bf16[1024,128]{1,0:T(8,128)(2,1)S(1)} %bitcast.13), channel_id=1, source_target_pairs={{0,112},{16,0},{32,16},{48,32},{64,48},{80,64},{96,80},{112,96},{1... | collective-permute-start | bytes 786440 | tf_op jit(solution)/shard_map/ppermute | solution.py:367
  34.3 2.4 %collective-permute-start.7 = (bf16[4,128,128]{2,1,0:T(8,128)(2,1)S(1)}, bf16[4,128,128]{2,1,0:T(8,128)(2,1)S(1)}, u32[]{:S(2)}, u32[]{:S(2)}) collective-permute-start(bf16[4,128,128]{2,1,0:T(8,128)(2,1)S(1)} %pad_maximum_fusion.3.mine_ref), channel_id=1, source_target_pairs={{0,128},{128,0},{1,129},{129,1},{2,130},{130,2},{3,131},{131,3},{4... | collective-permute-start | bytes 393224 | tf_op jit(solution)/shard_map/ppermute | solution.py:368
  36.7 2.1 %attend_first.1 = (bf16[1024,128]{1,0:T(8,128)(2,1)S(1)}, f32[8,8,128]{2,1,0:T(8,128)S(1)}, f32[1024,128]{1,0:T(8,128)S(1)}) custom-call(s32[128]{0:T(128)S(1)} %copy-done.2, s32[128,128]{1,0:T(8,128)S(1)} %copy-done.1, bf16[4,128,128]{2,1,0:T(8,128)(2,1)S(1)} %pad_maximum_fusion.3.mine_ref, bf16[1024,128]{1,0:T(8,128)(2,1)S(1)} %bitcast.14), custom_call_target="tpu_custom_call" | custom-call | flops 536870912 | bytes 4194304 | tf_op jit(solution)/shard_map/attend_first/pallas_call | solution.py:175
  38.9 1.0 %collective-permute-done.3.low_ref = bf16[1024,128]{1,0:T(8,128)(2,1)S(1)} collective-permute-done((bf16[1024,128]{1,0:T(8,128)(2,1)S(1)}, bf16[1024,128]{1,0:T(8,128)(2,1)S(1)}, u32[]{:S(2)}, u32[]{:S(2)}) %collective-permute-start.3) | collective-permute-done | bytes 262176 | tf_op jit(solution)/shard_map/ppermute | solution.py:367
  39.9 2.7 %collective-permute-start.6 = (bf16[1024,128]{1,0:T(8,128)(2,1)S(1)}, bf16[1024,128]{1,0:T(8,128)(2,1)S(1)}, u32[]{:S(2)}, u32[]{:S(2)}) collective-permute-start(bf16[1024,128]{1,0:T(8,128)(2,1)S(1)} %collective-permute-done.4.high_ref), channel_id=1, source_target_pairs={{0,112},{16,0},{32,16},{48,32},{64,48},{80,64},{96,80},{112,96},{1... | collective-permute-start | bytes 786440 | tf_op jit(solution)/shard_map/ppermute | solution.py:375
  42.6 6.2 %attend_second.1 = (bf16[1024,128]{1,0:T(8,128)(2,1)S(1)}, f32[1024,128]{1,0:T(8,128)S(1)}, f32[1024,128]{1,0:T(8,128)S(1)}) custom-call(bf16[1024,128]{1,0:T(8,128)(2,1)S(1)} %get-tuple-element.47.q_ref.refs_0_, bf16[4,128,128]{2,1,0:T(8,128)(2,1)S(1)} %collective-permute-done.7.other_ref, ...), custom_call_target="tpu_custom_call", output_to_operand_aliasing={{1}: (6, {})} | custom-call | flops 2684354560 | bytes 4194304 | tf_op jit(solution)/shard_map/attend_second/pallas_call | solution.py:213
  48.9 2.7 %collective-permute-start.9 = (bf16[1024,128]{1,0:T(8,128)(2,1)S(1)}, bf16[1024,128]{1,0:T(8,128)(2,1)S(1)}, u32[]{:S(2)}, u32[]{:S(2)}) collective-permute-start(bf16[1024,128]{1,0:T(8,128)(2,1)S(1)} %collective-permute-done.6.refs_4_), channel_id=1, source_target_pairs={{0,112},{16,0},{32,16},{48,32},{64,48},{80,64},{96,80},{112,96},{1... | collective-permute-start | bytes 786440 | tf_op jit(solution)/shard_map/ppermute | solution.py:375
  51.6 4.9 %attend_middle.2 = (f32[1024,128]{1,0:T(8,128)S(1)}, f32[1024,128]{1,0:T(8,128)S(1)}) custom-call(bf16[1024,128]{1,0:T(8,128)(2,1)S(1)} %get-tuple-element.47.q_ref.refs_0_, bf16[1024,128]{1,0:T(8,128)(2,1)S(1)} %get-tuple-element.56.refs_1_.q_ref, ...), custom_call_target="tpu_custom_call", output_to_operand_aliasing={{0}: (5, {}), {1}: (6, {})} | custom-call | flops 2147483648 | bytes 4194304 | tf_op jit(solution)/shard_map/attend_middle/pallas_call | solution.py:231
  56.6 3.0 %collective-permute-start.11 = (bf16[512,128]{1,0:T(8,128)(2,1)S(1)}, bf16[512,128]{1,0:T(8,128)(2,1)S(1)}, u32[]{:S(2)}, u32[]{:S(2)}) collective-permute-start(bf16[512,128]{1,0:T(8,128)(2,1)S(1)} %slice.15), channel_id=1, source_target_pairs={{0,112},{16,0},{32,16},{48,32},{64,48},{80,64},{96,80},{112,96},{1... | collective-permute-start | bytes 393224 | tf_op jit(solution)/shard_map/ppermute | solution.py:378
  59.6 4.9 %attend_middle.3 = (f32[1024,128]{1,0:T(8,128)S(1)}, f32[1024,128]{1,0:T(8,128)S(1)}) custom-call(bf16[1024,128]{1,0:T(8,128)(2,1)S(1)} %get-tuple-element.47.q_ref.refs_0_, bf16[1024,128]{1,0:T(8,128)(2,1)S(1)} %get-tuple-element.56.refs_1_.q_ref, ...), custom_call_target="tpu_custom_call", output_to_operand_aliasing={{0}: (5, {}), {1}: (6, {})} | custom-call | flops 2147483648 | bytes 4194304 | tf_op jit(solution)/shard_map/attend_middle/pallas_call | solution.py:231
  64.5 1.5 %attend_last_other.1 = bf16[528,128]{1,0:T(8,128)(2,1)S(1)} custom-call(bf16[1024,128]{1,0:T(8,128)(2,1)S(1)} %get-tuple-element.56.refs_1_.q_ref, f32[8,8,128]{2,1,0:T(8,128)S(1)} %get-tuple-element.48.bias_ref.refs_2_, bf16[512,128]{1,0:T(8,128)(2,1)S(1)} %collective-permute-done.10.low_ref, bf16[512,128]{1,0:T(8,128)(2,1)S(1)} %collective-permute-done.11.high_ref, ...), custom_call_target="tpu_custom_call" | custom-call | flops 536870912 | bytes 4194304 | tf_op jit(solution)/shard_map/attend_last_other/pallas_call | solution.py:274
  66.1 2.5 %collective-permute-start.12 = (bf16[528,128]{1,0:T(8,128)(2,1)S(1)}, bf16[528,128]{1,0:T(8,128)(2,1)S(1)}, u32[]{:S(2)}, u32[]{:S(2)}) collective-permute-start(bf16[528,128]{1,0:T(8,128)(2,1)S(1)} %attend_last_other.1), channel_id=1, source_target_pairs={{0,128},{128,0},{1,129},{129,1},{2,130},{130,2},{3,131},{131,3},{4... | collective-permute-start | bytes 405512 | tf_op jit(solution)/shard_map/ppermute | solution.py:388
  68.5 1.3 %attend_last_mine.1.mine_ref = f32[1024,128]{1,0:T(8,128)S(1)} custom-call(bf16[1024,128]{1,0:T(8,128)(2,1)S(1)} %get-tuple-element.47.q_ref.refs_0_, f32[8,8,128]{2,1,0:T(8,128)S(1)} %get-tuple-element.48.bias_ref.refs_2_, bf16[512,128]{1,0:T(8,128)(2,1)S(1)} %collective-permute-done.10.low_ref, ...), custom_call_target="tpu_custom_call", output_to_operand_aliasing={{}: (4, {})} | custom-call | flops 536870912 | bytes 4194304 | tf_op jit(solution)/shard_map/attend_last_mine/pallas_call | solution.py:291
  69.8 1.6 %collective-permute-done.12.message_ref = bf16[528,128]{1,0:T(8,128)(2,1)S(1)} collective-permute-done((bf16[528,128]{1,0:T(8,128)(2,1)S(1)}, bf16[528,128]{1,0:T(8,128)(2,1)S(1)}, u32[]{:S(2)}, u32[]{:S(2)}) %collective-permute-start.12) | collective-permute-done | bytes 135200 | tf_op jit(solution)/shard_map/ppermute | solution.py:388
  71.4 0.3 finish.1
  71.7 1.3 %collective-permute-start.13 = (bf16[128,128]{1,0:T(8,128)(2,1)S(1)}, bf16[128,128]{1,0:T(8,128)(2,1)S(1)}, u32[]{:S(2)}, u32[]{:S(2)}) collective-permute-start(bf16[128,128]{1,0:T(8,128)(2,1)S(1)} %get-tuple-element.73), channel_id=1, source_target_pairs={{0,12},{4,0},{8,4},{12,8},{1,13},{5,1},{9,5},{13,9},{2,14},{6,2},{... | collective-permute-start | bytes 98312 | tf_op jit(solution)/shard_map/ppermute | solution.py:390
  73.0 0.5 collective-permute-start.14
  73.6 0.7 collective-permute-start.15
  74.3 1.1 %constant_dynamic-slice_fusion.w_ref = bf16[1024,256]{1,0:T(8,128)(2,1)S(1)} fusion(bf16[1024,1024]{1,0:T(8,128)(2,1)} %all-gather.2.cloned.1.call-done, s32[]{:T(128)S(6)} %select_n.3), kind=kLoop, calls=%fused_computation.5 | loop fusion | bytes 1048580 | tf_op jit(solution)/shard_map/dynamic_slice | solution.py:385
  75.4 1.9 %collective-permute-done.14 = bf16[128,128]{1,0:T(8,128)(2,1)S(1)} collective-permute-done((bf16[128,128]{1,0:T(8,128)(2,1)S(1)}, bf16[128,128]{1,0:T(8,128)(2,1)S(1)}, u32[]{:S(2)}, u32[]{:S(2)}) %collective-permute-start.14) | collective-permute-done | bytes 32800 | tf_op jit(solution)/shard_map/ppermute | solution.py:390
  77.3 0.3 collective-permute-done.15
  77.7 13.1 %all_gather.11.a_ref = bf16[16,128,128]{2,1,0:T(8,128)(2,1)S(1)} all-gather(bf16[4,128,128]{2,1,0:T(8,128)(2,1)S(1)} %pad_maximum_fusion.4), channel_id=1, replica_groups=mesh['xh'=2,'z'=8,'y'=4,'xl'=2,'core'=2] {'xl','core'}, dimensions={0}, use_global_device_ids=true | all-gather | bytes 655360 | tf_op jit(solution)/shard_map/all_gather | solution.py:391
  90.7 1.1 %output.1 = bf16[256,256]{1,0:T(8,128)(2,1)} custom-call(bf16[16,128,128]{2,1,0:T(8,128)(2,1)S(1)} %all_gather.11.a_ref, bf16[1024,256]{1,0:T(8,128)(2,1)S(1)} %constant_dynamic-slice_fusion.w_ref), custom_call_target="tpu_custom_call" | custom-call | tf_op jit(solution)/shard_map/output/pallas_call | solution.py:350
  (26 shorter events, 0.4 us)
Async XLA Ops:
  6.5 30.2 %copy-start.1 = (s32[128,128]{1,0:T(8,128)S(1)}, s32[128,128]{1,0:T(8,128)}, u32[]{:S(2)}) copy-start(s32[128,128]{1,0:T(8,128)} %adjacency_ref.1) | copy-start | bytes 196612
  6.5 30.2 %copy-start.2 = (s32[128]{0:T(128)S(1)}, s32[128]{0:T(128)}, u32[]{:S(2)}) copy-start(s32[128]{0:T(128)} %order_ref.1) | copy-start | bytes 1540
  6.5 58.0 %all-gather.2.cloned.1.call-start = ((), (), s32[]{:S(2)}) async-start(), calls=%async_computation | async-start | bytes 2621440 | tf_op jit(solution)/shard_map/all_gather | solution.py:371
  16.5 0.7 copy-start
  20.7 5.5 %collective-permute-start = (bf16[384,128]{1,0:T(8,128)(2,1)S(1)}, bf16[384,128]{1,0:T(8,128)(2,1)S(1)}, u32[]{:S(2)}, u32[]{:S(2)}) collective-permute-start(bf16[384,128]{1,0:T(8,128)(2,1)S(1)} %get-tuple-element.42), channel_id=1, source_target_pairs={{0,4},{4,8},{8,12},{12,0},{1,5},{5,9},{9,13},{13,1},{2,6},{6,10},{... | collective-permute-start | bytes 294920 | tf_op jit(solution)/shard_map/ppermute | solution.py:363
  21.0 7.5 %collective-permute-start.1 = (bf16[384,128]{1,0:T(8,128)(2,1)S(1)}, bf16[384,128]{1,0:T(8,128)(2,1)S(1)}, u32[]{:S(2)}, u32[]{:S(2)}) collective-permute-start(bf16[384,128]{1,0:T(8,128)(2,1)S(1)} %get-tuple-element.43), channel_id=1, source_target_pairs={{0,8},{4,12},{8,0},{12,4},{1,9},{5,13},{9,1},{13,5},{2,10},{6,14},... | collective-permute-start | bytes 294920 | tf_op jit(solution)/shard_map/ppermute | solution.py:363
  23.6 5.0 %collective-permute-start.2 = (bf16[384,128]{1,0:T(8,128)(2,1)S(1)}, bf16[384,128]{1,0:T(8,128)(2,1)S(1)}, u32[]{:S(2)}, u32[]{:S(2)}) collective-permute-start(bf16[384,128]{1,0:T(8,128)(2,1)S(1)} %get-tuple-element.44), channel_id=1, source_target_pairs={{0,12},{4,0},{8,4},{12,8},{1,13},{5,1},{9,5},{13,9},{2,14},{6,2},{... | collective-permute-start | bytes 294920 | tf_op jit(solution)/shard_map/ppermute | solution.py:363
  28.6 11.3 %collective-permute-start.3 = (bf16[1024,128]{1,0:T(8,128)(2,1)S(1)}, bf16[1024,128]{1,0:T(8,128)(2,1)S(1)}, u32[]{:S(2)}, u32[]{:S(2)}) collective-permute-start(bf16[1024,128]{1,0:T(8,128)(2,1)S(1)} %bitcast.12), channel_id=1, source_target_pairs={{0,16},{16,32},{32,48},{48,64},{64,80},{80,96},{96,112},{112,0},{1... | collective-permute-start | bytes 786440 | tf_op jit(solution)/shard_map/ppermute | solution.py:367
  30.2 9.6 %collective-permute-start.4 = (bf16[1024,128]{1,0:T(8,128)(2,1)S(1)}, bf16[1024,128]{1,0:T(8,128)(2,1)S(1)}, u32[]{:S(2)}, u32[]{:S(2)}) collective-permute-start(bf16[1024,128]{1,0:T(8,128)(2,1)S(1)} %bitcast.13), channel_id=1, source_target_pairs={{0,112},{16,0},{32,16},{48,32},{64,48},{80,64},{96,80},{112,96},{1... | collective-permute-start | bytes 786440 | tf_op jit(solution)/shard_map/ppermute | solution.py:367
  34.3 8.3 %collective-permute-start.7 = (bf16[4,128,128]{2,1,0:T(8,128)(2,1)S(1)}, bf16[4,128,128]{2,1,0:T(8,128)(2,1)S(1)}, u32[]{:S(2)}, u32[]{:S(2)}) collective-permute-start(bf16[4,128,128]{2,1,0:T(8,128)(2,1)S(1)} %pad_maximum_fusion.3.mine_ref), channel_id=1, source_target_pairs={{0,128},{128,0},{1,129},{129,1},{2,130},{130,2},{3,131},{131,3},{4... | collective-permute-start | bytes 393224 | tf_op jit(solution)/shard_map/ppermute | solution.py:368
  39.9 8.9 %collective-permute-start.5 = (bf16[1024,128]{1,0:T(8,128)(2,1)S(1)}, bf16[1024,128]{1,0:T(8,128)(2,1)S(1)}, u32[]{:S(2)}, u32[]{:S(2)}) collective-permute-start(bf16[1024,128]{1,0:T(8,128)(2,1)S(1)} %collective-permute-done.3.low_ref), channel_id=1, source_target_pairs={{0,16},{16,32},{32,48},{48,64},{64,80},{80,96},{96,112},{112,0},{1... | collective-permute-start | bytes 786440 | tf_op jit(solution)/shard_map/ppermute | solution.py:375
  39.9 8.9 %collective-permute-start.6 = (bf16[1024,128]{1,0:T(8,128)(2,1)S(1)}, bf16[1024,128]{1,0:T(8,128)(2,1)S(1)}, u32[]{:S(2)}, u32[]{:S(2)}) collective-permute-start(bf16[1024,128]{1,0:T(8,128)(2,1)S(1)} %collective-permute-done.4.high_ref), channel_id=1, source_target_pairs={{0,112},{16,0},{32,16},{48,32},{64,48},{80,64},{96,80},{112,96},{1... | collective-permute-start | bytes 786440 | tf_op jit(solution)/shard_map/ppermute | solution.py:375
  48.8 7.6 %collective-permute-start.8 = (bf16[1024,128]{1,0:T(8,128)(2,1)S(1)}, bf16[1024,128]{1,0:T(8,128)(2,1)S(1)}, u32[]{:S(2)}, u32[]{:S(2)}) collective-permute-start(bf16[1024,128]{1,0:T(8,128)(2,1)S(1)} %collective-permute-done.5.refs_3_), channel_id=1, source_target_pairs={{0,16},{16,32},{32,48},{48,64},{64,80},{80,96},{96,112},{112,0},{1... | collective-permute-start | bytes 786440 | tf_op jit(solution)/shard_map/ppermute | solution.py:375
  48.9 7.6 %collective-permute-start.9 = (bf16[1024,128]{1,0:T(8,128)(2,1)S(1)}, bf16[1024,128]{1,0:T(8,128)(2,1)S(1)}, u32[]{:S(2)}, u32[]{:S(2)}) collective-permute-start(bf16[1024,128]{1,0:T(8,128)(2,1)S(1)} %collective-permute-done.6.refs_4_), channel_id=1, source_target_pairs={{0,112},{16,0},{32,16},{48,32},{64,48},{80,64},{96,80},{112,96},{1... | collective-permute-start | bytes 786440 | tf_op jit(solution)/shard_map/ppermute | solution.py:375
  56.5 8.0 %collective-permute-start.10 = (bf16[512,128]{1,0:T(8,128)(2,1)S(1)}, bf16[512,128]{1,0:T(8,128)(2,1)S(1)}, u32[]{:S(2)}, u32[]{:S(2)}) collective-permute-start(bf16[512,128]{1,0:T(8,128)(2,1)S(1)} %slice.14), channel_id=1, source_target_pairs={{0,16},{16,32},{32,48},{48,64},{64,80},{80,96},{96,112},{112,0},{1... | collective-permute-start | bytes 393224 | tf_op jit(solution)/shard_map/ppermute | solution.py:377
  56.6 7.9 %collective-permute-start.11 = (bf16[512,128]{1,0:T(8,128)(2,1)S(1)}, bf16[512,128]{1,0:T(8,128)(2,1)S(1)}, u32[]{:S(2)}, u32[]{:S(2)}) collective-permute-start(bf16[512,128]{1,0:T(8,128)(2,1)S(1)} %slice.15), channel_id=1, source_target_pairs={{0,112},{16,0},{32,16},{48,32},{64,48},{80,64},{96,80},{112,96},{1... | collective-permute-start | bytes 393224 | tf_op jit(solution)/shard_map/ppermute | solution.py:378
  66.1 5.4 %collective-permute-start.12 = (bf16[528,128]{1,0:T(8,128)(2,1)S(1)}, bf16[528,128]{1,0:T(8,128)(2,1)S(1)}, u32[]{:S(2)}, u32[]{:S(2)}) collective-permute-start(bf16[528,128]{1,0:T(8,128)(2,1)S(1)} %attend_last_other.1), channel_id=1, source_target_pairs={{0,128},{128,0},{1,129},{129,1},{2,130},{130,2},{3,131},{131,3},{4... | collective-permute-start | bytes 405512 | tf_op jit(solution)/shard_map/ppermute | solution.py:388
  71.7 3.6 %collective-permute-start.13 = (bf16[128,128]{1,0:T(8,128)(2,1)S(1)}, bf16[128,128]{1,0:T(8,128)(2,1)S(1)}, u32[]{:S(2)}, u32[]{:S(2)}) collective-permute-start(bf16[128,128]{1,0:T(8,128)(2,1)S(1)} %get-tuple-element.73), channel_id=1, source_target_pairs={{0,12},{4,0},{8,4},{12,8},{1,13},{5,1},{9,5},{13,9},{2,14},{6,2},{... | collective-permute-start | bytes 98312 | tf_op jit(solution)/shard_map/ppermute | solution.py:390
  73.0 4.3 %collective-permute-start.14 = (bf16[128,128]{1,0:T(8,128)(2,1)S(1)}, bf16[128,128]{1,0:T(8,128)(2,1)S(1)}, u32[]{:S(2)}, u32[]{:S(2)}) collective-permute-start(bf16[128,128]{1,0:T(8,128)(2,1)S(1)} %get-tuple-element.74), channel_id=1, source_target_pairs={{0,8},{4,12},{8,0},{12,4},{1,9},{5,13},{9,1},{13,5},{2,10},{6,14},... | collective-permute-start | bytes 98312 | tf_op jit(solution)/shard_map/ppermute | solution.py:390
  73.6 4.1 %collective-permute-start.15 = (bf16[128,128]{1,0:T(8,128)(2,1)S(1)}, bf16[128,128]{1,0:T(8,128)(2,1)S(1)}, u32[]{:S(2)}, u32[]{:S(2)}) collective-permute-start(bf16[128,128]{1,0:T(8,128)(2,1)S(1)} %get-tuple-element.75), channel_id=1, source_target_pairs={{0,4},{4,8},{8,12},{12,0},{1,5},{5,9},{9,13},{13,1},{2,6},{6,10},{... | collective-permute-start | bytes 98312 | tf_op jit(solution)/shard_map/ppermute | solution.py:390
Sparse Core Ops, SparseCore 0:
  28.7 34.3 all-gather.1

commit v3 on v2

--- a/solution.py
+++ b/solution.py
@@ -27,10 +27,16 @@
 
 
 def project_kernel(
-    temper_ref, x_ref, gain_hbm, wq_hbm, wk_hbm, wv_hbm, *refs
+    x_ref, temper_hbm, gain_hbm, wq_hbm, wk_hbm, wv_hbm, *refs
 ):
-    out_refs, (stage_ref, gain_ref, wq_ref, wk_ref, wv_ref, sems) = refs[:NY], refs[NY:]
-    pairs = ((gain_hbm, gain_ref), (wq_hbm, wq_ref), (wk_hbm, wk_ref), (wv_hbm, wv_ref))
+    out_refs, (stage_ref, temper_ref, gain_ref, wq_ref, wk_ref, wv_ref, sems) = refs[:NY], refs[NY:]
+    pairs = (
+        (gain_hbm, gain_ref),
+        (wq_hbm, wq_ref),
+        (wk_hbm, wk_ref),
+        (wv_hbm, wv_ref),
+        (temper_hbm, temper_ref),
+    )
     copies = [pltpu.make_async_copy(source, target, sems.at[n]) for n, (source, target) in enumerate(pairs)]
     for copy in copies:
         copy.start()
@@ -45,6 +51,8 @@
     copies[3].wait()
     values = jnp.dot(normed, wv_ref[...], preferred_element_type=F32)
 
+    copies[4].wait()
+
     def unit(part):
         return part * lax.rsqrt(jnp.mean(part * part, axis=-1, keepdims=True) + EPS)
 
@@ -65,19 +73,20 @@
     return pl.pallas_call(
         project_kernel,
         out_shape=[jax.ShapeDtypeStruct((ROWS + BLOCK, 128), BF16)] * NY,
-        in_specs=[SMEM, VMEM, HBM, HBM, HBM, HBM],
+        in_specs=[VMEM, HBM, HBM, HBM, HBM, HBM],
         out_specs=[VMEM] * NY,
         scratch_shapes=[
             pltpu.VMEM((NY, ROWS + BLOCK, 128), BF16),
+            pltpu.SMEM((4,), F32),
             pltpu.VMEM((1, 1024), F32),
             pltpu.VMEM((1024, 256), BF16),
             pltpu.VMEM((1024, 256), BF16),
             pltpu.VMEM((1024, 256), BF16),
-            pltpu.SemaphoreType.DMA((4,)),
+            pltpu.SemaphoreType.DMA((5,)),
         ],
         compiler_params=PARAMS,
         name="project",
-    )(temper, whole, hold(gain), hold(w_query), hold(w_key), hold(w_value))
+    )(whole, hold(temper), hold(gain), hold(w_query), hold(w_key), hold(w_value))
 
 
 QT = 256
@@ -328,8 +337,15 @@
     )(mine, message)
 
 
-def output_kernel(a_ref, w_ref, out_ref):
-    y = lax.axis_index("y").astype(jnp.int32)
+def output_kernel(a_ref, own_ref, near_ref, far_ref, out_ref, w_ref):
+    y, xl, core = (lax.axis_index(a).astype(jnp.int32) for a in ("y", "xl", "core"))
+    for side, turn, piece in (
+        (xl, core, own_ref[...]),
+        (xl, 1 - core, near_ref[...]),
+        (1 - xl, core, far_ref[:256, :]),
+        (1 - xl, 1 - core, far_ref[256:, :]),
+    ):
+        w_ref[pl.ds(pl.multiple_of((2 * side + turn) * 256, 256), 256), :] = piece
     lane = lax.broadcasted_iota(jnp.int32, (BLOCK, 128), 1)
     lefts, rights, weights = [], [], []
     for source in range(4):
@@ -346,15 +362,16 @@
     out_ref[BLOCK:, :] = jnp.dot(jnp.concatenate(rights, axis=1), w, preferred_element_type=F32).astype(BF16)
 
 
-def output(attended, w):
+def output(attended, own, near, far):
     return pl.pallas_call(
         output_kernel,
         out_shape=jax.ShapeDtypeStruct((ROWS, 256), BF16),
-        in_specs=[VMEM, VMEM],
+        in_specs=[VMEM] * 4,
         out_specs=VMEM,
+        scratch_shapes=[pltpu.VMEM((1024, 256), BF16)],
         compiler_params=PARAMS,
         name="output",
-    )(attended, w)
+    )(attended, own, near, far)
 
 
 def shards(tokens, gain, w_query, w_key, w_value, w_out, temper, adjacency, order):
@@ -367,10 +384,12 @@
     low, high = lax.ppermute(kv, "z", ring(NZ, 1)), lax.ppermute(kv, "z", ring(NZ, -1))
     other = lax.ppermute(query, "xh", [(0, 1), (1, 0)])
     q, bias, acc = attend_first(order, adjacency, query, kv)
-    w_late, _ = lax.optimization_barrier((w_out, kv))
-    w_whole = lax.all_gather(w_late, HEAD, axis=0, tiled=True)
+    xl, core = lax.axis_index("xl"), lax.axis_index("core")
+    block = lambda side, turn: lax.dynamic_slice_in_dim(w_out, (2 * side + turn) * 256, 256, 1)
+    own, relayed = block(xl, core), block(1 - xl, core)
+    near = jnp.concatenate([block(xl, 1 - core), block(1 - xl, 1 - core)], axis=0)
     for step in (1, 2, 3):
-        low, high, acc = lax.optimization_barrier((low, high, acc))
+        low, high, acc, near = lax.optimization_barrier((low, high, acc, near))
         if step < 3:
             next_low, next_high = lax.ppermute(low, "z", ring(NZ, 1)), lax.ppermute(high, "z", ring(NZ, -1))
         else:
@@ -381,15 +400,19 @@
         else:
             acc, acc2 = attend_middle(step, q, q2, bias, low, high, acc, acc2)
         low, high = next_low, next_high
-    low, high, acc, w_whole = lax.optimization_barrier((low, high, acc, w_whole))
-    w_columns = lax.dynamic_slice_in_dim(w_whole, lax.axis_index(HEAD) * 256, 256, 1)
+        if step == 1:
+            near = lax.ppermute(near, "core", ring(NCORE, 1))
+        if step == 2:
+            far = lax.ppermute(jnp.concatenate([relayed, near[256:]], axis=0), "xl", ring(NXL, 1))
+            near = near[:256]
+    low, high, acc, own, near, far = lax.optimization_barrier((low, high, acc, own, near, far))
     message = attend_last_other(q2, bias, low, high, acc2)
     message, acc = lax.optimization_barrier((message, acc))
     message = lax.ppermute(message, "xh", [(0, 1), (1, 0)])
     attended = finish(attend_last_mine(q, bias, low, high, acc), message)
     back = jnp.stack([attended[0]] + [lax.ppermute(attended[s], "y", ring(NY, -s)) for s in range(1, NY)])
     gathered = lax.all_gather(back, HEAD, axis=0, tiled=True)
-    return output(gathered, w_columns)
+    return output(gathered, own, near, far)
 
 
 def solution(mesh):

time: 98.9 us -> 87.8 us (0.89)
  between operations: 13.6 us -> 0.18 us
  waiting for transfers between devices: 8.94 us -> 12 us
  starting transfers between devices: 25.6 us -> 27.9 us
  blocking collectives: 23 us -> 20.9 us
    ppermute x0 -> x2, starting transfers between devices: none -> 2.99 us  [the longest x1 2.09 us: shards(): near = lax.ppermute(near, 'core', ring(NCORE, 1))]
    ppermute x2, waiting for transfers between devices: 0.01 us -> 2.43 us  [shards(): lax.ppermute(low, 'z', ring(NZ, 1))]
    all_gather x1, blocking collectives: 13.1 us -> 11.1 us  [shards(): gathered = lax.all_gather(back, HEAD, axis=0, tiled=True)]
    ppermute x3, waiting for transfers between devices: 2.29 us -> 3.37 us  [shards(): lax.ppermute(attended[s], 'y', ring(NY, -s))]
    ppermute x2, starting transfers between devices: 5.34 us -> 4.27 us  [shards(): lax.ppermute(high, 'z', ring(NZ, -1))]
    dynamic_slice x1, local copies, waits for them, and re-layouts: 1.08 us -> 0.07 us  [shards(): lax.dynamic_slice_in_dim(w_out, (2 * side + turn) * 256, 256, 1)]
    ppermute x1, waiting for transfers between devices: 1.04 us -> 0.04 us  [shards(): lax.ppermute(kv, 'z', ring(NZ, 1))]
  transfers between devices with their start and end apart: 17 -> 18, of which waited for: 7 -> 8; matrix products, arithmetic and copies ran while one was open for 1% -> 0% of each run, Pallas kernels for 20% -> 22%
where the time goes in v3:
time: 87.8 us; the launch traced here: 87.7 us
  starting transfers between devices  27.9 us (32%)
  Pallas kernels  25.7 us (29%)
  blocking collectives  20.9 us (24%)
  waiting for transfers between devices  12 us (14%)
  local copies, waits for them, and re-layouts  0.93 us (1%)
    all_gather x1, blocking collectives, shards(): gathered = lax.all_gather(back, HEAD, axis=0, tiled=True)  11.1 us
    all_gather x1, blocking collectives, shards(): whole = lax.all_gather(tokens, HEAD, axis=1, tiled=True)  9.78 us
    pallas_call x2, Pallas kernels, attend_middle(): pl.pallas_call(lambda *refs: middle_kernel(step, *refs), out_shape=(ACC,...  9.75 us
    pallas_call x1, Pallas kernels, attend_second(): pl.pallas_call(second_kernel, out_shape=(WIDE, ACC, ACC), in_specs=[VMEM]...  6.24 us
    ppermute x2, starting transfers between devices, shards(): lax.ppermute(high, 'z', ring(NZ, -1))  4.27 us
    ppermute x1, starting transfers between devices, shards(): lax.ppermute(kv, 'z', ring(NZ, -1))  4.03 us
    ppermute x3, starting transfers between devices, shards(): lax.ppermute(messages[s], 'y', ring(NY, s))  3.99 us
    ppermute x3, waiting for transfers between devices, shards(): lax.ppermute(messages[s], 'y', ring(NY, s))  3.91 us
  transfers between devices with their start and end apart: 18, of which 8 were waited for; matrix products, arithmetic and copies ran while one was open for 0% of the time, Pallas kernels for 22%

profile of v3, /device:TPU:1, one launch (start us, length us, event | category | flops | bytes accessed | tf_op | source)
XLA Modules:
  0.0 87.7 jit_solution(6985054010714828368)
XLA Ops:
  0.0 9.8 %all_gather.6.x_ref = bf16[256,1024]{1,0:T(8,128)(2,1)S(1)} all-gather(bf16[256,256]{1,0:T(8,128)(2,1)} %param.9), channel_id=1, replica_groups=mesh['xh'=2,'z'=8,'y'=4,'xl'=2,'core'=2] {'xl','core'}, dimensions={1}, use_global_device_ids=true | all-gather | bytes 655360 | tf_op jit(solution)/shard_map/all_gather | solution.py:378
  9.8 3.3 %project.1 = (bf16[384,128]{1,0:T(8,128)(2,1)S(1)}, bf16[384,128]{1,0:T(8,128)(2,1)S(1)}, bf16[384,128]{1,0:T(8,128)(2,1)S(1)}, bf16[384,128]{1,0:T(8,128)(2,1)S(1)}) custom-call(bf16[256,1024]{1,0:T(8,128)(2,1)S(1)} %all_gather.6.x_ref, f32[4]{0:T(128)} %temper_hbm.1, f32[1,1024]{1,0:T(1,128)} %bitcast.26, bf16[1024,256]{1,0:T(8,128)(2,1)} %wq_hbm.1, ...), custom_call_target="tpu_custom_call" | custom-call | tf_op jit(solution)/shard_map/project/pallas_call | solution.py:73
  13.4 2.6 %collective-permute-start.1 = (bf16[384,128]{1,0:T(8,128)(2,1)S(1)}, bf16[384,128]{1,0:T(8,128)(2,1)S(1)}, u32[]{:S(2)}, u32[]{:S(2)}) collective-permute-start(bf16[384,128]{1,0:T(8,128)(2,1)S(1)} %get-tuple-element.47), channel_id=1, source_target_pairs={{0,8},{4,12},{8,0},{12,4},{1,9},{5,13},{9,1},{13,5},{2,10},{6,14},... | collective-permute-start | bytes 294920 | tf_op jit(solution)/shard_map/ppermute | solution.py:380
  16.1 1.1 %collective-permute-start.2 = (bf16[384,128]{1,0:T(8,128)(2,1)S(1)}, bf16[384,128]{1,0:T(8,128)(2,1)S(1)}, u32[]{:S(2)}, u32[]{:S(2)}) collective-permute-start(bf16[384,128]{1,0:T(8,128)(2,1)S(1)} %get-tuple-element.48), channel_id=1, source_target_pairs={{0,12},{4,0},{8,4},{12,8},{1,13},{5,1},{9,5},{13,9},{2,14},{6,2},{... | collective-permute-start | bytes 294920 | tf_op jit(solution)/shard_map/ppermute | solution.py:380
  17.1 1.5 %collective-permute-done = bf16[384,128]{1,0:T(8,128)(2,1)S(1)} collective-permute-done((bf16[384,128]{1,0:T(8,128)(2,1)S(1)}, bf16[384,128]{1,0:T(8,128)(2,1)S(1)}, u32[]{:S(2)}, u32[]{:S(2)}) %collective-permute-start) | collective-permute-done | bytes 98336 | tf_op jit(solution)/shard_map/ppermute | solution.py:380
  18.7 2.3 %collective-permute-done.1 = bf16[384,128]{1,0:T(8,128)(2,1)S(1)} collective-permute-done((bf16[384,128]{1,0:T(8,128)(2,1)S(1)}, bf16[384,128]{1,0:T(8,128)(2,1)S(1)}, u32[]{:S(2)}, u32[]{:S(2)}) %collective-permute-start.1) | collective-permute-done | bytes 98336 | tf_op jit(solution)/shard_map/ppermute | solution.py:380
  21.1 1.6 %collective-permute-start.3 = (bf16[1024,128]{1,0:T(8,128)(2,1)S(1)}, bf16[1024,128]{1,0:T(8,128)(2,1)S(1)}, u32[]{:S(2)}, u32[]{:S(2)}) collective-permute-start(bf16[1024,128]{1,0:T(8,128)(2,1)S(1)} %bitcast.12), channel_id=1, source_target_pairs={{0,16},{16,32},{32,48},{48,64},{64,80},{80,96},{96,112},{112,0},{1... | collective-permute-start | bytes 786440 | tf_op jit(solution)/shard_map/ppermute | solution.py:384
  22.7 4.0 %collective-permute-start.4 = (bf16[1024,128]{1,0:T(8,128)(2,1)S(1)}, bf16[1024,128]{1,0:T(8,128)(2,1)S(1)}, u32[]{:S(2)}, u32[]{:S(2)}) collective-permute-start(bf16[1024,128]{1,0:T(8,128)(2,1)S(1)} %bitcast.13), channel_id=1, source_target_pairs={{0,112},{16,0},{32,16},{48,32},{64,48},{80,64},{96,80},{112,96},{1... | collective-permute-start | bytes 786440 | tf_op jit(solution)/shard_map/ppermute | solution.py:384
  26.8 2.5 %collective-permute-start.7 = (bf16[4,128,128]{2,1,0:T(8,128)(2,1)S(1)}, bf16[4,128,128]{2,1,0:T(8,128)(2,1)S(1)}, u32[]{:S(2)}, u32[]{:S(2)}) collective-permute-start(bf16[4,128,128]{2,1,0:T(8,128)(2,1)S(1)} %pad_maximum_fusion.5.mine_ref), channel_id=1, source_target_pairs={{0,128},{128,0},{1,129},{129,1},{2,130},{130,2},{3,131},{131,3},{4... | collective-permute-start | bytes 393224 | tf_op jit(solution)/shard_map/ppermute | solution.py:385
  29.4 0.8 copy-done
  30.2 2.1 %attend_first.1 = (bf16[1024,128]{1,0:T(8,128)(2,1)S(1)}, f32[8,8,128]{2,1,0:T(8,128)S(1)}, f32[1024,128]{1,0:T(8,128)S(1)}) custom-call(s32[128]{0:T(128)S(1)} %copy-done.1, s32[128,128]{1,0:T(8,128)S(1)} %copy-done, bf16[4,128,128]{2,1,0:T(8,128)(2,1)S(1)} %pad_maximum_fusion.5.mine_ref, bf16[1024,128]{1,0:T(8,128)(2,1)S(1)} %bitcast.14), custom_call_target="tpu_custom_call" | custom-call | flops 536870912 | bytes 4194304 | tf_op jit(solution)/shard_map/attend_first/pallas_call | solution.py:184
  32.4 2.7 %collective-permute-start.6 = (bf16[1024,128]{1,0:T(8,128)(2,1)S(1)}, bf16[1024,128]{1,0:T(8,128)(2,1)S(1)}, u32[]{:S(2)}, u32[]{:S(2)}) collective-permute-start(bf16[1024,128]{1,0:T(8,128)(2,1)S(1)} %collective-permute-done.4.high_ref), channel_id=1, source_target_pairs={{0,112},{16,0},{32,16},{48,32},{64,48},{80,64},{96,80},{112,96},{1... | collective-permute-start | bytes 786440 | tf_op jit(solution)/shard_map/ppermute | solution.py:394
  35.1 2.1 %collective-permute-start.8 = (bf16[512,256]{1,0:T(8,128)(2,1)S(1)}, bf16[512,256]{1,0:T(8,128)(2,1)S(1)}, u32[]{:S(2)}, u32[]{:S(2)}) collective-permute-start(bf16[512,256]{1,0:T(8,128)(2,1)S(1)} %pad_maximum_fusion.3), channel_id=1, source_target_pairs={{0,1},{1,0},{2,3},{3,2},{4,5},{5,4},{6,7},{7,6},{8,9},{9,8},{10,11... | collective-permute-start | bytes 786440 | tf_op jit(solution)/shard_map/ppermute | solution.py:404
  37.2 6.2 %attend_second.1 = (bf16[1024,128]{1,0:T(8,128)(2,1)S(1)}, f32[1024,128]{1,0:T(8,128)S(1)}, f32[1024,128]{1,0:T(8,128)S(1)}) custom-call(bf16[1024,128]{1,0:T(8,128)(2,1)S(1)} %get-tuple-element.51.q_ref.refs_0_, bf16[4,128,128]{2,1,0:T(8,128)(2,1)S(1)} %collective-permute-done.7.other_ref, ...), custom_call_target="tpu_custom_call", output_to_operand_aliasing={{1}: (6, {})} | custom-call | flops 2684354560 | bytes 4194304 | tf_op jit(solution)/shard_map/attend_second/pallas_call | solution.py:222
  43.5 1.6 %collective-permute-start.10 = (bf16[1024,128]{1,0:T(8,128)(2,1)S(1)}, bf16[1024,128]{1,0:T(8,128)(2,1)S(1)}, u32[]{:S(2)}, u32[]{:S(2)}) collective-permute-start(bf16[1024,128]{1,0:T(8,128)(2,1)S(1)} %collective-permute-done.6.refs_4_), channel_id=1, source_target_pairs={{0,112},{16,0},{32,16},{48,32},{64,48},{80,64},{96,80},{112,96},{1... | collective-permute-start | bytes 786440 | tf_op jit(solution)/shard_map/ppermute | solution.py:394
  45.1 0.9 %collective-permute-start.13 = (bf16[512,256]{1,0:T(8,128)(2,1)S(1)}, bf16[512,256]{1,0:T(8,128)(2,1)S(1)}, u32[]{:S(2)}, u32[]{:S(2)}) collective-permute-start(bf16[512,256]{1,0:T(8,128)(2,1)S(1)} %pad_maximum_fusion.4), channel_id=1, source_target_pairs={{0,2},{2,0},{1,3},{3,1},{4,6},{6,4},{5,7},{7,5},{8,10},{10,8},{9,1... | collective-permute-start | bytes 786440 | tf_op jit(solution)/shard_map/ppermute | solution.py:406
  46.0 4.9 %attend_middle.2 = (f32[1024,128]{1,0:T(8,128)S(1)}, f32[1024,128]{1,0:T(8,128)S(1)}) custom-call(bf16[1024,128]{1,0:T(8,128)(2,1)S(1)} %get-tuple-element.51.q_ref.refs_0_, bf16[1024,128]{1,0:T(8,128)(2,1)S(1)} %get-tuple-element.61.refs_1_.q_ref, ...), custom_call_target="tpu_custom_call", output_to_operand_aliasing={{0}: (5, {}), {1}: (6, {})} | custom-call | flops 2147483648 | bytes 4194304 | tf_op jit(solution)/shard_map/attend_middle/pallas_call | solution.py:240
  50.9 0.6 collective-permute-done.10.refs_4_
  51.5 2.4 %collective-permute-done.9.refs_3_ = bf16[1024,128]{1,0:T(8,128)(2,1)S(1)} collective-permute-done((bf16[1024,128]{1,0:T(8,128)(2,1)S(1)}, bf16[1024,128]{1,0:T(8,128)(2,1)S(1)}, u32[]{:S(2)}, u32[]{:S(2)}) %collective-permute-start.9) | collective-permute-done | bytes 262176 | tf_op jit(solution)/shard_map/ppermute | solution.py:394
  54.0 3.0 %collective-permute-start.12 = (bf16[512,128]{1,0:T(8,128)(2,1)S(1)}, bf16[512,128]{1,0:T(8,128)(2,1)S(1)}, u32[]{:S(2)}, u32[]{:S(2)}) collective-permute-start(bf16[512,128]{1,0:T(8,128)(2,1)S(1)} %slice.22), channel_id=1, source_target_pairs={{0,112},{16,0},{32,16},{48,32},{64,48},{80,64},{96,80},{112,96},{1... | collective-permute-start | bytes 393224 | tf_op jit(solution)/shard_map/ppermute | solution.py:397
  57.0 4.9 %attend_middle.3 = (f32[1024,128]{1,0:T(8,128)S(1)}, f32[1024,128]{1,0:T(8,128)S(1)}) custom-call(bf16[1024,128]{1,0:T(8,128)(2,1)S(1)} %get-tuple-element.51.q_ref.refs_0_, bf16[1024,128]{1,0:T(8,128)(2,1)S(1)} %get-tuple-element.61.refs_1_.q_ref, ...), custom_call_target="tpu_custom_call", output_to_operand_aliasing={{0}: (5, {}), {1}: (6, {})} | custom-call | flops 2147483648 | bytes 4194304 | tf_op jit(solution)/shard_map/attend_middle/pallas_call | solution.py:240
  61.9 1.5 %attend_last_other.1 = bf16[528,128]{1,0:T(8,128)(2,1)S(1)} custom-call(bf16[1024,128]{1,0:T(8,128)(2,1)S(1)} %get-tuple-element.61.refs_1_.q_ref, f32[8,8,128]{2,1,0:T(8,128)S(1)} %get-tuple-element.52.bias_ref.refs_2_, bf16[512,128]{1,0:T(8,128)(2,1)S(1)} %collective-permute-done.11.low_ref, bf16[512,128]{1,0:T(8,128)(2,1)S(1)} %collective-permute-done.12.high_ref, ...), custom_call_target="tpu_custom_call" | custom-call | flops 536870912 | bytes 4194304 | tf_op jit(solution)/shard_map/attend_last_other/pallas_call | solution.py:283
  63.4 2.5 %collective-permute-start.14 = (bf16[528,128]{1,0:T(8,128)(2,1)S(1)}, bf16[528,128]{1,0:T(8,128)(2,1)S(1)}, u32[]{:S(2)}, u32[]{:S(2)}) collective-permute-start(bf16[528,128]{1,0:T(8,128)(2,1)S(1)} %attend_last_other.1), channel_id=1, source_target_pairs={{0,128},{128,0},{1,129},{129,1},{2,130},{130,2},{3,131},{131,3},{4... | collective-permute-start | bytes 405512 | tf_op jit(solution)/shard_map/ppermute | solution.py:411
  65.9 1.3 %attend_last_mine.1.mine_ref = f32[1024,128]{1,0:T(8,128)S(1)} custom-call(bf16[1024,128]{1,0:T(8,128)(2,1)S(1)} %get-tuple-element.51.q_ref.refs_0_, f32[8,8,128]{2,1,0:T(8,128)S(1)} %get-tuple-element.52.bias_ref.refs_2_, bf16[512,128]{1,0:T(8,128)(2,1)S(1)} %collective-permute-done.11.low_ref, ...), custom_call_target="tpu_custom_call", output_to_operand_aliasing={{}: (4, {})} | custom-call | flops 536870912 | bytes 4194304 | tf_op jit(solution)/shard_map/attend_last_mine/pallas_call | solution.py:300
  67.2 1.6 %collective-permute-done.14.message_ref = bf16[528,128]{1,0:T(8,128)(2,1)S(1)} collective-permute-done((bf16[528,128]{1,0:T(8,128)(2,1)S(1)}, bf16[528,128]{1,0:T(8,128)(2,1)S(1)}, u32[]{:S(2)}, u32[]{:S(2)}) %collective-permute-start.14) | collective-permute-done | bytes 135200 | tf_op jit(solution)/shard_map/ppermute | solution.py:411
  69.1 1.6 %collective-permute-start.15 = (bf16[128,128]{1,0:T(8,128)(2,1)S(1)}, bf16[128,128]{1,0:T(8,128)(2,1)S(1)}, u32[]{:S(2)}, u32[]{:S(2)}) collective-permute-start(bf16[128,128]{1,0:T(8,128)(2,1)S(1)} %get-tuple-element.79), channel_id=1, source_target_pairs={{0,12},{4,0},{8,4},{12,8},{1,13},{5,1},{9,5},{13,9},{2,14},{6,2},{... | collective-permute-start | bytes 98312 | tf_op jit(solution)/shard_map/ppermute | solution.py:413
  70.6 0.8 collective-permute-start.16
  71.4 0.6 collective-permute-start.17
  72.0 2.9 %collective-permute-done.16 = bf16[128,128]{1,0:T(8,128)(2,1)S(1)} collective-permute-done((bf16[128,128]{1,0:T(8,128)(2,1)S(1)}, bf16[128,128]{1,0:T(8,128)(2,1)S(1)}, u32[]{:S(2)}, u32[]{:S(2)}) %collective-permute-start.16) | collective-permute-done | bytes 32800 | tf_op jit(solution)/shard_map/ppermute | solution.py:413
  74.9 0.5 collective-permute-done.17
  75.4 11.1 %all_gather.7.a_ref = bf16[16,128,128]{2,1,0:T(8,128)(2,1)S(1)} all-gather(bf16[4,128,128]{2,1,0:T(8,128)(2,1)S(1)} %pad_maximum_fusion.6), channel_id=1, replica_groups=mesh['xh'=2,'z'=8,'y'=4,'xl'=2,'core'=2] {'xl','core'}, dimensions={0}, use_global_device_ids=true | all-gather | bytes 655360 | tf_op jit(solution)/shard_map/all_gather | solution.py:414
  86.5 1.1 %output.1 = bf16[256,256]{1,0:T(8,128)(2,1)} custom-call(bf16[16,128,128]{2,1,0:T(8,128)(2,1)S(1)} %all_gather.7.a_ref, bf16[256,256]{1,0:T(8,128)(2,1)S(1)} %get-tuple-element.82.own_ref, bf16[256,256]{1,0:T(8,128)(2,1)S(1)} %get-tuple-element.83.near_ref, bf16[512,256]{1,0:T(8,128)(2,1)S(1)} %collective-permute-done.13.far_ref), custom_call_target="tpu_custom_call" | custom-call | tf_op jit(solution)/shard_map/output/pallas_call | solution.py:366
  (30 shorter events, 1.1 us)
Async XLA Ops:
  13.1 5.5 %collective-permute-start = (bf16[384,128]{1,0:T(8,128)(2,1)S(1)}, bf16[384,128]{1,0:T(8,128)(2,1)S(1)}, u32[]{:S(2)}, u32[]{:S(2)}) collective-permute-start(bf16[384,128]{1,0:T(8,128)(2,1)S(1)} %get-tuple-element.46), channel_id=1, source_target_pairs={{0,4},{4,8},{8,12},{12,0},{1,5},{5,9},{9,13},{13,1},{2,6},{6,10},{... | collective-permute-start | bytes 294920 | tf_op jit(solution)/shard_map/ppermute | solution.py:380
  13.4 7.5 %collective-permute-start.1 = (bf16[384,128]{1,0:T(8,128)(2,1)S(1)}, bf16[384,128]{1,0:T(8,128)(2,1)S(1)}, u32[]{:S(2)}, u32[]{:S(2)}) collective-permute-start(bf16[384,128]{1,0:T(8,128)(2,1)S(1)} %get-tuple-element.47), channel_id=1, source_target_pairs={{0,8},{4,12},{8,0},{12,4},{1,9},{5,13},{9,1},{13,5},{2,10},{6,14},... | collective-permute-start | bytes 294920 | tf_op jit(solution)/shard_map/ppermute | solution.py:380
  16.1 5.0 %collective-permute-start.2 = (bf16[384,128]{1,0:T(8,128)(2,1)S(1)}, bf16[384,128]{1,0:T(8,128)(2,1)S(1)}, u32[]{:S(2)}, u32[]{:S(2)}) collective-permute-start(bf16[384,128]{1,0:T(8,128)(2,1)S(1)} %get-tuple-element.48), channel_id=1, source_target_pairs={{0,12},{4,0},{8,4},{12,8},{1,13},{5,1},{9,5},{13,9},{2,14},{6,2},{... | collective-permute-start | bytes 294920 | tf_op jit(solution)/shard_map/ppermute | solution.py:380
  21.0 5.7 %copy-start.2 = (bf16[256,1024]{1,0:T(8,128)(2,1)S(1)}, bf16[256,1024]{1,0:T(8,128)(2,1)}, u32[]{:S(2)}) copy-start(bf16[256,1024]{1,0:T(8,128)(2,1)} %param.14) | copy-start | bytes 1572868
  21.1 11.3 %collective-permute-start.3 = (bf16[1024,128]{1,0:T(8,128)(2,1)S(1)}, bf16[1024,128]{1,0:T(8,128)(2,1)S(1)}, u32[]{:S(2)}, u32[]{:S(2)}) collective-permute-start(bf16[1024,128]{1,0:T(8,128)(2,1)S(1)} %bitcast.12), channel_id=1, source_target_pairs={{0,16},{16,32},{32,48},{48,64},{64,80},{80,96},{96,112},{112,0},{1... | collective-permute-start | bytes 786440 | tf_op jit(solution)/shard_map/ppermute | solution.py:384
  22.7 9.6 %collective-permute-start.4 = (bf16[1024,128]{1,0:T(8,128)(2,1)S(1)}, bf16[1024,128]{1,0:T(8,128)(2,1)S(1)}, u32[]{:S(2)}, u32[]{:S(2)}) collective-permute-start(bf16[1024,128]{1,0:T(8,128)(2,1)S(1)} %bitcast.13), channel_id=1, source_target_pairs={{0,112},{16,0},{32,16},{48,32},{64,48},{80,64},{96,80},{112,96},{1... | collective-permute-start | bytes 786440 | tf_op jit(solution)/shard_map/ppermute | solution.py:384
  26.8 10.4 %collective-permute-start.7 = (bf16[4,128,128]{2,1,0:T(8,128)(2,1)S(1)}, bf16[4,128,128]{2,1,0:T(8,128)(2,1)S(1)}, u32[]{:S(2)}, u32[]{:S(2)}) collective-permute-start(bf16[4,128,128]{2,1,0:T(8,128)(2,1)S(1)} %pad_maximum_fusion.5.mine_ref), channel_id=1, source_target_pairs={{0,128},{128,0},{1,129},{129,1},{2,130},{130,2},{3,131},{131,3},{4... | collective-permute-start | bytes 393224 | tf_op jit(solution)/shard_map/ppermute | solution.py:385
  29.3 0.8 copy-start
  29.3 0.8 copy-start.1
  32.4 11.1 %collective-permute-start.5 = (bf16[1024,128]{1,0:T(8,128)(2,1)S(1)}, bf16[1024,128]{1,0:T(8,128)(2,1)S(1)}, u32[]{:S(2)}, u32[]{:S(2)}) collective-permute-start(bf16[1024,128]{1,0:T(8,128)(2,1)S(1)} %collective-permute-done.3.low_ref), channel_id=1, source_target_pairs={{0,16},{16,32},{32,48},{48,64},{64,80},{80,96},{96,112},{112,0},{1... | collective-permute-start | bytes 786440 | tf_op jit(solution)/shard_map/ppermute | solution.py:394
  32.4 11.0 %collective-permute-start.6 = (bf16[1024,128]{1,0:T(8,128)(2,1)S(1)}, bf16[1024,128]{1,0:T(8,128)(2,1)S(1)}, u32[]{:S(2)}, u32[]{:S(2)}) collective-permute-start(bf16[1024,128]{1,0:T(8,128)(2,1)S(1)} %collective-permute-done.4.high_ref), channel_id=1, source_target_pairs={{0,112},{16,0},{32,16},{48,32},{64,48},{80,64},{96,80},{112,96},{1... | collective-permute-start | bytes 786440 | tf_op jit(solution)/shard_map/ppermute | solution.py:394
  35.1 8.4 %collective-permute-start.8 = (bf16[512,256]{1,0:T(8,128)(2,1)S(1)}, bf16[512,256]{1,0:T(8,128)(2,1)S(1)}, u32[]{:S(2)}, u32[]{:S(2)}) collective-permute-start(bf16[512,256]{1,0:T(8,128)(2,1)S(1)} %pad_maximum_fusion.3), channel_id=1, source_target_pairs={{0,1},{1,0},{2,3},{3,2},{4,5},{5,4},{6,7},{7,6},{8,9},{9,8},{10,11... | collective-permute-start | bytes 786440 | tf_op jit(solution)/shard_map/ppermute | solution.py:404
  43.5 8.0 %collective-permute-start.10 = (bf16[1024,128]{1,0:T(8,128)(2,1)S(1)}, bf16[1024,128]{1,0:T(8,128)(2,1)S(1)}, u32[]{:S(2)}, u32[]{:S(2)}) collective-permute-start(bf16[1024,128]{1,0:T(8,128)(2,1)S(1)} %collective-permute-done.6.refs_4_), channel_id=1, source_target_pairs={{0,112},{16,0},{32,16},{48,32},{64,48},{80,64},{96,80},{112,96},{1... | collective-permute-start | bytes 786440 | tf_op jit(solution)/shard_map/ppermute | solution.py:394
  45.1 8.8 %collective-permute-start.9 = (bf16[1024,128]{1,0:T(8,128)(2,1)S(1)}, bf16[1024,128]{1,0:T(8,128)(2,1)S(1)}, u32[]{:S(2)}, u32[]{:S(2)}) collective-permute-start(bf16[1024,128]{1,0:T(8,128)(2,1)S(1)} %collective-permute-done.5.refs_3_), channel_id=1, source_target_pairs={{0,16},{16,32},{32,48},{48,64},{64,80},{80,96},{96,112},{112,0},{1... | collective-permute-start | bytes 786440 | tf_op jit(solution)/shard_map/ppermute | solution.py:394
  45.1 16.7 %collective-permute-start.13 = (bf16[512,256]{1,0:T(8,128)(2,1)S(1)}, bf16[512,256]{1,0:T(8,128)(2,1)S(1)}, u32[]{:S(2)}, u32[]{:S(2)}) collective-permute-start(bf16[512,256]{1,0:T(8,128)(2,1)S(1)} %pad_maximum_fusion.4), channel_id=1, source_target_pairs={{0,2},{2,0},{1,3},{3,1},{4,6},{6,4},{5,7},{7,5},{8,10},{10,8},{9,1... | collective-permute-start | bytes 786440 | tf_op jit(solution)/shard_map/ppermute | solution.py:406
  53.9 8.0 %collective-permute-start.11 = (bf16[512,128]{1,0:T(8,128)(2,1)S(1)}, bf16[512,128]{1,0:T(8,128)(2,1)S(1)}, u32[]{:S(2)}, u32[]{:S(2)}) collective-permute-start(bf16[512,128]{1,0:T(8,128)(2,1)S(1)} %slice.21), channel_id=1, source_target_pairs={{0,16},{16,32},{32,48},{48,64},{64,80},{80,96},{96,112},{112,0},{1... | collective-permute-start | bytes 393224 | tf_op jit(solution)/shard_map/ppermute | solution.py:396
  54.0 7.9 %collective-permute-start.12 = (bf16[512,128]{1,0:T(8,128)(2,1)S(1)}, bf16[512,128]{1,0:T(8,128)(2,1)S(1)}, u32[]{:S(2)}, u32[]{:S(2)}) collective-permute-start(bf16[512,128]{1,0:T(8,128)(2,1)S(1)} %slice.22), channel_id=1, source_target_pairs={{0,112},{16,0},{32,16},{48,32},{64,48},{80,64},{96,80},{112,96},{1... | collective-permute-start | bytes 393224 | tf_op jit(solution)/shard_map/ppermute | solution.py:397
  63.4 5.4 %collective-permute-start.14 = (bf16[528,128]{1,0:T(8,128)(2,1)S(1)}, bf16[528,128]{1,0:T(8,128)(2,1)S(1)}, u32[]{:S(2)}, u32[]{:S(2)}) collective-permute-start(bf16[528,128]{1,0:T(8,128)(2,1)S(1)} %attend_last_other.1), channel_id=1, source_target_pairs={{0,128},{128,0},{1,129},{129,1},{2,130},{130,2},{3,131},{131,3},{4... | collective-permute-start | bytes 405512 | tf_op jit(solution)/shard_map/ppermute | solution.py:411
  69.1 2.9 %collective-permute-start.15 = (bf16[128,128]{1,0:T(8,128)(2,1)S(1)}, bf16[128,128]{1,0:T(8,128)(2,1)S(1)}, u32[]{:S(2)}, u32[]{:S(2)}) collective-permute-start(bf16[128,128]{1,0:T(8,128)(2,1)S(1)} %get-tuple-element.79), channel_id=1, source_target_pairs={{0,12},{4,0},{8,4},{12,8},{1,13},{5,1},{9,5},{13,9},{2,14},{6,2},{... | collective-permute-start | bytes 98312 | tf_op jit(solution)/shard_map/ppermute | solution.py:413
  70.6 4.3 %collective-permute-start.16 = (bf16[128,128]{1,0:T(8,128)(2,1)S(1)}, bf16[128,128]{1,0:T(8,128)(2,1)S(1)}, u32[]{:S(2)}, u32[]{:S(2)}) collective-permute-start(bf16[128,128]{1,0:T(8,128)(2,1)S(1)} %get-tuple-element.80), channel_id=1, source_target_pairs={{0,8},{4,12},{8,0},{12,4},{1,9},{5,13},{9,1},{13,5},{2,10},{6,14},... | collective-permute-start | bytes 98312 | tf_op jit(solution)/shard_map/ppermute | solution.py:413
  71.4 4.0 %collective-permute-start.17 = (bf16[128,128]{1,0:T(8,128)(2,1)S(1)}, bf16[128,128]{1,0:T(8,128)(2,1)S(1)}, u32[]{:S(2)}, u32[]{:S(2)}) collective-permute-start(bf16[128,128]{1,0:T(8,128)(2,1)S(1)} %get-tuple-element.81), channel_id=1, source_target_pairs={{0,4},{4,8},{8,12},{12,0},{1,5},{5,9},{9,13},{13,1},{2,6},{6,10},{... | collective-permute-start | bytes 98312 | tf_op jit(solution)/shard_map/ppermute | solution.py:413

commit v4 on v3

--- a/solution.py
+++ b/solution.py
@@ -194,60 +194,70 @@
 
 
 def both_tiles(step, bias_ref, low_ref, high_ref, kx_ref, vx_ref, pairs):
-    kx_ref[0], vx_ref[0] = split_kv(low_ref[...], -step, bias_ref)
-    kx_ref[1], vx_ref[1] = split_kv(high_ref[...], step, bias_ref)
-
-    def body(n, carry):
-        kx, vx = kx_ref[n], vx_ref[n]
-        for q_ref, acc_ref in pairs:
-            tile(q_ref, kx, vx, add(acc_ref))
-        return carry
-
-    lax.fori_loop(0, 2, body, 0)
-
-
-SPLIT = [pltpu.VMEM((2, NK, 128), BF16), pltpu.VMEM((2, NK, 128), BF16)]
-
-
-def second_kernel(
-    q_ref, other_ref, bias_ref, kv_ref, low_ref, high_ref, acc_in, q2_ref, acc_ref, acc2_ref, kx_ref, vx_ref
-):
+    kx_ref[:NK, :], vx_ref[:NK, :] = split_kv(low_ref[...], -step, bias_ref)
+    kx_ref[NK:, :], vx_ref[NK:, :] = split_kv(high_ref[...], step, bias_ref)
+    for q_ref, acc_ref in pairs:
+        tile(q_ref, kx_ref[...], vx_ref[...], add(acc_ref))
+
+
+SPLIT = [pltpu.VMEM((2 * NK, 128), BF16), pltpu.VMEM((2 * NK, 128), BF16)]
+
+
+def second_kernel(q_ref, other_ref, bias_ref, low_ref, high_ref, acc_in, q2_ref, acc_ref, acc2_ref, kx_ref, vx_ref):
     widen(other_ref, 8, q2_ref)
-    kx, vx = split_kv(kv_ref[...], 0, bias_ref)
-    tile(q2_ref, kx, vx, put(acc2_ref))
+    acc2_ref[...] = jnp.zeros_like(acc2_ref)
     both_tiles(1, bias_ref, low_ref, high_ref, kx_ref, vx_ref, ((q_ref, acc_ref), (q2_ref, acc2_ref)))
 
 
-def attend_second(q, other, bias, kv, low, high, acc):
+def attend_second(q, other, bias, low, high, acc):
     return pl.pallas_call(
         second_kernel,
         out_shape=(WIDE, ACC, ACC),
-        in_specs=[VMEM] * 7,
+        in_specs=[VMEM] * 6,
         out_specs=(VMEM, VMEM, VMEM),
         scratch_shapes=SPLIT,
-        input_output_aliases={6: 1},
-        compiler_params=PARAMS,
-        cost_estimate=cost(5 * NK),
+        input_output_aliases={5: 1},
+        compiler_params=PARAMS,
+        cost_estimate=cost(4 * NK),
         name="attend_second",
-    )(q, other, bias, kv, low, high, acc)
-
-
-def middle_kernel(step, q_ref, q2_ref, bias_ref, low_ref, high_ref, in1, in2, acc_ref, acc2_ref, kx_ref, vx_ref):
-    both_tiles(step, bias_ref, low_ref, high_ref, kx_ref, vx_ref, ((q_ref, acc_ref), (q2_ref, acc2_ref)))
-
-
-def attend_middle(step, q, q2, bias, low, high, acc, acc2):
-    return pl.pallas_call(
-        lambda *refs: middle_kernel(step, *refs),
+    )(q, other, bias, low, high, acc)
+
+
+def third_kernel(q_ref, q2_ref, bias_ref, kv_ref, low_ref, high_ref, in1, in2, acc_ref, acc2_ref, kx_ref, vx_ref):
+    both_tiles(2, bias_ref, low_ref, high_ref, kx_ref, vx_ref, ((q_ref, acc_ref), (q2_ref, acc2_ref)))
+    tile(q2_ref, *split_kv(kv_ref[...], 0, bias_ref), add(acc2_ref))
+
+
+def attend_third(q, q2, bias, kv, low, high, acc, acc2):
+    return pl.pallas_call(
+        third_kernel,
         out_shape=(ACC, ACC),
-        in_specs=[VMEM] * 7,
+        in_specs=[VMEM] * 8,
         out_specs=(VMEM, VMEM),
         scratch_shapes=SPLIT,
-        input_output_aliases={5: 0, 6: 1},
-        compiler_params=PARAMS,
-        cost_estimate=cost(4 * NK),
-        name="attend_middle",
-    )(q, q2, bias, low, high, acc, acc2)
+        input_output_aliases={6: 0, 7: 1},
+        compiler_params=PARAMS,
+        cost_estimate=cost(5 * NK),
+        name="attend_third",
+    )(q, q2, bias, kv, low, high, acc, acc2)
+
+
+def fourth_other_kernel(q_ref, bias_ref, low_ref, high_ref, acc_in, acc_ref, kx_ref, vx_ref):
+    both_tiles(3, bias_ref, low_ref, high_ref, kx_ref, vx_ref, ((q_ref, acc_ref),))
+
+
+def attend_fourth_other(q2, bias, low, high, acc2):
+    return pl.pallas_call(
+        fourth_other_kernel,
+        out_shape=ACC,
+        in_specs=[VMEM] * 5,
+        out_specs=VMEM,
+        scratch_shapes=SPLIT,
+        input_output_aliases={4: 0},
+        compiler_params=PARAMS,
+        cost_estimate=cost(2 * NK),
+        name="attend_fourth_other",
+    )(q2, bias, low, high, acc2)
 
 
 HALF = NQ // 2
@@ -292,21 +302,23 @@
     )(q2, bias, low, high, acc2)
 
 
-def last_mine_kernel(q_ref, bias_ref, low_ref, high_ref, in_ref, acc_ref):
-    tile(q_ref, *split_last(low_ref, high_ref, bias_ref), add(acc_ref))
-
-
-def attend_last_mine(q, bias, low, high, acc):
+def last_mine_kernel(q_ref, bias_ref, low_ref, high_ref, far_low, far_high, acc_in, acc_ref, kx_ref, vx_ref):
+    both_tiles(3, bias_ref, low_ref, high_ref, kx_ref, vx_ref, ((q_ref, acc_ref),))
+    tile(q_ref, *split_last(far_low, far_high, bias_ref), add(acc_ref))
+
+
+def attend_last_mine(q, bias, low, high, far_low, far_high, acc):
     return pl.pallas_call(
         last_mine_kernel,
         out_shape=ACC,
-        in_specs=[VMEM] * 5,
+        in_specs=[VMEM] * 7,
         out_specs=VMEM,
-        input_output_aliases={4: 0},
-        compiler_params=PARAMS,
-        cost_estimate=cost(NK),
+        scratch_shapes=SPLIT,
+        input_output_aliases={6: 0},
+        compiler_params=PARAMS,
+        cost_estimate=cost(3 * NK),
         name="attend_last_mine",
-    )(q, bias, low, high, acc)
+    )(q, bias, low, high, far_low, far_high, acc)
 
 
 def finish_kernel(mine_ref, message_ref, *out_refs):
@@ -377,42 +389,40 @@
 def shards(tokens, gain, w_query, w_key, w_value, w_out, temper, adjacency, order):
     whole = lax.all_gather(tokens, HEAD, axis=1, tiled=True)
     messages = project(whole, gain[None, :], w_query, w_key, w_value, temper)
-    got = jnp.stack([messages[0]] + [lax.ppermute(messages[s], "y", ring(NY, s)) for s in range(1, NY)])
-    kv = got[:, :ROWS, :].reshape(NK, 128)
-    query = got[:, ROWS:, :]
-    query, kv = lax.optimization_barrier((query, kv))
-    low, high = lax.ppermute(kv, "z", ring(NZ, 1)), lax.ppermute(kv, "z", ring(NZ, -1))
-    other = lax.ppermute(query, "xh", [(0, 1), (1, 0)])
-    q, bias, acc = attend_first(order, adjacency, query, kv)
     xl, core = lax.axis_index("xl"), lax.axis_index("core")
+    w_out, messages = lax.optimization_barrier((w_out, messages))
     block = lambda side, turn: lax.dynamic_slice_in_dim(w_out, (2 * side + turn) * 256, 256, 1)
     own, relayed = block(xl, core), block(1 - xl, core)
     near = jnp.concatenate([block(xl, 1 - core), block(1 - xl, 1 - core)], axis=0)
-    for step in (1, 2, 3):
-        low, high, acc, near = lax.optimization_barrier((low, high, acc, near))
-        if step < 3:
-            next_low, next_high = lax.ppermute(low, "z", ring(NZ, 1)), lax.ppermute(high, "z", ring(NZ, -1))
-        else:
-            next_low = lax.ppermute(low[: NK // 2], "z", ring(NZ, 1))
-            next_high = lax.ppermute(high[NK // 2 :], "z", ring(NZ, -1))
-        if step == 1:
-            q2, acc, acc2 = attend_second(q, other, bias, kv, low, high, acc)
-        else:
-            acc, acc2 = attend_middle(step, q, q2, bias, low, high, acc, acc2)
-        low, high = next_low, next_high
-        if step == 1:
-            near = lax.ppermute(near, "core", ring(NCORE, 1))
-        if step == 2:
-            far = lax.ppermute(jnp.concatenate([relayed, near[256:]], axis=0), "xl", ring(NXL, 1))
-            near = near[:256]
-    low, high, acc, own, near, far = lax.optimization_barrier((low, high, acc, own, near, far))
-    message = attend_last_other(q2, bias, low, high, acc2)
+    near = lax.ppermute(near, "core", ring(NCORE, 1))
+    turned = {s: lax.ppermute(messages[s], "y", ring(NY, s)) for s in (2, 1, 3)}
+    got = jnp.stack([messages[0]] + [turned[s] for s in range(1, NY)])
+    kv = got[:, :ROWS, :].reshape(NK, 128)
+    query = got[:, ROWS:, :]
+    query, kv, near = lax.optimization_barrier((query, kv, near))
+    up = lambda part: lax.ppermute(part, "z", ring(NZ, 1))
+    down = lambda part: lax.ppermute(part, "z", ring(NZ, -1))
+    low, high = up(kv), down(kv)
+    other = lax.ppermute(query, "xh", ring(NXH, 1))
+    q, bias, acc = attend_first(order, adjacency, query, kv)
+    low, high, acc = lax.optimization_barrier((low, high, acc))
+    low2, high2 = up(low), down(high)
+    q2, acc, acc2 = attend_second(q, other, bias, low, high, acc)
+    low2, high2, acc, near = lax.optimization_barrier((low2, high2, acc, near))
+    low3, high3 = up(low2), down(high2)
+    far = lax.ppermute(jnp.concatenate([relayed, near[256:]], axis=0), "xl", ring(NXL, 1))
+    acc, acc2 = attend_third(q, q2, bias, kv, low2, high2, acc, acc2)
+    low3, high3, acc2 = lax.optimization_barrier((low3, high3, acc2))
+    low4, high4 = up(low3[: NK // 2]), down(high3[NK // 2 :])
+    acc2 = attend_fourth_other(q2, bias, low3, high3, acc2)
+    low4, high4, acc2, far = lax.optimization_barrier((low4, high4, acc2, far))
+    message = attend_last_other(q2, bias, low4, high4, acc2)
     message, acc = lax.optimization_barrier((message, acc))
-    message = lax.ppermute(message, "xh", [(0, 1), (1, 0)])
-    attended = finish(attend_last_mine(q, bias, low, high, acc), message)
+    message = lax.ppermute(message, "xh", ring(NXH, 1))
+    attended = finish(attend_last_mine(q, bias, low3, high3, low4, high4, acc), message)
     back = jnp.stack([attended[0]] + [lax.ppermute(attended[s], "y", ring(NY, -s)) for s in range(1, NY)])
     gathered = lax.all_gather(back, HEAD, axis=0, tiled=True)
-    return output(gathered, own, near, far)
+    return output(gathered, own, near[:256], far)
 
 
 def solution(mesh):

time: 87.8 us -> 83.4 us (0.950)
  waiting for transfers between devices: 12 us -> 7.18 us
  blocking collectives: 20.9 us -> 23.9 us
  Pallas kernels: 25.7 us -> 24.6 us
    ppermute x13, waiting for transfers between devices: 8.6 us -> 3.96 us  [the longest x3 2.72 us: shards(): turned = {s: lax.ppermute(messages[s], 'y', ring(NY, s)) for s in (2, 1, 3)}]
    all_gather x1, blocking collectives: 11.1 us -> 14.1 us  [shards(): gathered = lax.all_gather(back, HEAD, axis=0, tiled=True)]
    pallas_call x1, Pallas kernels: 6.24 us -> 4.58 us  [attend_second(): pl.pallas_call(second_kernel, out_shape=(WIDE, ACC, ACC), in_specs=[VMEM]...]
    ppermute x1, starting transfers between devices: 2.09 us -> 1.09 us  [shards(): near = lax.ppermute(near, 'core', ring(NCORE, 1))]
where the time goes in v4:
time: 83.4 us; the launch traced here: 83.2 us
  starting transfers between devices  27.1 us (32%)
  Pallas kernels  24.6 us (29%)
  blocking collectives  23.9 us (29%)
  waiting for transfers between devices  7.18 us (9%)
    all_gather x1, blocking collectives, shards(): gathered = lax.all_gather(back, HEAD, axis=0, tiled=True)  14.1 us
    ppermute x4, starting transfers between devices, shards(): down = lambda part: lax.ppermute(part, 'z', ring(NZ, -1))  11.8 us
    all_gather x1, blocking collectives, shards(): whole = lax.all_gather(tokens, HEAD, axis=1, tiled=True)  9.78 us
    pallas_call x1, Pallas kernels, attend_third(): pl.pallas_call(third_kernel, out_shape=(ACC, ACC), in_specs=[VMEM] * 8, o...  5.69 us
    pallas_call x1, Pallas kernels, attend_second(): pl.pallas_call(second_kernel, out_shape=(WIDE, ACC, ACC), in_specs=[VMEM]...  4.58 us
    ppermute x3, starting transfers between devices, shards(): turned = {s: lax.ppermute(messages[s], 'y', ring(NY, s)) for s in (2, 1, 3)}  3.99 us
    pallas_call x1, Pallas kernels, attend_last_mine(): pl.pallas_call(last_mine_kernel, out_shape=ACC, in_specs=[VMEM] * 7, out_...  3.49 us
    pallas_call x1, Pallas kernels, project(): pl.pallas_call(project_kernel, out_shape=[jax.ShapeDtypeStruct((ROWS + BL...  3.4 us
  transfers between devices with their start and end apart: 18, of which 8 were waited for; matrix products, arithmetic and copies ran while one was open for 0% of the time, Pallas kernels for 22%

profile of v4, /device:TPU:1, one launch (start us, length us, event | category | flops | bytes accessed | tf_op | source)
XLA Modules:
  0.0 83.2 jit_solution(1808749531042826176)
XLA Ops:
  0.0 9.8 %all_gather.6.x_ref = bf16[256,1024]{1,0:T(8,128)(2,1)S(1)} all-gather(bf16[256,256]{1,0:T(8,128)(2,1)} %param.9), channel_id=1, replica_groups=mesh['xh'=2,'z'=8,'y'=4,'xl'=2,'core'=2] {'xl','core'}, dimensions={1}, use_global_device_ids=true | all-gather | bytes 655360 | tf_op jit(solution)/shard_map/all_gather | solution.py:390
  9.8 3.4 %project.1 = (bf16[384,128]{1,0:T(8,128)(2,1)S(1)}, bf16[384,128]{1,0:T(8,128)(2,1)S(1)}, bf16[384,128]{1,0:T(8,128)(2,1)S(1)}, bf16[384,128]{1,0:T(8,128)(2,1)S(1)}) custom-call(bf16[256,1024]{1,0:T(8,128)(2,1)S(1)} %all_gather.6.x_ref, f32[4]{0:T(128)} %temper_hbm.1, f32[1,1024]{1,0:T(1,128)} %bitcast.26, bf16[1024,256]{1,0:T(8,128)(2,1)} %wq_hbm.1, ...), custom_call_target="tpu_custom_call" | custom-call | tf_op jit(solution)/shard_map/project/pallas_call | solution.py:73
  13.2 0.3 collective-permute-start
  13.5 2.6 %collective-permute-start.1 = (bf16[384,128]{1,0:T(8,128)(2,1)S(1)}, bf16[384,128]{1,0:T(8,128)(2,1)S(1)}, u32[]{:S(2)}, u32[]{:S(2)}) collective-permute-start(bf16[384,128]{1,0:T(8,128)(2,1)S(1)} %get-tuple-element.51), channel_id=1, source_target_pairs={{0,8},{4,12},{8,0},{12,4},{1,9},{5,13},{9,1},{13,5},{2,10},{6,14},... | collective-permute-start | bytes 294920 | tf_op jit(solution)/shard_map/ppermute | solution.py:398
  16.1 1.1 %collective-permute-start.2 = (bf16[384,128]{1,0:T(8,128)(2,1)S(1)}, bf16[384,128]{1,0:T(8,128)(2,1)S(1)}, u32[]{:S(2)}, u32[]{:S(2)}) collective-permute-start(bf16[384,128]{1,0:T(8,128)(2,1)S(1)} %get-tuple-element.52), channel_id=1, source_target_pairs={{0,12},{4,0},{8,4},{12,8},{1,13},{5,1},{9,5},{13,9},{2,14},{6,2},{... | collective-permute-start | bytes 294920 | tf_op jit(solution)/shard_map/ppermute | solution.py:398
  17.3 1.1 %collective-permute-start.3 = (bf16[512,256]{1,0:T(8,128)(2,1)S(1)}, bf16[512,256]{1,0:T(8,128)(2,1)S(1)}, u32[]{:S(2)}, u32[]{:S(2)}) collective-permute-start(bf16[512,256]{1,0:T(8,128)(2,1)S(1)} %pad_maximum_fusion.3), channel_id=1, source_target_pairs={{0,1},{1,0},{2,3},{3,2},{4,5},{5,4},{6,7},{7,6},{8,9},{9,8},{10,11... | collective-permute-start | bytes 786440 | tf_op jit(solution)/shard_map/ppermute | solution.py:397
  18.4 0.4 collective-permute-done
  18.7 2.3 %collective-permute-done.1 = bf16[384,128]{1,0:T(8,128)(2,1)S(1)} collective-permute-done((bf16[384,128]{1,0:T(8,128)(2,1)S(1)}, bf16[384,128]{1,0:T(8,128)(2,1)S(1)}, u32[]{:S(2)}, u32[]{:S(2)}) %collective-permute-start.1) | collective-permute-done | bytes 98336 | tf_op jit(solution)/shard_map/ppermute | solution.py:398
  21.2 1.6 %collective-permute-start.4 = (bf16[1024,128]{1,0:T(8,128)(2,1)S(1)}, bf16[1024,128]{1,0:T(8,128)(2,1)S(1)}, u32[]{:S(2)}, u32[]{:S(2)}) collective-permute-start(bf16[1024,128]{1,0:T(8,128)(2,1)S(1)} %bitcast.12), channel_id=1, source_target_pairs={{0,16},{16,32},{32,48},{48,64},{64,80},{80,96},{96,112},{112,0},{1... | collective-permute-start | bytes 786440 | tf_op jit(solution)/shard_map/ppermute | solution.py:403
  22.8 4.0 %collective-permute-start.5 = (bf16[1024,128]{1,0:T(8,128)(2,1)S(1)}, bf16[1024,128]{1,0:T(8,128)(2,1)S(1)}, u32[]{:S(2)}, u32[]{:S(2)}) collective-permute-start(bf16[1024,128]{1,0:T(8,128)(2,1)S(1)} %bitcast.13), channel_id=1, source_target_pairs={{0,112},{16,0},{32,16},{48,32},{64,48},{80,64},{96,80},{112,96},{1... | collective-permute-start | bytes 786440 | tf_op jit(solution)/shard_map/ppermute | solution.py:404
  26.8 2.5 %collective-permute-start.8 = (bf16[4,128,128]{2,1,0:T(8,128)(2,1)S(1)}, bf16[4,128,128]{2,1,0:T(8,128)(2,1)S(1)}, u32[]{:S(2)}, u32[]{:S(2)}) collective-permute-start(bf16[4,128,128]{2,1,0:T(8,128)(2,1)S(1)} %pad_maximum_fusion.5.mine_ref), channel_id=1, source_target_pairs={{0,128},{128,0},{1,129},{129,1},{2,130},{130,2},{3,131},{131,3},{4... | collective-permute-start | bytes 393224 | tf_op jit(solution)/shard_map/ppermute | solution.py:406
  29.3 2.1 %attend_first.1 = (bf16[1024,128]{1,0:T(8,128)(2,1)S(1)}, f32[8,8,128]{2,1,0:T(8,128)S(1)}, f32[1024,128]{1,0:T(8,128)S(1)}) custom-call(s32[128]{0:T(128)S(1)} %copy-done.1, s32[128,128]{1,0:T(8,128)S(1)} %copy-done, bf16[4,128,128]{2,1,0:T(8,128)(2,1)S(1)} %pad_maximum_fusion.5.mine_ref, bf16[1024,128]{1,0:T(8,128)(2,1)S(1)} %bitcast.14), custom_call_target="tpu_custom_call" | custom-call | flops 536870912 | bytes 4194304 | tf_op jit(solution)/shard_map/attend_first/pallas_call | solution.py:184
  31.4 1.0 %collective-permute-done.4.low_ref = bf16[1024,128]{1,0:T(8,128)(2,1)S(1)} collective-permute-done((bf16[1024,128]{1,0:T(8,128)(2,1)S(1)}, bf16[1024,128]{1,0:T(8,128)(2,1)S(1)}, u32[]{:S(2)}, u32[]{:S(2)}) %collective-permute-start.4) | collective-permute-done | bytes 262176 | tf_op jit(solution)/shard_map/ppermute | solution.py:403
  32.4 2.7 %collective-permute-start.7 = (bf16[1024,128]{1,0:T(8,128)(2,1)S(1)}, bf16[1024,128]{1,0:T(8,128)(2,1)S(1)}, u32[]{:S(2)}, u32[]{:S(2)}) collective-permute-start(bf16[1024,128]{1,0:T(8,128)(2,1)S(1)} %collective-permute-done.5.high_ref), channel_id=1, source_target_pairs={{0,112},{16,0},{32,16},{48,32},{64,48},{80,64},{96,80},{112,96},{1... | collective-permute-start | bytes 786440 | tf_op jit(solution)/shard_map/ppermute | solution.py:404
  35.1 4.6 %attend_second.1 = (bf16[1024,128]{1,0:T(8,128)(2,1)S(1)}, f32[1024,128]{1,0:T(8,128)S(1)}, f32[1024,128]{1,0:T(8,128)S(1)}) custom-call(bf16[1024,128]{1,0:T(8,128)(2,1)S(1)} %get-tuple-element.56.q_ref, bf16[4,128,128]{2,1,0:T(8,128)(2,1)S(1)} %collective-permute-done.8.other_ref, ...), custom_call_target="tpu_custom_call", output_to_operand_aliasing={{1}: (5, {})} | custom-call | flops 2147483648 | bytes 4194304 | tf_op jit(solution)/shard_map/attend_second/pallas_call | solution.py:213
  39.9 2.4 %collective-permute-start.10 = (bf16[1024,128]{1,0:T(8,128)(2,1)S(1)}, bf16[1024,128]{1,0:T(8,128)(2,1)S(1)}, u32[]{:S(2)}, u32[]{:S(2)}) collective-permute-start(bf16[1024,128]{1,0:T(8,128)(2,1)S(1)} %collective-permute-done.7.high_ref), channel_id=1, source_target_pairs={{0,112},{16,0},{32,16},{48,32},{64,48},{80,64},{96,80},{112,96},{1... | collective-permute-start | bytes 786440 | tf_op jit(solution)/shard_map/ppermute | solution.py:404
  42.3 1.1 %collective-permute-start.13 = (bf16[512,256]{1,0:T(8,128)(2,1)S(1)}, bf16[512,256]{1,0:T(8,128)(2,1)S(1)}, u32[]{:S(2)}, u32[]{:S(2)}) collective-permute-start(bf16[512,256]{1,0:T(8,128)(2,1)S(1)} %pad_maximum_fusion.4), channel_id=1, source_target_pairs={{0,2},{2,0},{1,3},{3,1},{4,6},{6,4},{5,7},{7,5},{8,10},{10,8},{9,1... | collective-permute-start | bytes 786440 | tf_op jit(solution)/shard_map/ppermute | solution.py:413
  43.5 5.7 %attend_third.1 = (f32[1024,128]{1,0:T(8,128)S(1)}, f32[1024,128]{1,0:T(8,128)S(1)}) custom-call(bf16[1024,128]{1,0:T(8,128)(2,1)S(1)} %get-tuple-element.56.q_ref, bf16[1024,128]{1,0:T(8,128)(2,1)S(1)} %get-tuple-element.66.q2_ref.q_ref, f32[8,8,128]{2,1,0:T(8,128)S(1)} %get-tuple-element.57.bias_ref, ...), custom_call_target="tpu_custom_call", output_to_operand_aliasing={{0}: (6, {}), {1}: (7, {})} | custom-call | flops 2684354560 | bytes 4194304 | tf_op jit(solution)/shard_map/attend_third/pallas_call | solution.py:232
  49.3 2.7 %collective-permute-start.12 = (bf16[512,128]{1,0:T(8,128)(2,1)S(1)}, bf16[512,128]{1,0:T(8,128)(2,1)S(1)}, u32[]{:S(2)}, u32[]{:S(2)}) collective-permute-start(bf16[512,128]{1,0:T(8,128)(2,1)S(1)} %slice.21), channel_id=1, source_target_pairs={{0,112},{16,0},{32,16},{48,32},{64,48},{80,64},{96,80},{112,96},{1... | collective-permute-start | bytes 393224 | tf_op jit(solution)/shard_map/ppermute | solution.py:404
  52.1 2.4 %attend_fourth_other.1.in_ref = f32[1024,128]{1,0:T(8,128)S(1)} custom-call(bf16[1024,128]{1,0:T(8,128)(2,1)S(1)} %get-tuple-element.66.q2_ref.q_ref, f32[8,8,128]{2,1,0:T(8,128)S(1)} %get-tuple-element.57.bias_ref, bf16[1024,128]{1,0:T(8,128)(2,1)S(1)} %collective-permute-done.9.low_ref, ...), custom_call_target="tpu_custom_call", output_to_operand_aliasing={{}: (4, {})} | custom-call | flops 1073741824 | bytes 4194304 | tf_op jit(solution)/shard_map/attend_fourth_other/pallas_call | solution.py:250
  54.5 1.5 %attend_last_other.1 = bf16[528,128]{1,0:T(8,128)(2,1)S(1)} custom-call(bf16[1024,128]{1,0:T(8,128)(2,1)S(1)} %get-tuple-element.66.q2_ref.q_ref, f32[8,8,128]{2,1,0:T(8,128)S(1)} %get-tuple-element.57.bias_ref, bf16[512,128]{1,0:T(8,128)(2,1)S(1)} %collective-permute-done.11.low_ref.far_low, bf16[512,128]{1,0:T(8,128)(2,1)S(1)} %collective-permute-done.12.high_ref.far_high, ...), custom_call_target="tpu_custom_call" | custom-call | flops 536870912 | bytes 4194304 | tf_op jit(solution)/shard_map/attend_last_other/pallas_call | solution.py:293
  56.0 2.7 %collective-permute-start.14 = (bf16[528,128]{1,0:T(8,128)(2,1)S(1)}, bf16[528,128]{1,0:T(8,128)(2,1)S(1)}, u32[]{:S(2)}, u32[]{:S(2)}) collective-permute-start(bf16[528,128]{1,0:T(8,128)(2,1)S(1)} %attend_last_other.1), channel_id=1, source_target_pairs={{0,128},{128,0},{1,129},{129,1},{2,130},{130,2},{3,131},{131,3},{4... | collective-permute-start | bytes 405512 | tf_op jit(solution)/shard_map/ppermute | solution.py:421
  58.7 3.5 %attend_last_mine.1.mine_ref = f32[1024,128]{1,0:T(8,128)S(1)} custom-call(bf16[1024,128]{1,0:T(8,128)(2,1)S(1)} %get-tuple-element.56.q_ref, f32[8,8,128]{2,1,0:T(8,128)S(1)} %get-tuple-element.57.bias_ref, bf16[1024,128]{1,0:T(8,128)(2,1)S(1)} %collective-permute-done.9.low_ref, ...), custom_call_target="tpu_custom_call", output_to_operand_aliasing={{}: (6, {})} | custom-call | flops 1610612736 | bytes 4194304 | tf_op jit(solution)/shard_map/attend_last_mine/pallas_call | solution.py:311
  62.3 0.3 finish.1
  62.5 0.7 collective-permute-start.15
  63.2 0.7 collective-permute-start.16
  64.0 0.8 collective-permute-start.17
  64.7 1.0 %collective-permute-done.15 = bf16[128,128]{1,0:T(8,128)(2,1)S(1)} collective-permute-done((bf16[128,128]{1,0:T(8,128)(2,1)S(1)}, bf16[128,128]{1,0:T(8,128)(2,1)S(1)}, u32[]{:S(2)}, u32[]{:S(2)}) %collective-permute-start.15) | collective-permute-done | bytes 32800 | tf_op jit(solution)/shard_map/ppermute | solution.py:423
  65.7 1.8 %collective-permute-done.16 = bf16[128,128]{1,0:T(8,128)(2,1)S(1)} collective-permute-done((bf16[128,128]{1,0:T(8,128)(2,1)S(1)}, bf16[128,128]{1,0:T(8,128)(2,1)S(1)}, u32[]{:S(2)}, u32[]{:S(2)}) %collective-permute-start.16) | collective-permute-done | bytes 32800 | tf_op jit(solution)/shard_map/ppermute | solution.py:423
  67.5 0.4 collective-permute-done.17
  68.0 14.1 %all_gather.7.a_ref = bf16[16,128,128]{2,1,0:T(8,128)(2,1)S(1)} all-gather(bf16[4,128,128]{2,1,0:T(8,128)(2,1)S(1)} %pad_maximum_fusion.6), channel_id=1, replica_groups=mesh['xh'=2,'z'=8,'y'=4,'xl'=2,'core'=2] {'xl','core'}, dimensions={0}, use_global_device_ids=true | all-gather | bytes 655360 | tf_op jit(solution)/shard_map/all_gather | solution.py:424
  82.1 1.1 %output.1 = bf16[256,256]{1,0:T(8,128)(2,1)} custom-call(bf16[16,128,128]{2,1,0:T(8,128)(2,1)S(1)} %all_gather.7.a_ref, bf16[256,256]{1,0:T(8,128)(2,1)S(1)} %get-tuple-element.85.own_ref, bf16[256,256]{1,0:T(8,128)(2,1)S(1)} %get-tuple-element.89.near_ref, bf16[512,256]{1,0:T(8,128)(2,1)S(1)} %collective-permute-done.13.far_ref), custom_call_target="tpu_custom_call" | custom-call | tf_op jit(solution)/shard_map/output/pallas_call | solution.py:378
  (30 shorter events, 0.6 us)
Async XLA Ops:
  9.8 7.4 %copy-start.2 = (bf16[256,1024]{1,0:T(8,128)(2,1)S(1)}, bf16[256,1024]{1,0:T(8,128)(2,1)}, u32[]{:S(2)}) copy-start(bf16[256,1024]{1,0:T(8,128)(2,1)} %param.14) | copy-start | bytes 1572868
  13.2 5.5 %collective-permute-start = (bf16[384,128]{1,0:T(8,128)(2,1)S(1)}, bf16[384,128]{1,0:T(8,128)(2,1)S(1)}, u32[]{:S(2)}, u32[]{:S(2)}) collective-permute-start(bf16[384,128]{1,0:T(8,128)(2,1)S(1)} %get-tuple-element.50), channel_id=1, source_target_pairs={{0,4},{4,8},{8,12},{12,0},{1,5},{5,9},{9,13},{13,1},{2,6},{6,10},{... | collective-permute-start | bytes 294920 | tf_op jit(solution)/shard_map/ppermute | solution.py:398
  13.5 7.5 %collective-permute-start.1 = (bf16[384,128]{1,0:T(8,128)(2,1)S(1)}, bf16[384,128]{1,0:T(8,128)(2,1)S(1)}, u32[]{:S(2)}, u32[]{:S(2)}) collective-permute-start(bf16[384,128]{1,0:T(8,128)(2,1)S(1)} %get-tuple-element.51), channel_id=1, source_target_pairs={{0,8},{4,12},{8,0},{12,4},{1,9},{5,13},{9,1},{13,5},{2,10},{6,14},... | collective-permute-start | bytes 294920 | tf_op jit(solution)/shard_map/ppermute | solution.py:398
  16.1 5.0 %collective-permute-start.2 = (bf16[384,128]{1,0:T(8,128)(2,1)S(1)}, bf16[384,128]{1,0:T(8,128)(2,1)S(1)}, u32[]{:S(2)}, u32[]{:S(2)}) collective-permute-start(bf16[384,128]{1,0:T(8,128)(2,1)S(1)} %get-tuple-element.52), channel_id=1, source_target_pairs={{0,12},{4,0},{8,4},{12,8},{1,13},{5,1},{9,5},{13,9},{2,14},{6,2},{... | collective-permute-start | bytes 294920 | tf_op jit(solution)/shard_map/ppermute | solution.py:398
  17.3 3.9 %collective-permute-start.3 = (bf16[512,256]{1,0:T(8,128)(2,1)S(1)}, bf16[512,256]{1,0:T(8,128)(2,1)S(1)}, u32[]{:S(2)}, u32[]{:S(2)}) collective-permute-start(bf16[512,256]{1,0:T(8,128)(2,1)S(1)} %pad_maximum_fusion.3), channel_id=1, source_target_pairs={{0,1},{1,0},{2,3},{3,2},{4,5},{5,4},{6,7},{7,6},{8,9},{9,8},{10,11... | collective-permute-start | bytes 786440 | tf_op jit(solution)/shard_map/ppermute | solution.py:397
  21.1 8.2 %copy-start = (s32[128,128]{1,0:T(8,128)S(1)}, s32[128,128]{1,0:T(8,128)}, u32[]{:S(2)}) copy-start(s32[128,128]{1,0:T(8,128)} %adjacency_ref.1) | copy-start | bytes 196612
  21.1 8.1 %copy-start.1 = (s32[128]{0:T(128)S(1)}, s32[128]{0:T(128)}, u32[]{:S(2)}) copy-start(s32[128]{0:T(128)} %order_ref.1) | copy-start | bytes 1540
  21.2 11.3 %collective-permute-start.4 = (bf16[1024,128]{1,0:T(8,128)(2,1)S(1)}, bf16[1024,128]{1,0:T(8,128)(2,1)S(1)}, u32[]{:S(2)}, u32[]{:S(2)}) collective-permute-start(bf16[1024,128]{1,0:T(8,128)(2,1)S(1)} %bitcast.12), channel_id=1, source_target_pairs={{0,16},{16,32},{32,48},{48,64},{64,80},{80,96},{96,112},{112,0},{1... | collective-permute-start | bytes 786440 | tf_op jit(solution)/shard_map/ppermute | solution.py:403
  22.8 9.6 %collective-permute-start.5 = (bf16[1024,128]{1,0:T(8,128)(2,1)S(1)}, bf16[1024,128]{1,0:T(8,128)(2,1)S(1)}, u32[]{:S(2)}, u32[]{:S(2)}) collective-permute-start(bf16[1024,128]{1,0:T(8,128)(2,1)S(1)} %bitcast.13), channel_id=1, source_target_pairs={{0,112},{16,0},{32,16},{48,32},{64,48},{80,64},{96,80},{112,96},{1... | collective-permute-start | bytes 786440 | tf_op jit(solution)/shard_map/ppermute | solution.py:404
  26.8 8.3 %collective-permute-start.8 = (bf16[4,128,128]{2,1,0:T(8,128)(2,1)S(1)}, bf16[4,128,128]{2,1,0:T(8,128)(2,1)S(1)}, u32[]{:S(2)}, u32[]{:S(2)}) collective-permute-start(bf16[4,128,128]{2,1,0:T(8,128)(2,1)S(1)} %pad_maximum_fusion.5.mine_ref), channel_id=1, source_target_pairs={{0,128},{128,0},{1,129},{129,1},{2,130},{130,2},{3,131},{131,3},{4... | collective-permute-start | bytes 393224 | tf_op jit(solution)/shard_map/ppermute | solution.py:406
  32.4 7.5 %collective-permute-start.6 = (bf16[1024,128]{1,0:T(8,128)(2,1)S(1)}, bf16[1024,128]{1,0:T(8,128)(2,1)S(1)}, u32[]{:S(2)}, u32[]{:S(2)}) collective-permute-start(bf16[1024,128]{1,0:T(8,128)(2,1)S(1)} %collective-permute-done.4.low_ref), channel_id=1, source_target_pairs={{0,16},{16,32},{32,48},{48,64},{64,80},{80,96},{96,112},{112,0},{1... | collective-permute-start | bytes 786440 | tf_op jit(solution)/shard_map/ppermute | solution.py:403
  32.4 7.5 %collective-permute-start.7 = (bf16[1024,128]{1,0:T(8,128)(2,1)S(1)}, bf16[1024,128]{1,0:T(8,128)(2,1)S(1)}, u32[]{:S(2)}, u32[]{:S(2)}) collective-permute-start(bf16[1024,128]{1,0:T(8,128)(2,1)S(1)} %collective-permute-done.5.high_ref), channel_id=1, source_target_pairs={{0,112},{16,0},{32,16},{48,32},{64,48},{80,64},{96,80},{112,96},{1... | collective-permute-start | bytes 786440 | tf_op jit(solution)/shard_map/ppermute | solution.py:404
  39.9 9.3 %collective-permute-start.10 = (bf16[1024,128]{1,0:T(8,128)(2,1)S(1)}, bf16[1024,128]{1,0:T(8,128)(2,1)S(1)}, u32[]{:S(2)}, u32[]{:S(2)}) collective-permute-start(bf16[1024,128]{1,0:T(8,128)(2,1)S(1)} %collective-permute-done.7.high_ref), channel_id=1, source_target_pairs={{0,112},{16,0},{32,16},{48,32},{64,48},{80,64},{96,80},{112,96},{1... | collective-permute-start | bytes 786440 | tf_op jit(solution)/shard_map/ppermute | solution.py:404
  42.3 6.9 %collective-permute-start.9 = (bf16[1024,128]{1,0:T(8,128)(2,1)S(1)}, bf16[1024,128]{1,0:T(8,128)(2,1)S(1)}, u32[]{:S(2)}, u32[]{:S(2)}) collective-permute-start(bf16[1024,128]{1,0:T(8,128)(2,1)S(1)} %collective-permute-done.6.low_ref), channel_id=1, source_target_pairs={{0,16},{16,32},{32,48},{48,64},{64,80},{80,96},{96,112},{112,0},{1... | collective-permute-start | bytes 786440 | tf_op jit(solution)/shard_map/ppermute | solution.py:403
  42.3 12.1 %collective-permute-start.13 = (bf16[512,256]{1,0:T(8,128)(2,1)S(1)}, bf16[512,256]{1,0:T(8,128)(2,1)S(1)}, u32[]{:S(2)}, u32[]{:S(2)}) collective-permute-start(bf16[512,256]{1,0:T(8,128)(2,1)S(1)} %pad_maximum_fusion.4), channel_id=1, source_target_pairs={{0,2},{2,0},{1,3},{3,1},{4,6},{6,4},{5,7},{7,5},{8,10},{10,8},{9,1... | collective-permute-start | bytes 786440 | tf_op jit(solution)/shard_map/ppermute | solution.py:413
  49.2 5.3 %collective-permute-start.11 = (bf16[512,128]{1,0:T(8,128)(2,1)S(1)}, bf16[512,128]{1,0:T(8,128)(2,1)S(1)}, u32[]{:S(2)}, u32[]{:S(2)}) collective-permute-start(bf16[512,128]{1,0:T(8,128)(2,1)S(1)} %slice.20), channel_id=1, source_target_pairs={{0,16},{16,32},{32,48},{48,64},{64,80},{80,96},{96,112},{112,0},{1... | collective-permute-start | bytes 393224 | tf_op jit(solution)/shard_map/ppermute | solution.py:403
  49.3 5.2 %collective-permute-start.12 = (bf16[512,128]{1,0:T(8,128)(2,1)S(1)}, bf16[512,128]{1,0:T(8,128)(2,1)S(1)}, u32[]{:S(2)}, u32[]{:S(2)}) collective-permute-start(bf16[512,128]{1,0:T(8,128)(2,1)S(1)} %slice.21), channel_id=1, source_target_pairs={{0,112},{16,0},{32,16},{48,32},{64,48},{80,64},{96,80},{112,96},{1... | collective-permute-start | bytes 393224 | tf_op jit(solution)/shard_map/ppermute | solution.py:404
  56.0 6.2 %collective-permute-start.14 = (bf16[528,128]{1,0:T(8,128)(2,1)S(1)}, bf16[528,128]{1,0:T(8,128)(2,1)S(1)}, u32[]{:S(2)}, u32[]{:S(2)}) collective-permute-start(bf16[528,128]{1,0:T(8,128)(2,1)S(1)} %attend_last_other.1), channel_id=1, source_target_pairs={{0,128},{128,0},{1,129},{129,1},{2,130},{130,2},{3,131},{131,3},{4... | collective-permute-start | bytes 405512 | tf_op jit(solution)/shard_map/ppermute | solution.py:421
  62.5 3.1 %collective-permute-start.15 = (bf16[128,128]{1,0:T(8,128)(2,1)S(1)}, bf16[128,128]{1,0:T(8,128)(2,1)S(1)}, u32[]{:S(2)}, u32[]{:S(2)}) collective-permute-start(bf16[128,128]{1,0:T(8,128)(2,1)S(1)} %get-tuple-element.81), channel_id=1, source_target_pairs={{0,12},{4,0},{8,4},{12,8},{1,13},{5,1},{9,5},{13,9},{2,14},{6,2},{... | collective-permute-start | bytes 98312 | tf_op jit(solution)/shard_map/ppermute | solution.py:423
  63.2 4.3 %collective-permute-start.16 = (bf16[128,128]{1,0:T(8,128)(2,1)S(1)}, bf16[128,128]{1,0:T(8,128)(2,1)S(1)}, u32[]{:S(2)}, u32[]{:S(2)}) collective-permute-start(bf16[128,128]{1,0:T(8,128)(2,1)S(1)} %get-tuple-element.82), channel_id=1, source_target_pairs={{0,8},{4,12},{8,0},{12,4},{1,9},{5,13},{9,1},{13,5},{2,10},{6,14},... | collective-permute-start | bytes 98312 | tf_op jit(solution)/shard_map/ppermute | solution.py:423
  64.0 4.0 %collective-permute-start.17 = (bf16[128,128]{1,0:T(8,128)(2,1)S(1)}, bf16[128,128]{1,0:T(8,128)(2,1)S(1)}, u32[]{:S(2)}, u32[]{:S(2)}) collective-permute-start(bf16[128,128]{1,0:T(8,128)(2,1)S(1)} %get-tuple-element.83), channel_id=1, source_target_pairs={{0,4},{4,8},{8,12},{12,0},{1,5},{5,9},{9,13},{13,1},{2,6},{6,10},{... | collective-permute-start | bytes 98312 | tf_op jit(solution)/shard_map/ppermute | solution.py:423

commit v5 on v4

--- a/solution.py
+++ b/solution.py
@@ -53,16 +53,28 @@
 
     copies[4].wait()
 
-    def unit(part):
-        return part * lax.rsqrt(jnp.mean(part * part, axis=-1, keepdims=True) + EPS)
-
-    for j in range(4):
-        cols = slice(HD * j, HD * (j + 1))
-        q = unit(query[:, cols]) * (temper_ref[j] * (LOG2E / HD))
+    lower = lax.broadcasted_iota(jnp.int32, (ROWS, 128), 1) < HD
+    head = lower[:BLOCK]
+
+    def unit(pair, first=1.0, second=1.0):
+        square = pair * pair
+        low = jnp.sum(jnp.where(lower, square, 0.0), axis=-1, keepdims=True)
+        high = jnp.sum(jnp.where(lower, 0.0, square), axis=-1, keepdims=True)
+        low = lax.rsqrt(low / HD + EPS) * first
+        high = lax.rsqrt(high / HD + EPS) * second
+        return pair * jnp.where(lower, low, high)
+
+    for n in range(2):
+        j = 2 * n
+        cols = slice(128 * n, 128 * (n + 1))
+        q = unit(query[:, cols], temper_ref[j] * (LOG2E / HD), temper_ref[j + 1] * (LOG2E / HD))
         k = unit(keys[:, cols])
         v = values[:, cols]
-        stage_ref[j, :ROWS, :] = jnp.concatenate([k, v], axis=1).astype(BF16)
-        stage_ref[j, ROWS:, :] = jnp.concatenate([q[:BLOCK], q[BLOCK:]], axis=1).astype(BF16)
+        stage_ref[j, :ROWS, :] = jnp.where(lower, k, pltpu.roll(v, 64, 1)).astype(BF16)
+        stage_ref[j + 1, :ROWS, :] = jnp.where(lower, pltpu.roll(k, 64, 1), v).astype(BF16)
+        one, two = q[:BLOCK], q[BLOCK:]
+        stage_ref[j, ROWS:, :] = jnp.where(head, one, pltpu.roll(two, 64, 1)).astype(BF16)
+        stage_ref[j + 1, ROWS:, :] = jnp.where(head, pltpu.roll(one, 64, 1), two).astype(BF16)
     y = lax.axis_index("y").astype(jnp.int32)
     for s in range(NY):
         out_refs[s][...] = stage_ref[lax.rem(y + s, NY)]
@@ -359,19 +371,17 @@
     ):
         w_ref[pl.ds(pl.multiple_of((2 * side + turn) * 256, 256), 256), :] = piece
     lane = lax.broadcasted_iota(jnp.int32, (BLOCK, 128), 1)
-    lefts, rights, weights = [], [], []
+    tops, bottoms, weights = [], [], []
     for source in range(4):
-        for s in range(4):
-            pair = a_ref[4 * source + s].astype(F32)
-            lefts.append(jnp.where(lane < HD, pair, 0.0).astype(BF16))
-            rights.append(jnp.where(lane < HD, 0.0, pair).astype(BF16))
-            j = lax.rem(y + s, NY)
-            row = pl.multiple_of(source * 256 + j * HD, HD)
-            w = w_ref[pl.ds(row, HD), :]
-            weights += [w, w]
-    w = jnp.concatenate(weights, axis=0)
-    out_ref[:BLOCK, :] = jnp.dot(jnp.concatenate(lefts, axis=1), w, preferred_element_type=F32).astype(BF16)
-    out_ref[BLOCK:, :] = jnp.dot(jnp.concatenate(rights, axis=1), w, preferred_element_type=F32).astype(BF16)
+        for s in range(0, NY, 2):
+            one, two = a_ref[4 * source + s].astype(F32), a_ref[4 * source + s + 1].astype(F32)
+            tops.append(jnp.where(lane < HD, one, pltpu.roll(two, 64, 1)).astype(BF16))
+            bottoms.append(jnp.where(lane < HD, pltpu.roll(one, 64, 1), two).astype(BF16))
+            for at in (s, s + 1):
+                row = source * 256 + lax.rem(y + at, NY) * HD
+                weights.append(w_ref[pl.ds(pl.multiple_of(row, HD), HD), :])
+    features = jnp.concatenate([jnp.concatenate(tops, axis=1), jnp.concatenate(bottoms, axis=1)], axis=0)
+    out_ref[...] = jnp.dot(features, jnp.concatenate(weights, axis=0), preferred_element_type=F32).astype(BF16)
 
 
 def output(attended, own, near, far):

time: 83.4 us -> 82.9 us (level)
  no operation moved by 1% of the time
where the time goes in v5:
time: 82.9 us; the launch traced here: 82.8 us
  starting transfers between devices  27.1 us (33%)
  Pallas kernels  24.1 us (29%)
  blocking collectives  23.9 us (29%)
  waiting for transfers between devices  7.18 us (9%)
    all_gather x1, blocking collectives, shards(): gathered = lax.all_gather(back, HEAD, axis=0, tiled=True)  14.1 us
    ppermute x4, starting transfers between devices, shards(): down = lambda part: lax.ppermute(part, 'z', ring(NZ, -1))  11.8 us
    all_gather x1, blocking collectives, shards(): whole = lax.all_gather(tokens, HEAD, axis=1, tiled=True)  9.78 us
    pallas_call x1, Pallas kernels, attend_third(): pl.pallas_call(third_kernel, out_shape=(ACC, ACC), in_specs=[VMEM] * 8, o...  5.69 us
    pallas_call x1, Pallas kernels, attend_second(): pl.pallas_call(second_kernel, out_shape=(WIDE, ACC, ACC), in_specs=[VMEM]...  4.58 us
    ppermute x3, starting transfers between devices, shards(): turned = {s: lax.ppermute(messages[s], 'y', ring(NY, s)) for s in (2, 1, 3)}  3.99 us
    pallas_call x1, Pallas kernels, attend_last_mine(): pl.pallas_call(last_mine_kernel, out_shape=ACC, in_specs=[VMEM] * 7, out_...  3.49 us
    ppermute x3, waiting for transfers between devices, shards(): lax.ppermute(attended[s], 'y', ring(NY, -s))  3.21 us
  transfers between devices with their start and end apart: 18, of which 8 were waited for; matrix products, arithmetic and copies ran while one was open for 0% of the time, Pallas kernels for 22%

profile of v5, /device:TPU:1, one launch (start us, length us, event | category | flops | bytes accessed | tf_op | source)
XLA Modules:
  0.0 82.8 jit_solution(14606811283929623915)
XLA Ops:
  0.0 9.8 %all_gather.6.x_ref = bf16[256,1024]{1,0:T(8,128)(2,1)S(1)} all-gather(bf16[256,256]{1,0:T(8,128)(2,1)} %param.9), channel_id=1, replica_groups=mesh['xh'=2,'z'=8,'y'=4,'xl'=2,'core'=2] {'xl','core'}, dimensions={1}, use_global_device_ids=true | all-gather | bytes 655360 | tf_op jit(solution)/shard_map/all_gather | solution.py:400
  9.8 3.0 %project.1 = (bf16[384,128]{1,0:T(8,128)(2,1)S(1)}, bf16[384,128]{1,0:T(8,128)(2,1)S(1)}, bf16[384,128]{1,0:T(8,128)(2,1)S(1)}, bf16[384,128]{1,0:T(8,128)(2,1)S(1)}) custom-call(bf16[256,1024]{1,0:T(8,128)(2,1)S(1)} %all_gather.6.x_ref, f32[4]{0:T(128)} %temper_hbm.1, f32[1,1024]{1,0:T(1,128)} %bitcast.26, bf16[1024,256]{1,0:T(8,128)(2,1)} %wq_hbm.1, ...), custom_call_target="tpu_custom_call" | custom-call | tf_op jit(solution)/shard_map/project/pallas_call | solution.py:85
  12.8 0.3 collective-permute-start
  13.1 2.6 %collective-permute-start.1 = (bf16[384,128]{1,0:T(8,128)(2,1)S(1)}, bf16[384,128]{1,0:T(8,128)(2,1)S(1)}, u32[]{:S(2)}, u32[]{:S(2)}) collective-permute-start(bf16[384,128]{1,0:T(8,128)(2,1)S(1)} %get-tuple-element.51), channel_id=1, source_target_pairs={{0,8},{4,12},{8,0},{12,4},{1,9},{5,13},{9,1},{13,5},{2,10},{6,14},... | collective-permute-start | bytes 294920 | tf_op jit(solution)/shard_map/ppermute | solution.py:408
  15.7 1.1 %collective-permute-start.2 = (bf16[384,128]{1,0:T(8,128)(2,1)S(1)}, bf16[384,128]{1,0:T(8,128)(2,1)S(1)}, u32[]{:S(2)}, u32[]{:S(2)}) collective-permute-start(bf16[384,128]{1,0:T(8,128)(2,1)S(1)} %get-tuple-element.52), channel_id=1, source_target_pairs={{0,12},{4,0},{8,4},{12,8},{1,13},{5,1},{9,5},{13,9},{2,14},{6,2},{... | collective-permute-start | bytes 294920 | tf_op jit(solution)/shard_map/ppermute | solution.py:408
  16.9 1.1 %collective-permute-start.3 = (bf16[512,256]{1,0:T(8,128)(2,1)S(1)}, bf16[512,256]{1,0:T(8,128)(2,1)S(1)}, u32[]{:S(2)}, u32[]{:S(2)}) collective-permute-start(bf16[512,256]{1,0:T(8,128)(2,1)S(1)} %pad_maximum_fusion.3), channel_id=1, source_target_pairs={{0,1},{1,0},{2,3},{3,2},{4,5},{5,4},{6,7},{7,6},{8,9},{9,8},{10,11... | collective-permute-start | bytes 786440 | tf_op jit(solution)/shard_map/ppermute | solution.py:407
  18.0 0.4 collective-permute-done
  18.3 2.3 %collective-permute-done.1 = bf16[384,128]{1,0:T(8,128)(2,1)S(1)} collective-permute-done((bf16[384,128]{1,0:T(8,128)(2,1)S(1)}, bf16[384,128]{1,0:T(8,128)(2,1)S(1)}, u32[]{:S(2)}, u32[]{:S(2)}) %collective-permute-start.1) | collective-permute-done | bytes 98336 | tf_op jit(solution)/shard_map/ppermute | solution.py:408
  20.8 1.6 %collective-permute-start.4 = (bf16[1024,128]{1,0:T(8,128)(2,1)S(1)}, bf16[1024,128]{1,0:T(8,128)(2,1)S(1)}, u32[]{:S(2)}, u32[]{:S(2)}) collective-permute-start(bf16[1024,128]{1,0:T(8,128)(2,1)S(1)} %bitcast.12), channel_id=1, source_target_pairs={{0,16},{16,32},{32,48},{48,64},{64,80},{80,96},{96,112},{112,0},{1... | collective-permute-start | bytes 786440 | tf_op jit(solution)/shard_map/ppermute | solution.py:413
  22.4 4.0 %collective-permute-start.5 = (bf16[1024,128]{1,0:T(8,128)(2,1)S(1)}, bf16[1024,128]{1,0:T(8,128)(2,1)S(1)}, u32[]{:S(2)}, u32[]{:S(2)}) collective-permute-start(bf16[1024,128]{1,0:T(8,128)(2,1)S(1)} %bitcast.13), channel_id=1, source_target_pairs={{0,112},{16,0},{32,16},{48,32},{64,48},{80,64},{96,80},{112,96},{1... | collective-permute-start | bytes 786440 | tf_op jit(solution)/shard_map/ppermute | solution.py:414
  26.4 2.5 %collective-permute-start.8 = (bf16[4,128,128]{2,1,0:T(8,128)(2,1)S(1)}, bf16[4,128,128]{2,1,0:T(8,128)(2,1)S(1)}, u32[]{:S(2)}, u32[]{:S(2)}) collective-permute-start(bf16[4,128,128]{2,1,0:T(8,128)(2,1)S(1)} %pad_maximum_fusion.5.mine_ref), channel_id=1, source_target_pairs={{0,128},{128,0},{1,129},{129,1},{2,130},{130,2},{3,131},{131,3},{4... | collective-permute-start | bytes 393224 | tf_op jit(solution)/shard_map/ppermute | solution.py:416
  28.9 2.1 %attend_first.1 = (bf16[1024,128]{1,0:T(8,128)(2,1)S(1)}, f32[8,8,128]{2,1,0:T(8,128)S(1)}, f32[1024,128]{1,0:T(8,128)S(1)}) custom-call(s32[128]{0:T(128)S(1)} %copy-done.1, s32[128,128]{1,0:T(8,128)S(1)} %copy-done, bf16[4,128,128]{2,1,0:T(8,128)(2,1)S(1)} %pad_maximum_fusion.5.mine_ref, bf16[1024,128]{1,0:T(8,128)(2,1)S(1)} %bitcast.14), custom_call_target="tpu_custom_call" | custom-call | flops 536870912 | bytes 4194304 | tf_op jit(solution)/shard_map/attend_first/pallas_call | solution.py:196
  31.0 1.0 %collective-permute-done.4.low_ref = bf16[1024,128]{1,0:T(8,128)(2,1)S(1)} collective-permute-done((bf16[1024,128]{1,0:T(8,128)(2,1)S(1)}, bf16[1024,128]{1,0:T(8,128)(2,1)S(1)}, u32[]{:S(2)}, u32[]{:S(2)}) %collective-permute-start.4) | collective-permute-done | bytes 262176 | tf_op jit(solution)/shard_map/ppermute | solution.py:413
  32.1 2.7 %collective-permute-start.7 = (bf16[1024,128]{1,0:T(8,128)(2,1)S(1)}, bf16[1024,128]{1,0:T(8,128)(2,1)S(1)}, u32[]{:S(2)}, u32[]{:S(2)}) collective-permute-start(bf16[1024,128]{1,0:T(8,128)(2,1)S(1)} %collective-permute-done.5.high_ref), channel_id=1, source_target_pairs={{0,112},{16,0},{32,16},{48,32},{64,48},{80,64},{96,80},{112,96},{1... | collective-permute-start | bytes 786440 | tf_op jit(solution)/shard_map/ppermute | solution.py:414
  34.7 4.6 %attend_second.1 = (bf16[1024,128]{1,0:T(8,128)(2,1)S(1)}, f32[1024,128]{1,0:T(8,128)S(1)}, f32[1024,128]{1,0:T(8,128)S(1)}) custom-call(bf16[1024,128]{1,0:T(8,128)(2,1)S(1)} %get-tuple-element.56.q_ref, bf16[4,128,128]{2,1,0:T(8,128)(2,1)S(1)} %collective-permute-done.8.other_ref, ...), custom_call_target="tpu_custom_call", output_to_operand_aliasing={{1}: (5, {})} | custom-call | flops 2147483648 | bytes 4194304 | tf_op jit(solution)/shard_map/attend_second/pallas_call | solution.py:225
  39.5 2.4 %collective-permute-start.10 = (bf16[1024,128]{1,0:T(8,128)(2,1)S(1)}, bf16[1024,128]{1,0:T(8,128)(2,1)S(1)}, u32[]{:S(2)}, u32[]{:S(2)}) collective-permute-start(bf16[1024,128]{1,0:T(8,128)(2,1)S(1)} %collective-permute-done.7.high_ref), channel_id=1, source_target_pairs={{0,112},{16,0},{32,16},{48,32},{64,48},{80,64},{96,80},{112,96},{1... | collective-permute-start | bytes 786440 | tf_op jit(solution)/shard_map/ppermute | solution.py:414
  42.0 1.1 %collective-permute-start.13 = (bf16[512,256]{1,0:T(8,128)(2,1)S(1)}, bf16[512,256]{1,0:T(8,128)(2,1)S(1)}, u32[]{:S(2)}, u32[]{:S(2)}) collective-permute-start(bf16[512,256]{1,0:T(8,128)(2,1)S(1)} %pad_maximum_fusion.4), channel_id=1, source_target_pairs={{0,2},{2,0},{1,3},{3,1},{4,6},{6,4},{5,7},{7,5},{8,10},{10,8},{9,1... | collective-permute-start | bytes 786440 | tf_op jit(solution)/shard_map/ppermute | solution.py:423
  43.1 5.7 %attend_third.1 = (f32[1024,128]{1,0:T(8,128)S(1)}, f32[1024,128]{1,0:T(8,128)S(1)}) custom-call(bf16[1024,128]{1,0:T(8,128)(2,1)S(1)} %get-tuple-element.56.q_ref, bf16[1024,128]{1,0:T(8,128)(2,1)S(1)} %get-tuple-element.66.q2_ref.q_ref, f32[8,8,128]{2,1,0:T(8,128)S(1)} %get-tuple-element.57.bias_ref, ...), custom_call_target="tpu_custom_call", output_to_operand_aliasing={{0}: (6, {}), {1}: (7, {})} | custom-call | flops 2684354560 | bytes 4194304 | tf_op jit(solution)/shard_map/attend_third/pallas_call | solution.py:244
  48.9 2.7 %collective-permute-start.12 = (bf16[512,128]{1,0:T(8,128)(2,1)S(1)}, bf16[512,128]{1,0:T(8,128)(2,1)S(1)}, u32[]{:S(2)}, u32[]{:S(2)}) collective-permute-start(bf16[512,128]{1,0:T(8,128)(2,1)S(1)} %slice.21), channel_id=1, source_target_pairs={{0,112},{16,0},{32,16},{48,32},{64,48},{80,64},{96,80},{112,96},{1... | collective-permute-start | bytes 393224 | tf_op jit(solution)/shard_map/ppermute | solution.py:414
  51.7 2.4 %attend_fourth_other.1.in_ref = f32[1024,128]{1,0:T(8,128)S(1)} custom-call(bf16[1024,128]{1,0:T(8,128)(2,1)S(1)} %get-tuple-element.66.q2_ref.q_ref, f32[8,8,128]{2,1,0:T(8,128)S(1)} %get-tuple-element.57.bias_ref, bf16[1024,128]{1,0:T(8,128)(2,1)S(1)} %collective-permute-done.9.low_ref, ...), custom_call_target="tpu_custom_call", output_to_operand_aliasing={{}: (4, {})} | custom-call | flops 1073741824 | bytes 4194304 | tf_op jit(solution)/shard_map/attend_fourth_other/pallas_call | solution.py:262
  54.1 1.5 %attend_last_other.1 = bf16[528,128]{1,0:T(8,128)(2,1)S(1)} custom-call(bf16[1024,128]{1,0:T(8,128)(2,1)S(1)} %get-tuple-element.66.q2_ref.q_ref, f32[8,8,128]{2,1,0:T(8,128)S(1)} %get-tuple-element.57.bias_ref, bf16[512,128]{1,0:T(8,128)(2,1)S(1)} %collective-permute-done.11.low_ref.far_low, bf16[512,128]{1,0:T(8,128)(2,1)S(1)} %collective-permute-done.12.high_ref.far_high, ...), custom_call_target="tpu_custom_call" | custom-call | flops 536870912 | bytes 4194304 | tf_op jit(solution)/shard_map/attend_last_other/pallas_call | solution.py:305
  55.7 2.7 %collective-permute-start.14 = (bf16[528,128]{1,0:T(8,128)(2,1)S(1)}, bf16[528,128]{1,0:T(8,128)(2,1)S(1)}, u32[]{:S(2)}, u32[]{:S(2)}) collective-permute-start(bf16[528,128]{1,0:T(8,128)(2,1)S(1)} %attend_last_other.1), channel_id=1, source_target_pairs={{0,128},{128,0},{1,129},{129,1},{2,130},{130,2},{3,131},{131,3},{4... | collective-permute-start | bytes 405512 | tf_op jit(solution)/shard_map/ppermute | solution.py:431
  58.4 3.5 %attend_last_mine.1.mine_ref = f32[1024,128]{1,0:T(8,128)S(1)} custom-call(bf16[1024,128]{1,0:T(8,128)(2,1)S(1)} %get-tuple-element.56.q_ref, f32[8,8,128]{2,1,0:T(8,128)S(1)} %get-tuple-element.57.bias_ref, bf16[1024,128]{1,0:T(8,128)(2,1)S(1)} %collective-permute-done.9.low_ref, ...), custom_call_target="tpu_custom_call", output_to_operand_aliasing={{}: (6, {})} | custom-call | flops 1610612736 | bytes 4194304 | tf_op jit(solution)/shard_map/attend_last_mine/pallas_call | solution.py:323
  61.9 0.3 finish.1
  62.1 0.7 collective-permute-start.15
  62.8 0.7 collective-permute-start.16
  63.6 0.8 collective-permute-start.17
  64.3 1.0 %collective-permute-done.15 = bf16[128,128]{1,0:T(8,128)(2,1)S(1)} collective-permute-done((bf16[128,128]{1,0:T(8,128)(2,1)S(1)}, bf16[128,128]{1,0:T(8,128)(2,1)S(1)}, u32[]{:S(2)}, u32[]{:S(2)}) %collective-permute-start.15) | collective-permute-done | bytes 32800 | tf_op jit(solution)/shard_map/ppermute | solution.py:433
  65.3 1.8 %collective-permute-done.16 = bf16[128,128]{1,0:T(8,128)(2,1)S(1)} collective-permute-done((bf16[128,128]{1,0:T(8,128)(2,1)S(1)}, bf16[128,128]{1,0:T(8,128)(2,1)S(1)}, u32[]{:S(2)}, u32[]{:S(2)}) %collective-permute-start.16) | collective-permute-done | bytes 32800 | tf_op jit(solution)/shard_map/ppermute | solution.py:433
  67.1 0.4 collective-permute-done.17
  67.6 14.1 %all_gather.7.a_ref = bf16[16,128,128]{2,1,0:T(8,128)(2,1)S(1)} all-gather(bf16[4,128,128]{2,1,0:T(8,128)(2,1)S(1)} %pad_maximum_fusion.6), channel_id=1, replica_groups=mesh['xh'=2,'z'=8,'y'=4,'xl'=2,'core'=2] {'xl','core'}, dimensions={0}, use_global_device_ids=true | all-gather | bytes 655360 | tf_op jit(solution)/shard_map/all_gather | solution.py:434
  81.7 1.0 %output.1 = bf16[256,256]{1,0:T(8,128)(2,1)} custom-call(bf16[16,128,128]{2,1,0:T(8,128)(2,1)S(1)} %all_gather.7.a_ref, bf16[256,256]{1,0:T(8,128)(2,1)S(1)} %get-tuple-element.85.own_ref, bf16[256,256]{1,0:T(8,128)(2,1)S(1)} %get-tuple-element.89.near_ref, bf16[512,256]{1,0:T(8,128)(2,1)S(1)} %collective-permute-done.13.far_ref), custom_call_target="tpu_custom_call" | custom-call | tf_op jit(solution)/shard_map/output/pallas_call | solution.py:388
  (30 shorter events, 0.6 us)
Async XLA Ops:
  9.8 7.0 %copy-start.2 = (bf16[256,1024]{1,0:T(8,128)(2,1)S(1)}, bf16[256,1024]{1,0:T(8,128)(2,1)}, u32[]{:S(2)}) copy-start(bf16[256,1024]{1,0:T(8,128)(2,1)} %param.14) | copy-start | bytes 1572868
  12.8 5.5 %collective-permute-start = (bf16[384,128]{1,0:T(8,128)(2,1)S(1)}, bf16[384,128]{1,0:T(8,128)(2,1)S(1)}, u32[]{:S(2)}, u32[]{:S(2)}) collective-permute-start(bf16[384,128]{1,0:T(8,128)(2,1)S(1)} %get-tuple-element.50), channel_id=1, source_target_pairs={{0,4},{4,8},{8,12},{12,0},{1,5},{5,9},{9,13},{13,1},{2,6},{6,10},{... | collective-permute-start | bytes 294920 | tf_op jit(solution)/shard_map/ppermute | solution.py:408
  13.1 7.5 %collective-permute-start.1 = (bf16[384,128]{1,0:T(8,128)(2,1)S(1)}, bf16[384,128]{1,0:T(8,128)(2,1)S(1)}, u32[]{:S(2)}, u32[]{:S(2)}) collective-permute-start(bf16[384,128]{1,0:T(8,128)(2,1)S(1)} %get-tuple-element.51), channel_id=1, source_target_pairs={{0,8},{4,12},{8,0},{12,4},{1,9},{5,13},{9,1},{13,5},{2,10},{6,14},... | collective-permute-start | bytes 294920 | tf_op jit(solution)/shard_map/ppermute | solution.py:408
  15.7 5.0 %collective-permute-start.2 = (bf16[384,128]{1,0:T(8,128)(2,1)S(1)}, bf16[384,128]{1,0:T(8,128)(2,1)S(1)}, u32[]{:S(2)}, u32[]{:S(2)}) collective-permute-start(bf16[384,128]{1,0:T(8,128)(2,1)S(1)} %get-tuple-element.52), channel_id=1, source_target_pairs={{0,12},{4,0},{8,4},{12,8},{1,13},{5,1},{9,5},{13,9},{2,14},{6,2},{... | collective-permute-start | bytes 294920 | tf_op jit(solution)/shard_map/ppermute | solution.py:408
  16.9 3.9 %collective-permute-start.3 = (bf16[512,256]{1,0:T(8,128)(2,1)S(1)}, bf16[512,256]{1,0:T(8,128)(2,1)S(1)}, u32[]{:S(2)}, u32[]{:S(2)}) collective-permute-start(bf16[512,256]{1,0:T(8,128)(2,1)S(1)} %pad_maximum_fusion.3), channel_id=1, source_target_pairs={{0,1},{1,0},{2,3},{3,2},{4,5},{5,4},{6,7},{7,6},{8,9},{9,8},{10,11... | collective-permute-start | bytes 786440 | tf_op jit(solution)/shard_map/ppermute | solution.py:407
  20.7 8.2 %copy-start = (s32[128,128]{1,0:T(8,128)S(1)}, s32[128,128]{1,0:T(8,128)}, u32[]{:S(2)}) copy-start(s32[128,128]{1,0:T(8,128)} %adjacency_ref.1) | copy-start | bytes 196612
  20.8 8.1 %copy-start.1 = (s32[128]{0:T(128)S(1)}, s32[128]{0:T(128)}, u32[]{:S(2)}) copy-start(s32[128]{0:T(128)} %order_ref.1) | copy-start | bytes 1540
  20.8 11.3 %collective-permute-start.4 = (bf16[1024,128]{1,0:T(8,128)(2,1)S(1)}, bf16[1024,128]{1,0:T(8,128)(2,1)S(1)}, u32[]{:S(2)}, u32[]{:S(2)}) collective-permute-start(bf16[1024,128]{1,0:T(8,128)(2,1)S(1)} %bitcast.12), channel_id=1, source_target_pairs={{0,16},{16,32},{32,48},{48,64},{64,80},{80,96},{96,112},{112,0},{1... | collective-permute-start | bytes 786440 | tf_op jit(solution)/shard_map/ppermute | solution.py:413
  22.4 9.6 %collective-permute-start.5 = (bf16[1024,128]{1,0:T(8,128)(2,1)S(1)}, bf16[1024,128]{1,0:T(8,128)(2,1)S(1)}, u32[]{:S(2)}, u32[]{:S(2)}) collective-permute-start(bf16[1024,128]{1,0:T(8,128)(2,1)S(1)} %bitcast.13), channel_id=1, source_target_pairs={{0,112},{16,0},{32,16},{48,32},{64,48},{80,64},{96,80},{112,96},{1... | collective-permute-start | bytes 786440 | tf_op jit(solution)/shard_map/ppermute | solution.py:414
  26.4 8.3 %collective-permute-start.8 = (bf16[4,128,128]{2,1,0:T(8,128)(2,1)S(1)}, bf16[4,128,128]{2,1,0:T(8,128)(2,1)S(1)}, u32[]{:S(2)}, u32[]{:S(2)}) collective-permute-start(bf16[4,128,128]{2,1,0:T(8,128)(2,1)S(1)} %pad_maximum_fusion.5.mine_ref), channel_id=1, source_target_pairs={{0,128},{128,0},{1,129},{129,1},{2,130},{130,2},{3,131},{131,3},{4... | collective-permute-start | bytes 393224 | tf_op jit(solution)/shard_map/ppermute | solution.py:416
  32.1 7.5 %collective-permute-start.6 = (bf16[1024,128]{1,0:T(8,128)(2,1)S(1)}, bf16[1024,128]{1,0:T(8,128)(2,1)S(1)}, u32[]{:S(2)}, u32[]{:S(2)}) collective-permute-start(bf16[1024,128]{1,0:T(8,128)(2,1)S(1)} %collective-permute-done.4.low_ref), channel_id=1, source_target_pairs={{0,16},{16,32},{32,48},{48,64},{64,80},{80,96},{96,112},{112,0},{1... | collective-permute-start | bytes 786440 | tf_op jit(solution)/shard_map/ppermute | solution.py:413
  32.1 7.5 %collective-permute-start.7 = (bf16[1024,128]{1,0:T(8,128)(2,1)S(1)}, bf16[1024,128]{1,0:T(8,128)(2,1)S(1)}, u32[]{:S(2)}, u32[]{:S(2)}) collective-permute-start(bf16[1024,128]{1,0:T(8,128)(2,1)S(1)} %collective-permute-done.5.high_ref), channel_id=1, source_target_pairs={{0,112},{16,0},{32,16},{48,32},{64,48},{80,64},{96,80},{112,96},{1... | collective-permute-start | bytes 786440 | tf_op jit(solution)/shard_map/ppermute | solution.py:414
  39.5 9.3 %collective-permute-start.10 = (bf16[1024,128]{1,0:T(8,128)(2,1)S(1)}, bf16[1024,128]{1,0:T(8,128)(2,1)S(1)}, u32[]{:S(2)}, u32[]{:S(2)}) collective-permute-start(bf16[1024,128]{1,0:T(8,128)(2,1)S(1)} %collective-permute-done.7.high_ref), channel_id=1, source_target_pairs={{0,112},{16,0},{32,16},{48,32},{64,48},{80,64},{96,80},{112,96},{1... | collective-permute-start | bytes 786440 | tf_op jit(solution)/shard_map/ppermute | solution.py:414
  41.9 6.9 %collective-permute-start.9 = (bf16[1024,128]{1,0:T(8,128)(2,1)S(1)}, bf16[1024,128]{1,0:T(8,128)(2,1)S(1)}, u32[]{:S(2)}, u32[]{:S(2)}) collective-permute-start(bf16[1024,128]{1,0:T(8,128)(2,1)S(1)} %collective-permute-done.6.low_ref), channel_id=1, source_target_pairs={{0,16},{16,32},{32,48},{48,64},{64,80},{80,96},{96,112},{112,0},{1... | collective-permute-start | bytes 786440 | tf_op jit(solution)/shard_map/ppermute | solution.py:413
  42.0 12.1 %collective-permute-start.13 = (bf16[512,256]{1,0:T(8,128)(2,1)S(1)}, bf16[512,256]{1,0:T(8,128)(2,1)S(1)}, u32[]{:S(2)}, u32[]{:S(2)}) collective-permute-start(bf16[512,256]{1,0:T(8,128)(2,1)S(1)} %pad_maximum_fusion.4), channel_id=1, source_target_pairs={{0,2},{2,0},{1,3},{3,1},{4,6},{6,4},{5,7},{7,5},{8,10},{10,8},{9,1... | collective-permute-start | bytes 786440 | tf_op jit(solution)/shard_map/ppermute | solution.py:423
  48.8 5.3 %collective-permute-start.11 = (bf16[512,128]{1,0:T(8,128)(2,1)S(1)}, bf16[512,128]{1,0:T(8,128)(2,1)S(1)}, u32[]{:S(2)}, u32[]{:S(2)}) collective-permute-start(bf16[512,128]{1,0:T(8,128)(2,1)S(1)} %slice.20), channel_id=1, source_target_pairs={{0,16},{16,32},{32,48},{48,64},{64,80},{80,96},{96,112},{112,0},{1... | collective-permute-start | bytes 393224 | tf_op jit(solution)/shard_map/ppermute | solution.py:413
  48.9 5.2 %collective-permute-start.12 = (bf16[512,128]{1,0:T(8,128)(2,1)S(1)}, bf16[512,128]{1,0:T(8,128)(2,1)S(1)}, u32[]{:S(2)}, u32[]{:S(2)}) collective-permute-start(bf16[512,128]{1,0:T(8,128)(2,1)S(1)} %slice.21), channel_id=1, source_target_pairs={{0,112},{16,0},{32,16},{48,32},{64,48},{80,64},{96,80},{112,96},{1... | collective-permute-start | bytes 393224 | tf_op jit(solution)/shard_map/ppermute | solution.py:414
  55.7 6.2 %collective-permute-start.14 = (bf16[528,128]{1,0:T(8,128)(2,1)S(1)}, bf16[528,128]{1,0:T(8,128)(2,1)S(1)}, u32[]{:S(2)}, u32[]{:S(2)}) collective-permute-start(bf16[528,128]{1,0:T(8,128)(2,1)S(1)} %attend_last_other.1), channel_id=1, source_target_pairs={{0,128},{128,0},{1,129},{129,1},{2,130},{130,2},{3,131},{131,3},{4... | collective-permute-start | bytes 405512 | tf_op jit(solution)/shard_map/ppermute | solution.py:431
  62.1 3.1 %collective-permute-start.15 = (bf16[128,128]{1,0:T(8,128)(2,1)S(1)}, bf16[128,128]{1,0:T(8,128)(2,1)S(1)}, u32[]{:S(2)}, u32[]{:S(2)}) collective-permute-start(bf16[128,128]{1,0:T(8,128)(2,1)S(1)} %get-tuple-element.81), channel_id=1, source_target_pairs={{0,12},{4,0},{8,4},{12,8},{1,13},{5,1},{9,5},{13,9},{2,14},{6,2},{... | collective-permute-start | bytes 98312 | tf_op jit(solution)/shard_map/ppermute | solution.py:433
  62.8 4.3 %collective-permute-start.16 = (bf16[128,128]{1,0:T(8,128)(2,1)S(1)}, bf16[128,128]{1,0:T(8,128)(2,1)S(1)}, u32[]{:S(2)}, u32[]{:S(2)}) collective-permute-start(bf16[128,128]{1,0:T(8,128)(2,1)S(1)} %get-tuple-element.82), channel_id=1, source_target_pairs={{0,8},{4,12},{8,0},{12,4},{1,9},{5,13},{9,1},{13,5},{2,10},{6,14},... | collective-permute-start | bytes 98312 | tf_op jit(solution)/shard_map/ppermute | solution.py:433
  63.6 4.0 %collective-permute-start.17 = (bf16[128,128]{1,0:T(8,128)(2,1)S(1)}, bf16[128,128]{1,0:T(8,128)(2,1)S(1)}, u32[]{:S(2)}, u32[]{:S(2)}) collective-permute-start(bf16[128,128]{1,0:T(8,128)(2,1)S(1)} %get-tuple-element.83), channel_id=1, source_target_pairs={{0,4},{4,8},{8,12},{12,0},{1,5},{5,9},{9,13},{13,1},{2,6},{6,10},{... | collective-permute-start | bytes 98312 | tf_op jit(solution)/shard_map/ppermute | solution.py:433

commit v6 on v5

--- a/solution.py
+++ b/solution.py
@@ -8,6 +8,7 @@
 CTX = ("xh", "z", "y")
 HEAD = ("xl", "core")
 NXH, NZ, NY, NXL, NCORE = 2, 8, 4, 2, 2
+ORDER = (0, 2, 1, 3)
 BLOCK = 128
 HD = 64
 ROWS = 256
@@ -126,9 +127,9 @@
         return jnp.where(lane == order_ref[block], 1.0, 0.0)
 
     queries_ref[...] = jnp.zeros_like(queries_ref)
-    for s in range(NY):
+    for i, s in enumerate(ORDER):
         for b in range(2):
-            n = 2 * s + b
+            n = 2 * i + b
             queries_ref[HD + n : HD + n + 1, :] = pick(xh, z, s, b)
             queries_ref[HD + 8 + n : HD + 9 + n, :] = pick(1 - xh, z, s, b)
             for zs in range(NZ):
@@ -378,7 +379,7 @@
             tops.append(jnp.where(lane < HD, one, pltpu.roll(two, 64, 1)).astype(BF16))
             bottoms.append(jnp.where(lane < HD, pltpu.roll(one, 64, 1), two).astype(BF16))
             for at in (s, s + 1):
-                row = source * 256 + lax.rem(y + at, NY) * HD
+                row = source * 256 + lax.rem(y + ORDER[at], NY) * HD
                 weights.append(w_ref[pl.ds(pl.multiple_of(row, HD), HD), :])
     features = jnp.concatenate([jnp.concatenate(tops, axis=1), jnp.concatenate(bottoms, axis=1)], axis=0)
     out_ref[...] = jnp.dot(features, jnp.concatenate(weights, axis=0), preferred_element_type=F32).astype(BF16)
@@ -405,8 +406,7 @@
     own, relayed = block(xl, core), block(1 - xl, core)
     near = jnp.concatenate([block(xl, 1 - core), block(1 - xl, 1 - core)], axis=0)
     near = lax.ppermute(near, "core", ring(NCORE, 1))
-    turned = {s: lax.ppermute(messages[s], "y", ring(NY, s)) for s in (2, 1, 3)}
-    got = jnp.stack([messages[0]] + [turned[s] for s in range(1, NY)])
+    got = jnp.stack([messages[s] if s == 0 else lax.ppermute(messages[s], "y", ring(NY, s)) for s in ORDER])
     kv = got[:, :ROWS, :].reshape(NK, 128)
     query = got[:, ROWS:, :]
     query, kv, near = lax.optimization_barrier((query, kv, near))
@@ -430,7 +430,7 @@
     message, acc = lax.optimization_barrier((message, acc))
     message = lax.ppermute(message, "xh", ring(NXH, 1))
     attended = finish(attend_last_mine(q, bias, low3, high3, low4, high4, acc), message)
-    back = jnp.stack([attended[0]] + [lax.ppermute(attended[s], "y", ring(NY, -s)) for s in range(1, NY)])
+    back = jnp.stack([a if s == 0 else lax.ppermute(a, "y", ring(NY, -s)) for a, s in zip(attended, ORDER)])
     gathered = lax.all_gather(back, HEAD, axis=0, tiled=True)
     return output(gathered, own, near[:256], far)
 

time: 82.9 us -> 84.5 us (1.019)
  starting transfers between devices: 27.1 us -> 29.7 us
  blocking collectives: 23.9 us -> 23 us
    ppermute x6, starting transfers between devices: 6.17 us -> 9.64 us  [the longest x3 5.03 us: shards(): lax.ppermute(a, 'y', ring(NY, -s))]
    all_gather x1, blocking collectives: 14.1 us -> 13.2 us  [shards(): gathered = lax.all_gather(back, HEAD, axis=0, tiled=True)]
  transfers between devices with their start and end apart: 18 -> 18, of which waited for: 8 -> 4; matrix products, arithmetic and copies ran while one was open for 0% -> 0% of each run, Pallas kernels for 22% -> 22%
where the time goes in v6:
time: 84.5 us; the launch traced here: 84.4 us
  starting transfers between devices  29.7 us (35%)
  Pallas kernels  24.1 us (29%)
  blocking collectives  23 us (27%)
  waiting for transfers between devices  7.12 us (8%)
    all_gather x1, blocking collectives, shards(): gathered = lax.all_gather(back, HEAD, axis=0, tiled=True)  13.2 us
    ppermute x4, starting transfers between devices, shards(): down = lambda part: lax.ppermute(part, 'z', ring(NZ, -1))  11.7 us
    all_gather x1, blocking collectives, shards(): whole = lax.all_gather(tokens, HEAD, axis=1, tiled=True)  9.78 us
    pallas_call x1, Pallas kernels, attend_third(): pl.pallas_call(third_kernel, out_shape=(ACC, ACC), in_specs=[VMEM] * 8, o...  5.69 us
    ppermute x3, starting transfers between devices, shards(): lax.ppermute(a, 'y', ring(NY, -s))  5.03 us
    ppermute x3, starting transfers between devices, shards(): lax.ppermute(messages[s], 'y', ring(NY, s))  4.6 us
    pallas_call x1, Pallas kernels, attend_second(): pl.pallas_call(second_kernel, out_shape=(WIDE, ACC, ACC), in_specs=[VMEM]...  4.58 us
    ppermute x3, waiting for transfers between devices, shards(): lax.ppermute(a, 'y', ring(NY, -s))  3.97 us
  transfers between devices with their start and end apart: 18, of which 4 were waited for; matrix products, arithmetic and copies ran while one was open for 0% of the time, Pallas kernels for 22%

profile of v6, /device:TPU:1, one launch (start us, length us, event | category | flops | bytes accessed | tf_op | source)
XLA Modules:
  0.0 84.4 jit_solution(5216392714585272476)
XLA Ops:
  0.0 9.8 %all_gather.6.x_ref = bf16[256,1024]{1,0:T(8,128)(2,1)S(1)} all-gather(bf16[256,256]{1,0:T(8,128)(2,1)} %param.9), channel_id=1, replica_groups=mesh['xh'=2,'z'=8,'y'=4,'xl'=2,'core'=2] {'xl','core'}, dimensions={1}, use_global_device_ids=true | all-gather | bytes 655360 | tf_op jit(solution)/shard_map/all_gather | solution.py:401
  9.8 3.0 %project.1 = (bf16[384,128]{1,0:T(8,128)(2,1)S(1)}, bf16[384,128]{1,0:T(8,128)(2,1)S(1)}, bf16[384,128]{1,0:T(8,128)(2,1)S(1)}, bf16[384,128]{1,0:T(8,128)(2,1)S(1)}) custom-call(bf16[256,1024]{1,0:T(8,128)(2,1)S(1)} %all_gather.6.x_ref, f32[4]{0:T(128)} %temper_hbm.1, f32[1,1024]{1,0:T(1,128)} %bitcast.26, bf16[1024,256]{1,0:T(8,128)(2,1)} %wq_hbm.1, ...), custom_call_target="tpu_custom_call" | custom-call | tf_op jit(solution)/shard_map/project/pallas_call | solution.py:86
  12.8 1.9 %collective-permute-start = (bf16[384,128]{1,0:T(8,128)(2,1)S(1)}, bf16[384,128]{1,0:T(8,128)(2,1)S(1)}, u32[]{:S(2)}, u32[]{:S(2)}) collective-permute-start(bf16[384,128]{1,0:T(8,128)(2,1)S(1)} %get-tuple-element.50), channel_id=1, source_target_pairs={{0,8},{4,12},{8,0},{12,4},{1,9},{5,13},{9,1},{13,5},{2,10},{6,14},... | collective-permute-start | bytes 294920 | tf_op jit(solution)/shard_map/ppermute | solution.py:409
  14.7 0.4 collective-permute-start.1
  15.1 2.3 %collective-permute-start.2 = (bf16[384,128]{1,0:T(8,128)(2,1)S(1)}, bf16[384,128]{1,0:T(8,128)(2,1)S(1)}, u32[]{:S(2)}, u32[]{:S(2)}) collective-permute-start(bf16[384,128]{1,0:T(8,128)(2,1)S(1)} %get-tuple-element.52), channel_id=1, source_target_pairs={{0,12},{4,0},{8,4},{12,8},{1,13},{5,1},{9,5},{13,9},{2,14},{6,2},{... | collective-permute-start | bytes 294920 | tf_op jit(solution)/shard_map/ppermute | solution.py:409
  17.4 0.1 constant_dynamic-slice_fusion
  17.5 1.1 %collective-permute-start.3 = (bf16[512,256]{1,0:T(8,128)(2,1)S(1)}, bf16[512,256]{1,0:T(8,128)(2,1)S(1)}, u32[]{:S(2)}, u32[]{:S(2)}) collective-permute-start(bf16[512,256]{1,0:T(8,128)(2,1)S(1)} %pad_maximum_fusion.3), channel_id=1, source_target_pairs={{0,1},{1,0},{2,3},{3,2},{4,5},{5,4},{6,7},{7,6},{8,9},{9,8},{10,11... | collective-permute-start | bytes 786440 | tf_op jit(solution)/shard_map/ppermute | solution.py:408
  18.6 0.0 collective-permute-done
  18.6 2.2 %collective-permute-done.1 = bf16[384,128]{1,0:T(8,128)(2,1)S(1)} collective-permute-done((bf16[384,128]{1,0:T(8,128)(2,1)S(1)}, bf16[384,128]{1,0:T(8,128)(2,1)S(1)}, u32[]{:S(2)}, u32[]{:S(2)}) %collective-permute-start.1) | collective-permute-done | bytes 98336 | tf_op jit(solution)/shard_map/ppermute | solution.py:409
  21.0 0.8 collective-permute-start.4
  21.8 4.0 %collective-permute-start.5 = (bf16[1024,128]{1,0:T(8,128)(2,1)S(1)}, bf16[1024,128]{1,0:T(8,128)(2,1)S(1)}, u32[]{:S(2)}, u32[]{:S(2)}) collective-permute-start(bf16[1024,128]{1,0:T(8,128)(2,1)S(1)} %bitcast.13), channel_id=1, source_target_pairs={{0,112},{16,0},{32,16},{48,32},{64,48},{80,64},{96,80},{112,96},{1... | collective-permute-start | bytes 786440 | tf_op jit(solution)/shard_map/ppermute | solution.py:414
  25.8 2.5 %collective-permute-start.8 = (bf16[4,128,128]{2,1,0:T(8,128)(2,1)S(1)}, bf16[4,128,128]{2,1,0:T(8,128)(2,1)S(1)}, u32[]{:S(2)}, u32[]{:S(2)}) collective-permute-start(bf16[4,128,128]{2,1,0:T(8,128)(2,1)S(1)} %pad_maximum_fusion.5.mine_ref), channel_id=1, source_target_pairs={{0,128},{128,0},{1,129},{129,1},{2,130},{130,2},{3,131},{131,3},{4... | collective-permute-start | bytes 393224 | tf_op jit(solution)/shard_map/ppermute | solution.py:416
  28.3 2.1 %attend_first.1 = (bf16[1024,128]{1,0:T(8,128)(2,1)S(1)}, f32[8,8,128]{2,1,0:T(8,128)S(1)}, f32[1024,128]{1,0:T(8,128)S(1)}) custom-call(s32[128]{0:T(128)S(1)} %copy-done.1, s32[128,128]{1,0:T(8,128)S(1)} %copy-done, bf16[4,128,128]{2,1,0:T(8,128)(2,1)S(1)} %pad_maximum_fusion.5.mine_ref, bf16[1024,128]{1,0:T(8,128)(2,1)S(1)} %bitcast.14), custom_call_target="tpu_custom_call" | custom-call | flops 536870912 | bytes 4194304 | tf_op jit(solution)/shard_map/attend_first/pallas_call | solution.py:197
  30.4 0.8 collective-permute-done.4.low_ref
  31.3 2.7 %collective-permute-start.7 = (bf16[1024,128]{1,0:T(8,128)(2,1)S(1)}, bf16[1024,128]{1,0:T(8,128)(2,1)S(1)}, u32[]{:S(2)}, u32[]{:S(2)}) collective-permute-start(bf16[1024,128]{1,0:T(8,128)(2,1)S(1)} %collective-permute-done.5.high_ref), channel_id=1, source_target_pairs={{0,112},{16,0},{32,16},{48,32},{64,48},{80,64},{96,80},{112,96},{1... | collective-permute-start | bytes 786440 | tf_op jit(solution)/shard_map/ppermute | solution.py:414
  33.9 4.6 %attend_second.1 = (bf16[1024,128]{1,0:T(8,128)(2,1)S(1)}, f32[1024,128]{1,0:T(8,128)S(1)}, f32[1024,128]{1,0:T(8,128)S(1)}) custom-call(bf16[1024,128]{1,0:T(8,128)(2,1)S(1)} %get-tuple-element.56.q_ref, bf16[4,128,128]{2,1,0:T(8,128)(2,1)S(1)} %collective-permute-done.8.other_ref, ...), custom_call_target="tpu_custom_call", output_to_operand_aliasing={{1}: (5, {})} | custom-call | flops 2147483648 | bytes 4194304 | tf_op jit(solution)/shard_map/attend_second/pallas_call | solution.py:226
  38.5 2.4 %collective-permute-start.10 = (bf16[1024,128]{1,0:T(8,128)(2,1)S(1)}, bf16[1024,128]{1,0:T(8,128)(2,1)S(1)}, u32[]{:S(2)}, u32[]{:S(2)}) collective-permute-start(bf16[1024,128]{1,0:T(8,128)(2,1)S(1)} %collective-permute-done.7.high_ref), channel_id=1, source_target_pairs={{0,112},{16,0},{32,16},{48,32},{64,48},{80,64},{96,80},{112,96},{1... | collective-permute-start | bytes 786440 | tf_op jit(solution)/shard_map/ppermute | solution.py:414
  41.0 1.1 %collective-permute-start.13 = (bf16[512,256]{1,0:T(8,128)(2,1)S(1)}, bf16[512,256]{1,0:T(8,128)(2,1)S(1)}, u32[]{:S(2)}, u32[]{:S(2)}) collective-permute-start(bf16[512,256]{1,0:T(8,128)(2,1)S(1)} %pad_maximum_fusion.4), channel_id=1, source_target_pairs={{0,2},{2,0},{1,3},{3,1},{4,6},{6,4},{5,7},{7,5},{8,10},{10,8},{9,1... | collective-permute-start | bytes 786440 | tf_op jit(solution)/shard_map/ppermute | solution.py:423
  42.1 5.7 %attend_third.1 = (f32[1024,128]{1,0:T(8,128)S(1)}, f32[1024,128]{1,0:T(8,128)S(1)}) custom-call(bf16[1024,128]{1,0:T(8,128)(2,1)S(1)} %get-tuple-element.56.q_ref, bf16[1024,128]{1,0:T(8,128)(2,1)S(1)} %get-tuple-element.66.q2_ref.q_ref, f32[8,8,128]{2,1,0:T(8,128)S(1)} %get-tuple-element.57.bias_ref, ...), custom_call_target="tpu_custom_call", output_to_operand_aliasing={{0}: (6, {}), {1}: (7, {})} | custom-call | flops 2684354560 | bytes 4194304 | tf_op jit(solution)/shard_map/attend_third/pallas_call | solution.py:245
  47.8 0.2 collective-permute-start.11
  48.0 2.6 %collective-permute-start.12 = (bf16[512,128]{1,0:T(8,128)(2,1)S(1)}, bf16[512,128]{1,0:T(8,128)(2,1)S(1)}, u32[]{:S(2)}, u32[]{:S(2)}) collective-permute-start(bf16[512,128]{1,0:T(8,128)(2,1)S(1)} %slice.21), channel_id=1, source_target_pairs={{0,112},{16,0},{32,16},{48,32},{64,48},{80,64},{96,80},{112,96},{1... | collective-permute-start | bytes 393224 | tf_op jit(solution)/shard_map/ppermute | solution.py:414
  50.7 2.4 %attend_fourth_other.1.in_ref = f32[1024,128]{1,0:T(8,128)S(1)} custom-call(bf16[1024,128]{1,0:T(8,128)(2,1)S(1)} %get-tuple-element.66.q2_ref.q_ref, f32[8,8,128]{2,1,0:T(8,128)S(1)} %get-tuple-element.57.bias_ref, bf16[1024,128]{1,0:T(8,128)(2,1)S(1)} %collective-permute-done.9.low_ref, ...), custom_call_target="tpu_custom_call", output_to_operand_aliasing={{}: (4, {})} | custom-call | flops 1073741824 | bytes 4194304 | tf_op jit(solution)/shard_map/attend_fourth_other/pallas_call | solution.py:263
  53.1 1.5 %attend_last_other.1 = bf16[528,128]{1,0:T(8,128)(2,1)S(1)} custom-call(bf16[1024,128]{1,0:T(8,128)(2,1)S(1)} %get-tuple-element.66.q2_ref.q_ref, f32[8,8,128]{2,1,0:T(8,128)S(1)} %get-tuple-element.57.bias_ref, bf16[512,128]{1,0:T(8,128)(2,1)S(1)} %collective-permute-done.11.low_ref.far_low, bf16[512,128]{1,0:T(8,128)(2,1)S(1)} %collective-permute-done.12.high_ref.far_high, ...), custom_call_target="tpu_custom_call" | custom-call | flops 536870912 | bytes 4194304 | tf_op jit(solution)/shard_map/attend_last_other/pallas_call | solution.py:306
  54.7 2.7 %collective-permute-start.14 = (bf16[528,128]{1,0:T(8,128)(2,1)S(1)}, bf16[528,128]{1,0:T(8,128)(2,1)S(1)}, u32[]{:S(2)}, u32[]{:S(2)}) collective-permute-start(bf16[528,128]{1,0:T(8,128)(2,1)S(1)} %attend_last_other.1), channel_id=1, source_target_pairs={{0,128},{128,0},{1,129},{129,1},{2,130},{130,2},{3,131},{131,3},{4... | collective-permute-start | bytes 405512 | tf_op jit(solution)/shard_map/ppermute | solution.py:431
  57.3 3.5 %attend_last_mine.1.mine_ref = f32[1024,128]{1,0:T(8,128)S(1)} custom-call(bf16[1024,128]{1,0:T(8,128)(2,1)S(1)} %get-tuple-element.56.q_ref, f32[8,8,128]{2,1,0:T(8,128)S(1)} %get-tuple-element.57.bias_ref, bf16[1024,128]{1,0:T(8,128)(2,1)S(1)} %collective-permute-done.9.low_ref, ...), custom_call_target="tpu_custom_call", output_to_operand_aliasing={{}: (6, {})} | custom-call | flops 1610612736 | bytes 4194304 | tf_op jit(solution)/shard_map/attend_last_mine/pallas_call | solution.py:324
  60.8 0.3 finish.1
  61.1 2.3 %collective-permute-start.15 = (bf16[128,128]{1,0:T(8,128)(2,1)S(1)}, bf16[128,128]{1,0:T(8,128)(2,1)S(1)}, u32[]{:S(2)}, u32[]{:S(2)}) collective-permute-start(bf16[128,128]{1,0:T(8,128)(2,1)S(1)} %get-tuple-element.81), channel_id=1, source_target_pairs={{0,8},{4,12},{8,0},{12,4},{1,9},{5,13},{9,1},{13,5},{2,10},{6,14},... | collective-permute-start | bytes 98312 | tf_op jit(solution)/shard_map/ppermute | solution.py:433
  63.4 2.7 %collective-permute-start.16 = (bf16[128,128]{1,0:T(8,128)(2,1)S(1)}, bf16[128,128]{1,0:T(8,128)(2,1)S(1)}, u32[]{:S(2)}, u32[]{:S(2)}) collective-permute-start(bf16[128,128]{1,0:T(8,128)(2,1)S(1)} %get-tuple-element.82), channel_id=1, source_target_pairs={{0,12},{4,0},{8,4},{12,8},{1,13},{5,1},{9,5},{13,9},{2,14},{6,2},{... | collective-permute-start | bytes 98312 | tf_op jit(solution)/shard_map/ppermute | solution.py:433
  66.2 1.0 %collective-permute-done.16 = bf16[128,128]{1,0:T(8,128)(2,1)S(1)} collective-permute-done((bf16[128,128]{1,0:T(8,128)(2,1)S(1)}, bf16[128,128]{1,0:T(8,128)(2,1)S(1)}, u32[]{:S(2)}, u32[]{:S(2)}) %collective-permute-start.16) | collective-permute-done | bytes 32800 | tf_op jit(solution)/shard_map/ppermute | solution.py:433
  67.2 3.0 %collective-permute-done.17 = bf16[128,128]{1,0:T(8,128)(2,1)S(1)} collective-permute-done((bf16[128,128]{1,0:T(8,128)(2,1)S(1)}, bf16[128,128]{1,0:T(8,128)(2,1)S(1)}, u32[]{:S(2)}, u32[]{:S(2)}) %collective-permute-start.17) | collective-permute-done | bytes 32800 | tf_op jit(solution)/shard_map/ppermute | solution.py:433
  70.2 13.2 %all_gather.7.a_ref = bf16[16,128,128]{2,1,0:T(8,128)(2,1)S(1)} all-gather(bf16[4,128,128]{2,1,0:T(8,128)(2,1)S(1)} %pad_maximum_fusion.6), channel_id=1, replica_groups=mesh['xh'=2,'z'=8,'y'=4,'xl'=2,'core'=2] {'xl','core'}, dimensions={0}, use_global_device_ids=true | all-gather | bytes 655360 | tf_op jit(solution)/shard_map/all_gather | solution.py:434
  83.4 1.0 %output.1 = bf16[256,256]{1,0:T(8,128)(2,1)} custom-call(bf16[16,128,128]{2,1,0:T(8,128)(2,1)S(1)} %all_gather.7.a_ref, bf16[256,256]{1,0:T(8,128)(2,1)S(1)} %get-tuple-element.85.own_ref, bf16[256,256]{1,0:T(8,128)(2,1)S(1)} %get-tuple-element.89.near_ref, bf16[512,256]{1,0:T(8,128)(2,1)S(1)} %collective-permute-done.13.far_ref), custom_call_target="tpu_custom_call" | custom-call | tf_op jit(solution)/shard_map/output/pallas_call | solution.py:389
  (30 shorter events, 0.2 us)
Async XLA Ops:
  9.8 7.6 %copy-start.2 = (bf16[256,1024]{1,0:T(8,128)(2,1)S(1)}, bf16[256,1024]{1,0:T(8,128)(2,1)}, u32[]{:S(2)}) copy-start(bf16[256,1024]{1,0:T(8,128)(2,1)} %param.14) | copy-start | bytes 1572868
  12.8 5.8 %collective-permute-start = (bf16[384,128]{1,0:T(8,128)(2,1)S(1)}, bf16[384,128]{1,0:T(8,128)(2,1)S(1)}, u32[]{:S(2)}, u32[]{:S(2)}) collective-permute-start(bf16[384,128]{1,0:T(8,128)(2,1)S(1)} %get-tuple-element.50), channel_id=1, source_target_pairs={{0,8},{4,12},{8,0},{12,4},{1,9},{5,13},{9,1},{13,5},{2,10},{6,14},... | collective-permute-start | bytes 294920 | tf_op jit(solution)/shard_map/ppermute | solution.py:409
  14.7 6.2 %collective-permute-start.1 = (bf16[384,128]{1,0:T(8,128)(2,1)S(1)}, bf16[384,128]{1,0:T(8,128)(2,1)S(1)}, u32[]{:S(2)}, u32[]{:S(2)}) collective-permute-start(bf16[384,128]{1,0:T(8,128)(2,1)S(1)} %get-tuple-element.51), channel_id=1, source_target_pairs={{0,4},{4,8},{8,12},{12,0},{1,5},{5,9},{9,13},{13,1},{2,6},{6,10},{... | collective-permute-start | bytes 294920 | tf_op jit(solution)/shard_map/ppermute | solution.py:409
  15.1 5.8 %collective-permute-start.2 = (bf16[384,128]{1,0:T(8,128)(2,1)S(1)}, bf16[384,128]{1,0:T(8,128)(2,1)S(1)}, u32[]{:S(2)}, u32[]{:S(2)}) collective-permute-start(bf16[384,128]{1,0:T(8,128)(2,1)S(1)} %get-tuple-element.52), channel_id=1, source_target_pairs={{0,12},{4,0},{8,4},{12,8},{1,13},{5,1},{9,5},{13,9},{2,14},{6,2},{... | collective-permute-start | bytes 294920 | tf_op jit(solution)/shard_map/ppermute | solution.py:409
  17.5 3.4 %collective-permute-start.3 = (bf16[512,256]{1,0:T(8,128)(2,1)S(1)}, bf16[512,256]{1,0:T(8,128)(2,1)S(1)}, u32[]{:S(2)}, u32[]{:S(2)}) collective-permute-start(bf16[512,256]{1,0:T(8,128)(2,1)S(1)} %pad_maximum_fusion.3), channel_id=1, source_target_pairs={{0,1},{1,0},{2,3},{3,2},{4,5},{5,4},{6,7},{7,6},{8,9},{9,8},{10,11... | collective-permute-start | bytes 786440 | tf_op jit(solution)/shard_map/ppermute | solution.py:408
  20.9 7.4 %copy-start = (s32[128,128]{1,0:T(8,128)S(1)}, s32[128,128]{1,0:T(8,128)}, u32[]{:S(2)}) copy-start(s32[128,128]{1,0:T(8,128)} %adjacency_ref.1) | copy-start | bytes 196612
  20.9 7.3 %copy-start.1 = (s32[128]{0:T(128)S(1)}, s32[128]{0:T(128)}, u32[]{:S(2)}) copy-start(s32[128]{0:T(128)} %order_ref.1) | copy-start | bytes 1540
  21.0 10.3 %collective-permute-start.4 = (bf16[1024,128]{1,0:T(8,128)(2,1)S(1)}, bf16[1024,128]{1,0:T(8,128)(2,1)S(1)}, u32[]{:S(2)}, u32[]{:S(2)}) collective-permute-start(bf16[1024,128]{1,0:T(8,128)(2,1)S(1)} %bitcast.12), channel_id=1, source_target_pairs={{0,16},{16,32},{32,48},{48,64},{64,80},{80,96},{96,112},{112,0},{1... | collective-permute-start | bytes 786440 | tf_op jit(solution)/shard_map/ppermute | solution.py:413
  21.8 9.4 %collective-permute-start.5 = (bf16[1024,128]{1,0:T(8,128)(2,1)S(1)}, bf16[1024,128]{1,0:T(8,128)(2,1)S(1)}, u32[]{:S(2)}, u32[]{:S(2)}) collective-permute-start(bf16[1024,128]{1,0:T(8,128)(2,1)S(1)} %bitcast.13), channel_id=1, source_target_pairs={{0,112},{16,0},{32,16},{48,32},{64,48},{80,64},{96,80},{112,96},{1... | collective-permute-start | bytes 786440 | tf_op jit(solution)/shard_map/ppermute | solution.py:414
  25.8 8.1 %collective-permute-start.8 = (bf16[4,128,128]{2,1,0:T(8,128)(2,1)S(1)}, bf16[4,128,128]{2,1,0:T(8,128)(2,1)S(1)}, u32[]{:S(2)}, u32[]{:S(2)}) collective-permute-start(bf16[4,128,128]{2,1,0:T(8,128)(2,1)S(1)} %pad_maximum_fusion.5.mine_ref), channel_id=1, source_target_pairs={{0,128},{128,0},{1,129},{129,1},{2,130},{130,2},{3,131},{131,3},{4... | collective-permute-start | bytes 393224 | tf_op jit(solution)/shard_map/ppermute | solution.py:416
  31.3 7.3 %collective-permute-start.6 = (bf16[1024,128]{1,0:T(8,128)(2,1)S(1)}, bf16[1024,128]{1,0:T(8,128)(2,1)S(1)}, u32[]{:S(2)}, u32[]{:S(2)}) collective-permute-start(bf16[1024,128]{1,0:T(8,128)(2,1)S(1)} %collective-permute-done.4.low_ref), channel_id=1, source_target_pairs={{0,16},{16,32},{32,48},{48,64},{64,80},{80,96},{96,112},{112,0},{1... | collective-permute-start | bytes 786440 | tf_op jit(solution)/shard_map/ppermute | solution.py:413
  31.3 7.3 %collective-permute-start.7 = (bf16[1024,128]{1,0:T(8,128)(2,1)S(1)}, bf16[1024,128]{1,0:T(8,128)(2,1)S(1)}, u32[]{:S(2)}, u32[]{:S(2)}) collective-permute-start(bf16[1024,128]{1,0:T(8,128)(2,1)S(1)} %collective-permute-done.5.high_ref), channel_id=1, source_target_pairs={{0,112},{16,0},{32,16},{48,32},{64,48},{80,64},{96,80},{112,96},{1... | collective-permute-start | bytes 786440 | tf_op jit(solution)/shard_map/ppermute | solution.py:414
  38.5 9.2 %collective-permute-start.10 = (bf16[1024,128]{1,0:T(8,128)(2,1)S(1)}, bf16[1024,128]{1,0:T(8,128)(2,1)S(1)}, u32[]{:S(2)}, u32[]{:S(2)}) collective-permute-start(bf16[1024,128]{1,0:T(8,128)(2,1)S(1)} %collective-permute-done.7.high_ref), channel_id=1, source_target_pairs={{0,112},{16,0},{32,16},{48,32},{64,48},{80,64},{96,80},{112,96},{1... | collective-permute-start | bytes 786440 | tf_op jit(solution)/shard_map/ppermute | solution.py:414
  40.9 6.9 %collective-permute-start.9 = (bf16[1024,128]{1,0:T(8,128)(2,1)S(1)}, bf16[1024,128]{1,0:T(8,128)(2,1)S(1)}, u32[]{:S(2)}, u32[]{:S(2)}) collective-permute-start(bf16[1024,128]{1,0:T(8,128)(2,1)S(1)} %collective-permute-done.6.low_ref), channel_id=1, source_target_pairs={{0,16},{16,32},{32,48},{48,64},{64,80},{80,96},{96,112},{112,0},{1... | collective-permute-start | bytes 786440 | tf_op jit(solution)/shard_map/ppermute | solution.py:413
  41.0 12.1 %collective-permute-start.13 = (bf16[512,256]{1,0:T(8,128)(2,1)S(1)}, bf16[512,256]{1,0:T(8,128)(2,1)S(1)}, u32[]{:S(2)}, u32[]{:S(2)}) collective-permute-start(bf16[512,256]{1,0:T(8,128)(2,1)S(1)} %pad_maximum_fusion.4), channel_id=1, source_target_pairs={{0,2},{2,0},{1,3},{3,1},{4,6},{6,4},{5,7},{7,5},{8,10},{10,8},{9,1... | collective-permute-start | bytes 786440 | tf_op jit(solution)/shard_map/ppermute | solution.py:423
  47.8 5.3 %collective-permute-start.11 = (bf16[512,128]{1,0:T(8,128)(2,1)S(1)}, bf16[512,128]{1,0:T(8,128)(2,1)S(1)}, u32[]{:S(2)}, u32[]{:S(2)}) collective-permute-start(bf16[512,128]{1,0:T(8,128)(2,1)S(1)} %slice.20), channel_id=1, source_target_pairs={{0,16},{16,32},{32,48},{48,64},{64,80},{80,96},{96,112},{112,0},{1... | collective-permute-start | bytes 393224 | tf_op jit(solution)/shard_map/ppermute | solution.py:413
  48.0 5.1 %collective-permute-start.12 = (bf16[512,128]{1,0:T(8,128)(2,1)S(1)}, bf16[512,128]{1,0:T(8,128)(2,1)S(1)}, u32[]{:S(2)}, u32[]{:S(2)}) collective-permute-start(bf16[512,128]{1,0:T(8,128)(2,1)S(1)} %slice.21), channel_id=1, source_target_pairs={{0,112},{16,0},{32,16},{48,32},{64,48},{80,64},{96,80},{112,96},{1... | collective-permute-start | bytes 393224 | tf_op jit(solution)/shard_map/ppermute | solution.py:414
  54.7 6.2 %collective-permute-start.14 = (bf16[528,128]{1,0:T(8,128)(2,1)S(1)}, bf16[528,128]{1,0:T(8,128)(2,1)S(1)}, u32[]{:S(2)}, u32[]{:S(2)}) collective-permute-start(bf16[528,128]{1,0:T(8,128)(2,1)S(1)} %attend_last_other.1), channel_id=1, source_target_pairs={{0,128},{128,0},{1,129},{129,1},{2,130},{130,2},{3,131},{131,3},{4... | collective-permute-start | bytes 405512 | tf_op jit(solution)/shard_map/ppermute | solution.py:431
  61.1 5.0 %collective-permute-start.15 = (bf16[128,128]{1,0:T(8,128)(2,1)S(1)}, bf16[128,128]{1,0:T(8,128)(2,1)S(1)}, u32[]{:S(2)}, u32[]{:S(2)}) collective-permute-start(bf16[128,128]{1,0:T(8,128)(2,1)S(1)} %get-tuple-element.81), channel_id=1, source_target_pairs={{0,8},{4,12},{8,0},{12,4},{1,9},{5,13},{9,1},{13,5},{2,10},{6,14},... | collective-permute-start | bytes 98312 | tf_op jit(solution)/shard_map/ppermute | solution.py:433
  63.4 3.8 %collective-permute-start.16 = (bf16[128,128]{1,0:T(8,128)(2,1)S(1)}, bf16[128,128]{1,0:T(8,128)(2,1)S(1)}, u32[]{:S(2)}, u32[]{:S(2)}) collective-permute-start(bf16[128,128]{1,0:T(8,128)(2,1)S(1)} %get-tuple-element.82), channel_id=1, source_target_pairs={{0,12},{4,0},{8,4},{12,8},{1,13},{5,1},{9,5},{13,9},{2,14},{6,2},{... | collective-permute-start | bytes 98312 | tf_op jit(solution)/shard_map/ppermute | solution.py:433
  66.2 4.0 %collective-permute-start.17 = (bf16[128,128]{1,0:T(8,128)(2,1)S(1)}, bf16[128,128]{1,0:T(8,128)(2,1)S(1)}, u32[]{:S(2)}, u32[]{:S(2)}) collective-permute-start(bf16[128,128]{1,0:T(8,128)(2,1)S(1)} %get-tuple-element.83), channel_id=1, source_target_pairs={{0,4},{4,8},{8,12},{12,0},{1,5},{5,9},{9,13},{13,1},{2,6},{6,10},{... | collective-permute-start | bytes 98312 | tf_op jit(solution)/shard_map/ppermute | solution.py:433

commit v7 on v6

--- a/solution.py
+++ b/solution.py
@@ -8,7 +8,7 @@
 CTX = ("xh", "z", "y")
 HEAD = ("xl", "core")
 NXH, NZ, NY, NXL, NCORE = 2, 8, 4, 2, 2
-ORDER = (0, 2, 1, 3)
+ORDER = (0, 1, 3, 2)
 BLOCK = 128
 HD = 64
 ROWS = 256

time: 84.5 us -> 82.2 us (0.973)
  starting transfers between devices: 29.7 us -> 26.6 us
    ppermute x3, starting transfers between devices: 5.03 us -> 2.46 us  [shards(): lax.ppermute(a, 'y', ring(NY, -s))]
    ppermute x3, starting transfers between devices: 4.6 us -> 3.38 us  [shards(): lax.ppermute(messages[s], 'y', ring(NY, s))]
    ppermute x3, waiting for transfers between devices: 2.29 us -> 3.15 us  [shards(): lax.ppermute(messages[s], 'y', ring(NY, s))]
  transfers between devices with their start and end apart: 18 -> 18, of which waited for: 4 -> 7; matrix products, arithmetic and copies ran while one was open for 0% -> 0% of each run, Pallas kernels for 22% -> 22%
where the time goes in v7:
time: 82.2 us; the launch traced here: 82.1 us
  starting transfers between devices  26.6 us (32%)
  Pallas kernels  24.2 us (29%)
  blocking collectives  23.6 us (29%)
  waiting for transfers between devices  7.29 us (9%)
    all_gather x1, blocking collectives, shards(): gathered = lax.all_gather(back, HEAD, axis=0, tiled=True)  13.8 us
    ppermute x4, starting transfers between devices, shards(): down = lambda part: lax.ppermute(part, 'z', ring(NZ, -1))  11.5 us
    all_gather x1, blocking collectives, shards(): whole = lax.all_gather(tokens, HEAD, axis=1, tiled=True)  9.78 us
    pallas_call x1, Pallas kernels, attend_third(): pl.pallas_call(third_kernel, out_shape=(ACC, ACC), in_specs=[VMEM] * 8, o...  5.69 us
    pallas_call x1, Pallas kernels, attend_second(): pl.pallas_call(second_kernel, out_shape=(WIDE, ACC, ACC), in_specs=[VMEM]...  4.59 us
    pallas_call x1, Pallas kernels, attend_last_mine(): pl.pallas_call(last_mine_kernel, out_shape=ACC, in_specs=[VMEM] * 7, out_...  3.49 us
    ppermute x3, starting transfers between devices, shards(): lax.ppermute(messages[s], 'y', ring(NY, s))  3.38 us
    ppermute x3, waiting for transfers between devices, shards(): lax.ppermute(a, 'y', ring(NY, -s))  3.35 us
  transfers between devices with their start and end apart: 18, of which 7 were waited for; matrix products, arithmetic and copies ran while one was open for 0% of the time, Pallas kernels for 22%

profile of v7, /device:TPU:1, one launch (start us, length us, event | category | flops | bytes accessed | tf_op | source)
XLA Modules:
  0.0 82.1 jit_solution(16990193080900145703)
XLA Ops:
  0.0 9.8 %all_gather.6.x_ref = bf16[256,1024]{1,0:T(8,128)(2,1)S(1)} all-gather(bf16[256,256]{1,0:T(8,128)(2,1)} %param.9), channel_id=1, replica_groups=mesh['xh'=2,'z'=8,'y'=4,'xl'=2,'core'=2] {'xl','core'}, dimensions={1}, use_global_device_ids=true | all-gather | bytes 655360 | tf_op jit(solution)/shard_map/all_gather | solution.py:401
  9.8 3.0 %project.1 = (bf16[384,128]{1,0:T(8,128)(2,1)S(1)}, bf16[384,128]{1,0:T(8,128)(2,1)S(1)}, bf16[384,128]{1,0:T(8,128)(2,1)S(1)}, bf16[384,128]{1,0:T(8,128)(2,1)S(1)}) custom-call(bf16[256,1024]{1,0:T(8,128)(2,1)S(1)} %all_gather.6.x_ref, f32[4]{0:T(128)} %temper_hbm.1, f32[1,1024]{1,0:T(1,128)} %bitcast.26, bf16[1024,256]{1,0:T(8,128)(2,1)} %wq_hbm.1, ...), custom_call_target="tpu_custom_call" | custom-call | tf_op jit(solution)/shard_map/project/pallas_call | solution.py:86
  12.8 0.3 collective-permute-start
  13.1 2.5 %collective-permute-start.1 = (bf16[384,128]{1,0:T(8,128)(2,1)S(1)}, bf16[384,128]{1,0:T(8,128)(2,1)S(1)}, u32[]{:S(2)}, u32[]{:S(2)}) collective-permute-start(bf16[384,128]{1,0:T(8,128)(2,1)S(1)} %get-tuple-element.51), channel_id=1, source_target_pairs={{0,12},{4,0},{8,4},{12,8},{1,13},{5,1},{9,5},{13,9},{2,14},{6,2},{... | collective-permute-start | bytes 294920 | tf_op jit(solution)/shard_map/ppermute | solution.py:409
  15.6 0.6 collective-permute-start.2
  16.3 1.1 %collective-permute-start.3 = (bf16[512,256]{1,0:T(8,128)(2,1)S(1)}, bf16[512,256]{1,0:T(8,128)(2,1)S(1)}, u32[]{:S(2)}, u32[]{:S(2)}) collective-permute-start(bf16[512,256]{1,0:T(8,128)(2,1)S(1)} %pad_maximum_fusion.3), channel_id=1, source_target_pairs={{0,1},{1,0},{2,3},{3,2},{4,5},{5,4},{6,7},{7,6},{8,9},{9,8},{10,11... | collective-permute-start | bytes 786440 | tf_op jit(solution)/shard_map/ppermute | solution.py:408
  17.4 1.0 %collective-permute-done = bf16[384,128]{1,0:T(8,128)(2,1)S(1)} collective-permute-done((bf16[384,128]{1,0:T(8,128)(2,1)S(1)}, bf16[384,128]{1,0:T(8,128)(2,1)S(1)}, u32[]{:S(2)}, u32[]{:S(2)}) %collective-permute-start) | collective-permute-done | bytes 98336 | tf_op jit(solution)/shard_map/ppermute | solution.py:409
  18.3 1.0 %collective-permute-done.1 = bf16[384,128]{1,0:T(8,128)(2,1)S(1)} collective-permute-done((bf16[384,128]{1,0:T(8,128)(2,1)S(1)}, bf16[384,128]{1,0:T(8,128)(2,1)S(1)}, u32[]{:S(2)}, u32[]{:S(2)}) %collective-permute-start.1) | collective-permute-done | bytes 98336 | tf_op jit(solution)/shard_map/ppermute | solution.py:409
  19.3 1.2 %collective-permute-done.2 = bf16[384,128]{1,0:T(8,128)(2,1)S(1)} collective-permute-done((bf16[384,128]{1,0:T(8,128)(2,1)S(1)}, bf16[384,128]{1,0:T(8,128)(2,1)S(1)}, u32[]{:S(2)}, u32[]{:S(2)}) %collective-permute-start.2) | collective-permute-done | bytes 98336 | tf_op jit(solution)/shard_map/ppermute | solution.py:409
  20.6 1.6 %collective-permute-start.4 = (bf16[1024,128]{1,0:T(8,128)(2,1)S(1)}, bf16[1024,128]{1,0:T(8,128)(2,1)S(1)}, u32[]{:S(2)}, u32[]{:S(2)}) collective-permute-start(bf16[1024,128]{1,0:T(8,128)(2,1)S(1)} %bitcast.12), channel_id=1, source_target_pairs={{0,16},{16,32},{32,48},{48,64},{64,80},{80,96},{96,112},{112,0},{1... | collective-permute-start | bytes 786440 | tf_op jit(solution)/shard_map/ppermute | solution.py:413
  22.2 4.0 %collective-permute-start.5 = (bf16[1024,128]{1,0:T(8,128)(2,1)S(1)}, bf16[1024,128]{1,0:T(8,128)(2,1)S(1)}, u32[]{:S(2)}, u32[]{:S(2)}) collective-permute-start(bf16[1024,128]{1,0:T(8,128)(2,1)S(1)} %bitcast.13), channel_id=1, source_target_pairs={{0,112},{16,0},{32,16},{48,32},{64,48},{80,64},{96,80},{112,96},{1... | collective-permute-start | bytes 786440 | tf_op jit(solution)/shard_map/ppermute | solution.py:414
  26.2 2.5 %collective-permute-start.8 = (bf16[4,128,128]{2,1,0:T(8,128)(2,1)S(1)}, bf16[4,128,128]{2,1,0:T(8,128)(2,1)S(1)}, u32[]{:S(2)}, u32[]{:S(2)}) collective-permute-start(bf16[4,128,128]{2,1,0:T(8,128)(2,1)S(1)} %pad_maximum_fusion.5.mine_ref), channel_id=1, source_target_pairs={{0,128},{128,0},{1,129},{129,1},{2,130},{130,2},{3,131},{131,3},{4... | collective-permute-start | bytes 393224 | tf_op jit(solution)/shard_map/ppermute | solution.py:416
  28.7 2.1 %attend_first.1 = (bf16[1024,128]{1,0:T(8,128)(2,1)S(1)}, f32[8,8,128]{2,1,0:T(8,128)S(1)}, f32[1024,128]{1,0:T(8,128)S(1)}) custom-call(s32[128]{0:T(128)S(1)} %copy-done.1, s32[128,128]{1,0:T(8,128)S(1)} %copy-done, bf16[4,128,128]{2,1,0:T(8,128)(2,1)S(1)} %pad_maximum_fusion.5.mine_ref, bf16[1024,128]{1,0:T(8,128)(2,1)S(1)} %bitcast.14), custom_call_target="tpu_custom_call" | custom-call | flops 536870912 | bytes 4194304 | tf_op jit(solution)/shard_map/attend_first/pallas_call | solution.py:197
  30.8 0.8 collective-permute-done.4.low_ref
  31.5 2.7 %collective-permute-start.7 = (bf16[1024,128]{1,0:T(8,128)(2,1)S(1)}, bf16[1024,128]{1,0:T(8,128)(2,1)S(1)}, u32[]{:S(2)}, u32[]{:S(2)}) collective-permute-start(bf16[1024,128]{1,0:T(8,128)(2,1)S(1)} %collective-permute-done.5.high_ref), channel_id=1, source_target_pairs={{0,112},{16,0},{32,16},{48,32},{64,48},{80,64},{96,80},{112,96},{1... | collective-permute-start | bytes 786440 | tf_op jit(solution)/shard_map/ppermute | solution.py:414
  34.2 4.6 %attend_second.1 = (bf16[1024,128]{1,0:T(8,128)(2,1)S(1)}, f32[1024,128]{1,0:T(8,128)S(1)}, f32[1024,128]{1,0:T(8,128)S(1)}) custom-call(bf16[1024,128]{1,0:T(8,128)(2,1)S(1)} %get-tuple-element.56.q_ref, bf16[4,128,128]{2,1,0:T(8,128)(2,1)S(1)} %collective-permute-done.8.other_ref, ...), custom_call_target="tpu_custom_call", output_to_operand_aliasing={{1}: (5, {})} | custom-call | flops 2147483648 | bytes 4194304 | tf_op jit(solution)/shard_map/attend_second/pallas_call | solution.py:226
  38.8 2.3 %collective-permute-start.10 = (bf16[1024,128]{1,0:T(8,128)(2,1)S(1)}, bf16[1024,128]{1,0:T(8,128)(2,1)S(1)}, u32[]{:S(2)}, u32[]{:S(2)}) collective-permute-start(bf16[1024,128]{1,0:T(8,128)(2,1)S(1)} %collective-permute-done.7.high_ref), channel_id=1, source_target_pairs={{0,112},{16,0},{32,16},{48,32},{64,48},{80,64},{96,80},{112,96},{1... | collective-permute-start | bytes 786440 | tf_op jit(solution)/shard_map/ppermute | solution.py:414
  41.2 1.1 %collective-permute-start.13 = (bf16[512,256]{1,0:T(8,128)(2,1)S(1)}, bf16[512,256]{1,0:T(8,128)(2,1)S(1)}, u32[]{:S(2)}, u32[]{:S(2)}) collective-permute-start(bf16[512,256]{1,0:T(8,128)(2,1)S(1)} %pad_maximum_fusion.4), channel_id=1, source_target_pairs={{0,2},{2,0},{1,3},{3,1},{4,6},{6,4},{5,7},{7,5},{8,10},{10,8},{9,1... | collective-permute-start | bytes 786440 | tf_op jit(solution)/shard_map/ppermute | solution.py:423
  42.3 5.7 %attend_third.1 = (f32[1024,128]{1,0:T(8,128)S(1)}, f32[1024,128]{1,0:T(8,128)S(1)}) custom-call(bf16[1024,128]{1,0:T(8,128)(2,1)S(1)} %get-tuple-element.56.q_ref, bf16[1024,128]{1,0:T(8,128)(2,1)S(1)} %get-tuple-element.66.q2_ref.q_ref, f32[8,8,128]{2,1,0:T(8,128)S(1)} %get-tuple-element.57.bias_ref, ...), custom_call_target="tpu_custom_call", output_to_operand_aliasing={{0}: (6, {}), {1}: (7, {})} | custom-call | flops 2684354560 | bytes 4194304 | tf_op jit(solution)/shard_map/attend_third/pallas_call | solution.py:245
  48.0 0.3 collective-permute-start.11
  48.3 2.6 %collective-permute-start.12 = (bf16[512,128]{1,0:T(8,128)(2,1)S(1)}, bf16[512,128]{1,0:T(8,128)(2,1)S(1)}, u32[]{:S(2)}, u32[]{:S(2)}) collective-permute-start(bf16[512,128]{1,0:T(8,128)(2,1)S(1)} %slice.21), channel_id=1, source_target_pairs={{0,112},{16,0},{32,16},{48,32},{64,48},{80,64},{96,80},{112,96},{1... | collective-permute-start | bytes 393224 | tf_op jit(solution)/shard_map/ppermute | solution.py:414
  50.9 2.4 %attend_fourth_other.1.in_ref = f32[1024,128]{1,0:T(8,128)S(1)} custom-call(bf16[1024,128]{1,0:T(8,128)(2,1)S(1)} %get-tuple-element.66.q2_ref.q_ref, f32[8,8,128]{2,1,0:T(8,128)S(1)} %get-tuple-element.57.bias_ref, bf16[1024,128]{1,0:T(8,128)(2,1)S(1)} %collective-permute-done.9.low_ref, ...), custom_call_target="tpu_custom_call", output_to_operand_aliasing={{}: (4, {})} | custom-call | flops 1073741824 | bytes 4194304 | tf_op jit(solution)/shard_map/attend_fourth_other/pallas_call | solution.py:263
  53.3 1.5 %attend_last_other.1 = bf16[528,128]{1,0:T(8,128)(2,1)S(1)} custom-call(bf16[1024,128]{1,0:T(8,128)(2,1)S(1)} %get-tuple-element.66.q2_ref.q_ref, f32[8,8,128]{2,1,0:T(8,128)S(1)} %get-tuple-element.57.bias_ref, bf16[512,128]{1,0:T(8,128)(2,1)S(1)} %collective-permute-done.11.low_ref.far_low, bf16[512,128]{1,0:T(8,128)(2,1)S(1)} %collective-permute-done.12.high_ref.far_high, ...), custom_call_target="tpu_custom_call" | custom-call | flops 536870912 | bytes 4194304 | tf_op jit(solution)/shard_map/attend_last_other/pallas_call | solution.py:306
  54.9 2.7 %collective-permute-start.14 = (bf16[528,128]{1,0:T(8,128)(2,1)S(1)}, bf16[528,128]{1,0:T(8,128)(2,1)S(1)}, u32[]{:S(2)}, u32[]{:S(2)}) collective-permute-start(bf16[528,128]{1,0:T(8,128)(2,1)S(1)} %attend_last_other.1), channel_id=1, source_target_pairs={{0,128},{128,0},{1,129},{129,1},{2,130},{130,2},{3,131},{131,3},{4... | collective-permute-start | bytes 405512 | tf_op jit(solution)/shard_map/ppermute | solution.py:431
  57.6 3.5 %attend_last_mine.1.mine_ref = f32[1024,128]{1,0:T(8,128)S(1)} custom-call(bf16[1024,128]{1,0:T(8,128)(2,1)S(1)} %get-tuple-element.56.q_ref, f32[8,8,128]{2,1,0:T(8,128)S(1)} %get-tuple-element.57.bias_ref, bf16[1024,128]{1,0:T(8,128)(2,1)S(1)} %collective-permute-done.9.low_ref, ...), custom_call_target="tpu_custom_call", output_to_operand_aliasing={{}: (6, {})} | custom-call | flops 1610612736 | bytes 4194304 | tf_op jit(solution)/shard_map/attend_last_mine/pallas_call | solution.py:324
  61.4 1.5 %collective-permute-start.16 = (bf16[128,128]{1,0:T(8,128)(2,1)S(1)}, bf16[128,128]{1,0:T(8,128)(2,1)S(1)}, u32[]{:S(2)}, u32[]{:S(2)}) collective-permute-start(bf16[128,128]{1,0:T(8,128)(2,1)S(1)} %get-tuple-element.82), channel_id=1, source_target_pairs={{0,4},{4,8},{8,12},{12,0},{1,5},{5,9},{9,13},{13,1},{2,6},{6,10},{... | collective-permute-start | bytes 98312 | tf_op jit(solution)/shard_map/ppermute | solution.py:433
  62.9 0.9 %collective-permute-start.17 = (bf16[128,128]{1,0:T(8,128)(2,1)S(1)}, bf16[128,128]{1,0:T(8,128)(2,1)S(1)}, u32[]{:S(2)}, u32[]{:S(2)}) collective-permute-start(bf16[128,128]{1,0:T(8,128)(2,1)S(1)} %get-tuple-element.83), channel_id=1, source_target_pairs={{0,8},{4,12},{8,0},{12,4},{1,9},{5,13},{9,1},{13,5},{2,10},{6,14},... | collective-permute-start | bytes 98312 | tf_op jit(solution)/shard_map/ppermute | solution.py:433
  63.8 0.4 collective-permute-done.15
  64.2 1.6 %collective-permute-done.16 = bf16[128,128]{1,0:T(8,128)(2,1)S(1)} collective-permute-done((bf16[128,128]{1,0:T(8,128)(2,1)S(1)}, bf16[128,128]{1,0:T(8,128)(2,1)S(1)}, u32[]{:S(2)}, u32[]{:S(2)}) %collective-permute-start.16) | collective-permute-done | bytes 32800 | tf_op jit(solution)/shard_map/ppermute | solution.py:433
  65.8 1.4 %collective-permute-done.17 = bf16[128,128]{1,0:T(8,128)(2,1)S(1)} collective-permute-done((bf16[128,128]{1,0:T(8,128)(2,1)S(1)}, bf16[128,128]{1,0:T(8,128)(2,1)S(1)}, u32[]{:S(2)}, u32[]{:S(2)}) %collective-permute-start.17) | collective-permute-done | bytes 32800 | tf_op jit(solution)/shard_map/ppermute | solution.py:433
  67.2 13.8 %all_gather.7.a_ref = bf16[16,128,128]{2,1,0:T(8,128)(2,1)S(1)} all-gather(bf16[4,128,128]{2,1,0:T(8,128)(2,1)S(1)} %pad_maximum_fusion.6), channel_id=1, replica_groups=mesh['xh'=2,'z'=8,'y'=4,'xl'=2,'core'=2] {'xl','core'}, dimensions={0}, use_global_device_ids=true | all-gather | bytes 655360 | tf_op jit(solution)/shard_map/all_gather | solution.py:434
  81.0 1.0 %output.1 = bf16[256,256]{1,0:T(8,128)(2,1)} custom-call(bf16[16,128,128]{2,1,0:T(8,128)(2,1)S(1)} %all_gather.7.a_ref, bf16[256,256]{1,0:T(8,128)(2,1)S(1)} %get-tuple-element.85.own_ref, bf16[256,256]{1,0:T(8,128)(2,1)S(1)} %get-tuple-element.89.near_ref, bf16[512,256]{1,0:T(8,128)(2,1)S(1)} %collective-permute-done.13.far_ref), custom_call_target="tpu_custom_call" | custom-call | tf_op jit(solution)/shard_map/output/pallas_call | solution.py:389
  (30 shorter events, 0.6 us)
Async XLA Ops:
  9.8 6.4 %copy-start.2 = (bf16[256,1024]{1,0:T(8,128)(2,1)S(1)}, bf16[256,1024]{1,0:T(8,128)(2,1)}, u32[]{:S(2)}) copy-start(bf16[256,1024]{1,0:T(8,128)(2,1)} %param.14) | copy-start | bytes 1572868
  12.8 5.5 %collective-permute-start = (bf16[384,128]{1,0:T(8,128)(2,1)S(1)}, bf16[384,128]{1,0:T(8,128)(2,1)S(1)}, u32[]{:S(2)}, u32[]{:S(2)}) collective-permute-start(bf16[384,128]{1,0:T(8,128)(2,1)S(1)} %get-tuple-element.50), channel_id=1, source_target_pairs={{0,4},{4,8},{8,12},{12,0},{1,5},{5,9},{9,13},{13,1},{2,6},{6,10},{... | collective-permute-start | bytes 294920 | tf_op jit(solution)/shard_map/ppermute | solution.py:409
  13.1 6.2 %collective-permute-start.1 = (bf16[384,128]{1,0:T(8,128)(2,1)S(1)}, bf16[384,128]{1,0:T(8,128)(2,1)S(1)}, u32[]{:S(2)}, u32[]{:S(2)}) collective-permute-start(bf16[384,128]{1,0:T(8,128)(2,1)S(1)} %get-tuple-element.51), channel_id=1, source_target_pairs={{0,12},{4,0},{8,4},{12,8},{1,13},{5,1},{9,5},{13,9},{2,14},{6,2},{... | collective-permute-start | bytes 294920 | tf_op jit(solution)/shard_map/ppermute | solution.py:409
  15.6 5.0 %collective-permute-start.2 = (bf16[384,128]{1,0:T(8,128)(2,1)S(1)}, bf16[384,128]{1,0:T(8,128)(2,1)S(1)}, u32[]{:S(2)}, u32[]{:S(2)}) collective-permute-start(bf16[384,128]{1,0:T(8,128)(2,1)S(1)} %get-tuple-element.52), channel_id=1, source_target_pairs={{0,8},{4,12},{8,0},{12,4},{1,9},{5,13},{9,1},{13,5},{2,10},{6,14},... | collective-permute-start | bytes 294920 | tf_op jit(solution)/shard_map/ppermute | solution.py:409
  16.3 4.3 %collective-permute-start.3 = (bf16[512,256]{1,0:T(8,128)(2,1)S(1)}, bf16[512,256]{1,0:T(8,128)(2,1)S(1)}, u32[]{:S(2)}, u32[]{:S(2)}) collective-permute-start(bf16[512,256]{1,0:T(8,128)(2,1)S(1)} %pad_maximum_fusion.3), channel_id=1, source_target_pairs={{0,1},{1,0},{2,3},{3,2},{4,5},{5,4},{6,7},{7,6},{8,9},{9,8},{10,11... | collective-permute-start | bytes 786440 | tf_op jit(solution)/shard_map/ppermute | solution.py:408
  20.5 8.1 %copy-start = (s32[128,128]{1,0:T(8,128)S(1)}, s32[128,128]{1,0:T(8,128)}, u32[]{:S(2)}) copy-start(s32[128,128]{1,0:T(8,128)} %adjacency_ref.1) | copy-start | bytes 196612
  20.6 8.1 %copy-start.1 = (s32[128]{0:T(128)S(1)}, s32[128]{0:T(128)}, u32[]{:S(2)}) copy-start(s32[128]{0:T(128)} %order_ref.1) | copy-start | bytes 1540
  20.6 10.9 %collective-permute-start.4 = (bf16[1024,128]{1,0:T(8,128)(2,1)S(1)}, bf16[1024,128]{1,0:T(8,128)(2,1)S(1)}, u32[]{:S(2)}, u32[]{:S(2)}) collective-permute-start(bf16[1024,128]{1,0:T(8,128)(2,1)S(1)} %bitcast.12), channel_id=1, source_target_pairs={{0,16},{16,32},{32,48},{48,64},{64,80},{80,96},{96,112},{112,0},{1... | collective-permute-start | bytes 786440 | tf_op jit(solution)/shard_map/ppermute | solution.py:413
  22.2 9.4 %collective-permute-start.5 = (bf16[1024,128]{1,0:T(8,128)(2,1)S(1)}, bf16[1024,128]{1,0:T(8,128)(2,1)S(1)}, u32[]{:S(2)}, u32[]{:S(2)}) collective-permute-start(bf16[1024,128]{1,0:T(8,128)(2,1)S(1)} %bitcast.13), channel_id=1, source_target_pairs={{0,112},{16,0},{32,16},{48,32},{64,48},{80,64},{96,80},{112,96},{1... | collective-permute-start | bytes 786440 | tf_op jit(solution)/shard_map/ppermute | solution.py:414
  26.2 8.0 %collective-permute-start.8 = (bf16[4,128,128]{2,1,0:T(8,128)(2,1)S(1)}, bf16[4,128,128]{2,1,0:T(8,128)(2,1)S(1)}, u32[]{:S(2)}, u32[]{:S(2)}) collective-permute-start(bf16[4,128,128]{2,1,0:T(8,128)(2,1)S(1)} %pad_maximum_fusion.5.mine_ref), channel_id=1, source_target_pairs={{0,128},{128,0},{1,129},{129,1},{2,130},{130,2},{3,131},{131,3},{4... | collective-permute-start | bytes 393224 | tf_op jit(solution)/shard_map/ppermute | solution.py:416
  31.5 7.3 %collective-permute-start.6 = (bf16[1024,128]{1,0:T(8,128)(2,1)S(1)}, bf16[1024,128]{1,0:T(8,128)(2,1)S(1)}, u32[]{:S(2)}, u32[]{:S(2)}) collective-permute-start(bf16[1024,128]{1,0:T(8,128)(2,1)S(1)} %collective-permute-done.4.low_ref), channel_id=1, source_target_pairs={{0,16},{16,32},{32,48},{48,64},{64,80},{80,96},{96,112},{112,0},{1... | collective-permute-start | bytes 786440 | tf_op jit(solution)/shard_map/ppermute | solution.py:413
  31.5 7.3 %collective-permute-start.7 = (bf16[1024,128]{1,0:T(8,128)(2,1)S(1)}, bf16[1024,128]{1,0:T(8,128)(2,1)S(1)}, u32[]{:S(2)}, u32[]{:S(2)}) collective-permute-start(bf16[1024,128]{1,0:T(8,128)(2,1)S(1)} %collective-permute-done.5.high_ref), channel_id=1, source_target_pairs={{0,112},{16,0},{32,16},{48,32},{64,48},{80,64},{96,80},{112,96},{1... | collective-permute-start | bytes 786440 | tf_op jit(solution)/shard_map/ppermute | solution.py:414
  38.8 9.2 %collective-permute-start.10 = (bf16[1024,128]{1,0:T(8,128)(2,1)S(1)}, bf16[1024,128]{1,0:T(8,128)(2,1)S(1)}, u32[]{:S(2)}, u32[]{:S(2)}) collective-permute-start(bf16[1024,128]{1,0:T(8,128)(2,1)S(1)} %collective-permute-done.7.high_ref), channel_id=1, source_target_pairs={{0,112},{16,0},{32,16},{48,32},{64,48},{80,64},{96,80},{112,96},{1... | collective-permute-start | bytes 786440 | tf_op jit(solution)/shard_map/ppermute | solution.py:414
  41.1 6.9 %collective-permute-start.9 = (bf16[1024,128]{1,0:T(8,128)(2,1)S(1)}, bf16[1024,128]{1,0:T(8,128)(2,1)S(1)}, u32[]{:S(2)}, u32[]{:S(2)}) collective-permute-start(bf16[1024,128]{1,0:T(8,128)(2,1)S(1)} %collective-permute-done.6.low_ref), channel_id=1, source_target_pairs={{0,16},{16,32},{32,48},{48,64},{64,80},{80,96},{96,112},{112,0},{1... | collective-permute-start | bytes 786440 | tf_op jit(solution)/shard_map/ppermute | solution.py:413
  41.2 12.1 %collective-permute-start.13 = (bf16[512,256]{1,0:T(8,128)(2,1)S(1)}, bf16[512,256]{1,0:T(8,128)(2,1)S(1)}, u32[]{:S(2)}, u32[]{:S(2)}) collective-permute-start(bf16[512,256]{1,0:T(8,128)(2,1)S(1)} %pad_maximum_fusion.4), channel_id=1, source_target_pairs={{0,2},{2,0},{1,3},{3,1},{4,6},{6,4},{5,7},{7,5},{8,10},{10,8},{9,1... | collective-permute-start | bytes 786440 | tf_op jit(solution)/shard_map/ppermute | solution.py:423
  48.0 5.3 %collective-permute-start.11 = (bf16[512,128]{1,0:T(8,128)(2,1)S(1)}, bf16[512,128]{1,0:T(8,128)(2,1)S(1)}, u32[]{:S(2)}, u32[]{:S(2)}) collective-permute-start(bf16[512,128]{1,0:T(8,128)(2,1)S(1)} %slice.20), channel_id=1, source_target_pairs={{0,16},{16,32},{32,48},{48,64},{64,80},{80,96},{96,112},{112,0},{1... | collective-permute-start | bytes 393224 | tf_op jit(solution)/shard_map/ppermute | solution.py:413
  48.3 5.0 %collective-permute-start.12 = (bf16[512,128]{1,0:T(8,128)(2,1)S(1)}, bf16[512,128]{1,0:T(8,128)(2,1)S(1)}, u32[]{:S(2)}, u32[]{:S(2)}) collective-permute-start(bf16[512,128]{1,0:T(8,128)(2,1)S(1)} %slice.21), channel_id=1, source_target_pairs={{0,112},{16,0},{32,16},{48,32},{64,48},{80,64},{96,80},{112,96},{1... | collective-permute-start | bytes 393224 | tf_op jit(solution)/shard_map/ppermute | solution.py:414
  54.9 6.2 %collective-permute-start.14 = (bf16[528,128]{1,0:T(8,128)(2,1)S(1)}, bf16[528,128]{1,0:T(8,128)(2,1)S(1)}, u32[]{:S(2)}, u32[]{:S(2)}) collective-permute-start(bf16[528,128]{1,0:T(8,128)(2,1)S(1)} %attend_last_other.1), channel_id=1, source_target_pairs={{0,128},{128,0},{1,129},{129,1},{2,130},{130,2},{3,131},{131,3},{4... | collective-permute-start | bytes 405512 | tf_op jit(solution)/shard_map/ppermute | solution.py:431
  61.4 2.8 %collective-permute-start.15 = (bf16[128,128]{1,0:T(8,128)(2,1)S(1)}, bf16[128,128]{1,0:T(8,128)(2,1)S(1)}, u32[]{:S(2)}, u32[]{:S(2)}) collective-permute-start(bf16[128,128]{1,0:T(8,128)(2,1)S(1)} %get-tuple-element.81), channel_id=1, source_target_pairs={{0,12},{4,0},{8,4},{12,8},{1,13},{5,1},{9,5},{13,9},{2,14},{6,2},{... | collective-permute-start | bytes 98312 | tf_op jit(solution)/shard_map/ppermute | solution.py:433
  61.4 4.3 %collective-permute-start.16 = (bf16[128,128]{1,0:T(8,128)(2,1)S(1)}, bf16[128,128]{1,0:T(8,128)(2,1)S(1)}, u32[]{:S(2)}, u32[]{:S(2)}) collective-permute-start(bf16[128,128]{1,0:T(8,128)(2,1)S(1)} %get-tuple-element.82), channel_id=1, source_target_pairs={{0,4},{4,8},{8,12},{12,0},{1,5},{5,9},{9,13},{13,1},{2,6},{6,10},{... | collective-permute-start | bytes 98312 | tf_op jit(solution)/shard_map/ppermute | solution.py:433
  62.9 4.3 %collective-permute-start.17 = (bf16[128,128]{1,0:T(8,128)(2,1)S(1)}, bf16[128,128]{1,0:T(8,128)(2,1)S(1)}, u32[]{:S(2)}, u32[]{:S(2)}) collective-permute-start(bf16[128,128]{1,0:T(8,128)(2,1)S(1)} %get-tuple-element.83), channel_id=1, source_target_pairs={{0,8},{4,12},{8,0},{12,4},{1,9},{5,13},{9,1},{13,5},{2,10},{6,14},... | collective-permute-start | bytes 98312 | tf_op jit(solution)/shard_map/ppermute | solution.py:433
